TPU v7x, 128 devices: a whole 4x4x4 slice. The times are simulated.
128 devices in a mesh: gx: 8 (over y, z_hi), gz: 16 (over x, z_lo, core).
Axes of the slice: x: 4, y: 4, z: 4 (z_hi: 2, z_lo: 2; z = z_hi * 2 + z_lo), core: 2. Of those that a mesh axis runs over, the one named last changes fastest.
Arguments:
- estimate: float32 [256, 128, 128], P('gz', 'gx'), may hold values from 0.5 to 2
- view_tiles: bfloat16 [128, 128, 2048], P(('gx', 'gz')), may hold values from 0.25 to 4
- incoming_label: int32 [128, 128], P(('gx', 'gz')), may hold values from -1 to 95, as said below
- lateral_bank: float32 [6, 16, 2, 33], replicated, may hold values from 0.05 to 1
- axial_kernel: float32 [6, 33], replicated, may hold values from 0.05 to 1
- kernel_index: int32 [256], replicated, may hold values from 0 to 15
Outputs:
- joined: float32 [256, 128, 128], P('gz', 'gx')
Inputs may be any that keep to these rules, and one draw needn't show every extreme that they name: `incoming_label`: for every block owner, every plane of each view that covers the block arrives in exactly one slot, labelled view * 16 + plane, and a view covers either all planes of a block or none; other slots are -1. Every block is covered by at least one view, and in every draw one block is covered by all 6 views.
All inputs are finite; a program needn't handle non-finite values.
Results may differ from a plain program's by a relative error of at most 0.00055.
Values may be sent and summed in bfloat16 or wider, within the bound.
A program may use at most 128 MiB of HBM per device.

v0:
```python
import jax
import jax.numpy as jnp
from jax import lax
from jax.sharding import PartitionSpec as P

TAPS = 33
ITERS = 2
HALO = 16


def extended(x, sides, width):
    for axis, dim in sides:
        peers, length = (lax.axis_size(axis), x.shape[dim])
        up = [(i, (i + 1) % peers) for i in range(peers - 1)]
        down = [(j, i) for i, j in up]
        last = lax.slice_in_dim(x, length - width, length, axis=dim)
        leading = lax.slice_in_dim(x, 0, width, axis=dim)
        before = lax.ppermute(last, axis, up)
        after = lax.ppermute(leading, axis, down)
        x = jnp.concatenate([before, x, after], axis=dim)
    return x


def shifted_sum(padded, weights, axis, length, flip):
    total = None
    for tap in range(TAPS):
        start = 2 * HALO - tap if flip else tap
        piece = lax.slice_in_dim(padded, start, start + length, axis=axis)
        term = weights[tap] * piece
        total = term if total is None else total + term
    return total


def lateral(padx, kernel_x, kernel_y, cols, flip):
    across = shifted_sum(padx, kernel_x, 1, cols, flip)
    along = jnp.pad(across, ((0, 0), (0, 0), (HALO, HALO)))
    return shifted_sum(along, kernel_y, 2, across.shape[2], flip)


def axial_sum(padz, weights, depth, flip):
    return shifted_sum(padz, weights, 0, depth, flip)


def depth_weights(bank_view, rows_index):
    onehot = (
        rows_index[:, None] == jnp.arange(bank_view.shape[0], dtype=jnp.int32)[None, :]
    ).astype(jnp.float32)
    table = jnp.dot(
        onehot, bank_view.reshape(bank_view.shape[0], 2 * TAPS), precision=lax.Precision.HIGHEST
    )
    return (table[:, :TAPS].T[:, :, None, None], table[:, TAPS:].T[:, :, None, None])


def shards(estimate, view_tiles, incoming_label, lateral_bank, axial_kernel, kernel_index):
    depth, cols, line = estimate.shape
    views = lateral_bank.shape[0]
    bank = lateral_bank / jnp.sum(lateral_bank, axis=-1, keepdims=True)
    axial_norm = axial_kernel / jnp.sum(axial_kernel, axis=-1, keepdims=True)
    padded_index = jnp.pad(kernel_index, (HALO, HALO))
    near_index = lax.dynamic_slice_in_dim(
        padded_index, lax.axis_index("gz") * depth, depth + 2 * HALO
    )
    own_index = near_index[HALO : HALO + depth]
    outgoing = view_tiles[0]
    arrived = lax.all_to_all(outgoing, ("gx", "gz"), split_axis=0, concat_axis=0, tiled=True)
    labels = incoming_label[0]
    codes = jnp.arange(views * depth, dtype=jnp.int32)
    select = (labels[None, :] == codes[:, None]).astype(jnp.bfloat16)
    data = jnp.dot(select, arrived, preferred_element_type=jnp.float32).astype(jnp.bfloat16)
    data = data.reshape(views, depth, cols, line)
    owner_view = jnp.where(labels >= 0, labels // depth, -1)
    counts = jnp.sum(
        (owner_view[None, :] == jnp.arange(views, dtype=jnp.int32)[:, None]).astype(jnp.int32),
        axis=1,
    )
    covered = counts > 0
    near_weights = [depth_weights(bank[view], near_index) for view in range(views)]
    own_weights = [depth_weights(bank[view], own_index) for view in range(views)]
    joined = estimate
    for sweep in range(ITERS):
        wide = extended(joined.astype(jnp.bfloat16), (("gx", 1), ("gz", 0)), HALO).astype(
            joined.dtype
        )
        ratios = []
        for view in range(views):
            grown = lateral(wide, near_weights[view][0], near_weights[view][1], cols, False)
            blurred = axial_sum(grown, axial_norm[view], depth, False)
            ratio = jnp.where(
                covered[view], (data[view].astype(jnp.float32) / blurred).astype(jnp.bfloat16), 1.0
            )
            ratios.append(lax.optimization_barrier(ratio))
        ratio_stack = jnp.stack(ratios)
        correction = jnp.zeros((depth, cols, line), jnp.float32)
        ratio_wide = extended(ratio_stack, (("gx", 2), ("gz", 1)), HALO)
        for view in range(views):
            spread = axial_sum(ratio_wide[view].astype(jnp.float32), axial_norm[view], depth, True)
            correction = correction + lateral(
                spread, own_weights[view][0], own_weights[view][1], cols, True
            )
        joined = joined * (correction / views)
    return joined


def solution(mesh):
    return jax.shard_map(
        shards,
        mesh=mesh,
        in_specs=(
            P("gz", "gx", None),
            P(("gx", "gz"), None, None),
            P(("gx", "gz"), None),
            P(),
            P(),
            P(),
        ),
        out_specs=P("gz", "gx", None),
        check_vma=False,
    )
```

profile of v0, /device:TPU:13, one launch (start us, length us, event | category | flops | bytes accessed | tf_op | source)
XLA Modules:
  0.0 912.5 jit_solution(2744737751123371071)
XLA Ops:
  12.4 10.8 %all-to-all-start = ((bf16[128,2,1024]{2,1,0:T(2,128)(2,1)}), bf16[128,2,1024]{2,1,0:T(2,128)(2,1)}, u32[]{:S(2)}, u32[]{:S(2)}) async-start(bf16[128,2,1024]{2,1,0:T(2,128)(2,1)} %reshape.4970), calls=%async_computation | async-start | bytes 1048576 | tf_op jit(solution)/shard_map/all_to_all | solution.py:65
  149.9 21.5 %broadcast_select_fusion.1 = bf16[16,16,128]{2,1,0:T(8,128)(2,1)S(1)} fusion(pred[]{:T(512)} %bitcast.190, f32[48,16,128]{2,1,0:T(8,128)S(1)} %fusion.376, f32[]{:T(128)} %bitcast.225, f32[]{:T(128)} %bitcast.224, f32[]{:T(128)} %bitcast.223, f32[]{:T(128)} %bitcast.222, f32[]{:T(128)} %bitcast.221, f32[]{:T(128)} %bitcast.220, f32[]{:T(128)} %bitcast.219, ...), kind=kLoop, calls=%fused_computation.4962 | loop fusion | flops 2228224 | bytes 4522117 | tf_op jit(solution)/shard_map/jit(_where)/select_n | solution.py:88
  171.3 21.7 %broadcast_select_fusion.3 = bf16[16,16,128]{2,1,0:T(8,128)(2,1)S(1)} fusion(pred[]{:T(512)} %bitcast.153, f32[48,16,128]{2,1,0:T(8,128)S(1)} %fusion.312, f32[]{:T(128)} %bitcast.188, f32[]{:T(128)} %bitcast.187, f32[]{:T(128)} %bitcast.186, f32[]{:T(128)} %bitcast.185, f32[]{:T(128)} %bitcast.184, f32[]{:T(128)} %bitcast.183, f32[]{:T(128)} %bitcast.182, ...), kind=kLoop, calls=%fused_computation.4964 | loop fusion | flops 2228224 | bytes 4522117 | tf_op jit(solution)/shard_map/jit(_where)/select_n | solution.py:88
  193.0 21.5 %broadcast_select_fusion.5 = bf16[16,16,128]{2,1,0:T(8,128)(2,1)S(1)} fusion(pred[]{:T(512)} %bitcast.116, f32[48,16,128]{2,1,0:T(8,128)S(1)} %fusion.248, f32[]{:T(128)} %bitcast.151, f32[]{:T(128)} %bitcast.150, f32[]{:T(128)} %bitcast.149, f32[]{:T(128)} %bitcast.148, f32[]{:T(128)} %bitcast.147, f32[]{:T(128)} %bitcast.146, f32[]{:T(128)} %bitcast.145, ...), kind=kLoop, calls=%fused_computation.4966 | loop fusion | flops 2228224 | bytes 4522117 | tf_op jit(solution)/shard_map/jit(_where)/select_n | solution.py:88
  214.6 21.8 %broadcast_select_fusion.7 = bf16[16,16,128]{2,1,0:T(8,128)(2,1)S(1)} fusion(pred[]{:T(512)} %bitcast.79, f32[48,16,128]{2,1,0:T(8,128)S(1)} %fusion.184, f32[]{:T(128)} %bitcast.114, f32[]{:T(128)} %bitcast.113, f32[]{:T(128)} %bitcast.112, f32[]{:T(128)} %bitcast.111, f32[]{:T(128)} %bitcast.110, f32[]{:T(128)} %bitcast.109, f32[]{:T(128)} %bitcast.108, ...), kind=kLoop, calls=%fused_computation.4968 | loop fusion | flops 2228224 | bytes 4522117 | tf_op jit(solution)/shard_map/jit(_where)/select_n | solution.py:88
  236.4 21.6 %broadcast_select_fusion.9 = bf16[16,16,128]{2,1,0:T(8,128)(2,1)S(1)} fusion(pred[]{:T(512)} %bitcast.42, f32[48,16,128]{2,1,0:T(8,128)S(1)} %fusion.120, f32[]{:T(128)} %bitcast.77, f32[]{:T(128)} %bitcast.76, f32[]{:T(128)} %bitcast.75, f32[]{:T(128)} %bitcast.74, f32[]{:T(128)} %bitcast.73, f32[]{:T(128)} %bitcast.72, f32[]{:T(128)} %bitcast.71, ...), kind=kLoop, calls=%fused_computation.4970 | loop fusion | flops 2228224 | bytes 4522117 | tf_op jit(solution)/shard_map/jit(_where)/select_n | solution.py:88
  258.0 21.7 %broadcast_select_fusion.11 = bf16[16,16,128]{2,1,0:T(8,128)(2,1)S(1)} fusion(pred[]{:T(512)} %bitcast.4, f32[48,16,128]{2,1,0:T(8,128)S(1)} %fusion.56, f32[]{:T(128)} %bitcast.40, f32[]{:T(128)} %bitcast.39, f32[]{:T(128)} %bitcast.38, f32[]{:T(128)} %bitcast.37, f32[]{:T(128)} %bitcast.36, f32[]{:T(128)} %bitcast.35, f32[]{:T(128)} %bitcast.34, ...), kind=kLoop, calls=%fused_computation.4972 | loop fusion | flops 2228224 | bytes 4522117 | tf_op jit(solution)/shard_map/jit(_where)/select_n | solution.py:88
  289.4 12.5 %collective-permute-done.4 = bf16[6,16,16,128]{3,2,1,0:T(8,128)(2,1)S(1)} collective-permute-done((bf16[6,16,16,128]{3,2,1,0:T(8,128)(2,1)S(1)}, bf16[6,16,16,128]{3,2,1,0:T(8,128)(2,1)S(1)}, u32[]{:S(2)}, u32[]{:S(2)}) %collective-permute-start.4) | collective-permute-done | bytes 393248 | tf_op jit(solution)/shard_map/ppermute | solution.py:18
  313.6 18.5 %collective-permute-done.6 = bf16[6,16,48,128]{3,2,1,0:T(8,128)(2,1)S(1)} collective-permute-done((bf16[6,16,48,128]{3,2,1,0:T(8,128)(2,1)S(1)}, bf16[6,16,48,128]{3,2,1,0:T(8,128)(2,1)S(1)}, u32[]{:S(2)}, u32[]{:S(2)}) %collective-permute-start.6) | collective-permute-done | bytes 1179680 | tf_op jit(solution)/shard_map/ppermute | solution.py:18
  336.2 21.7 %fusion.1332 = f32[16,48,128]{2,1,0:T(8,128)S(1)} fusion(f32[1,48,48,128]{3,2,1,0:T(8,128)S(1)} %get-tuple-element.805, f32[]{:T(128)} %bitcast.40, f32[]{:T(128)} %bitcast.39, f32[]{:T(128)} %bitcast.38, f32[]{:T(128)} %bitcast.37, f32[]{:T(128)} %bitcast.36, f32[]{:T(128)} %bitcast.35, f32[]{:T(128)} %bitcast.34, f32[]{:T(128)} %bitcast.33, f32[]{:T(128)} %bitcast.32, ...), kind=kLoop, calls=%fused_computation.2483 | loop fusion | flops 6389760 | bytes 13369476 | tf_op jit(solution)/shard_map/add | solution.py:30
  357.9 21.5 %fusion.1281 = f32[16,48,128]{2,1,0:T(8,128)S(1)} fusion(f32[1,48,48,128]{3,2,1,0:T(8,128)S(1)} %get-tuple-element.810, f32[]{:T(128)} %bitcast.77, f32[]{:T(128)} %bitcast.76, f32[]{:T(128)} %bitcast.75, f32[]{:T(128)} %bitcast.74, f32[]{:T(128)} %bitcast.73, f32[]{:T(128)} %bitcast.72, f32[]{:T(128)} %bitcast.71, f32[]{:T(128)} %bitcast.70, f32[]{:T(128)} %bitcast.69, ...), kind=kLoop, calls=%fused_computation.2399 | loop fusion | flops 6389760 | bytes 13369476 | tf_op jit(solution)/shard_map/add | solution.py:30
  379.4 21.7 %fusion.1230 = f32[16,48,128]{2,1,0:T(8,128)S(1)} fusion(f32[1,48,48,128]{3,2,1,0:T(8,128)S(1)} %get-tuple-element.809, f32[]{:T(128)} %bitcast.114, f32[]{:T(128)} %bitcast.113, f32[]{:T(128)} %bitcast.112, f32[]{:T(128)} %bitcast.111, f32[]{:T(128)} %bitcast.110, f32[]{:T(128)} %bitcast.109, f32[]{:T(128)} %bitcast.108, f32[]{:T(128)} %bitcast.107, ...), kind=kLoop, calls=%fused_computation.2315 | loop fusion | flops 6389760 | bytes 13369476 | tf_op jit(solution)/shard_map/add | solution.py:30
  401.1 21.4 %fusion.1179 = f32[16,48,128]{2,1,0:T(8,128)S(1)} fusion(f32[1,48,48,128]{3,2,1,0:T(8,128)S(1)} %get-tuple-element.808, f32[]{:T(128)} %bitcast.151, f32[]{:T(128)} %bitcast.150, f32[]{:T(128)} %bitcast.149, f32[]{:T(128)} %bitcast.148, f32[]{:T(128)} %bitcast.147, f32[]{:T(128)} %bitcast.146, f32[]{:T(128)} %bitcast.145, f32[]{:T(128)} %bitcast.144, ...), kind=kLoop, calls=%fused_computation.2231 | loop fusion | flops 6389760 | bytes 13369476 | tf_op jit(solution)/shard_map/add | solution.py:30
  422.5 21.6 %fusion.1128 = f32[16,48,128]{2,1,0:T(8,128)S(1)} fusion(f32[1,48,48,128]{3,2,1,0:T(8,128)S(1)} %get-tuple-element.807, f32[]{:T(128)} %bitcast.188, f32[]{:T(128)} %bitcast.187, f32[]{:T(128)} %bitcast.186, f32[]{:T(128)} %bitcast.185, f32[]{:T(128)} %bitcast.184, f32[]{:T(128)} %bitcast.183, f32[]{:T(128)} %bitcast.182, f32[]{:T(128)} %bitcast.181, ...), kind=kLoop, calls=%fused_computation.2147 | loop fusion | flops 6389760 | bytes 13369476 | tf_op jit(solution)/shard_map/add | solution.py:30
  444.2 21.4 %fusion.1077 = f32[16,48,128]{2,1,0:T(8,128)S(1)} fusion(f32[1,48,48,128]{3,2,1,0:T(8,128)S(1)} %get-tuple-element.806, f32[]{:T(128)} %bitcast.225, f32[]{:T(128)} %bitcast.224, f32[]{:T(128)} %bitcast.223, f32[]{:T(128)} %bitcast.222, f32[]{:T(128)} %bitcast.221, f32[]{:T(128)} %bitcast.220, f32[]{:T(128)} %bitcast.219, f32[]{:T(128)} %bitcast.218, ...), kind=kLoop, calls=%fused_computation.2063 | loop fusion | flops 6389760 | bytes 13369476 | tf_op jit(solution)/shard_map/add | solution.py:30
  473.4 16.6 %fusion.2966 = (bf16[16,16,128]{2,1,0:T(8,128)(2,1)S(1)}, f32[16,16,128]{2,1,0:T(8,128)S(1)}) fusion(f32[16,16,128]{2,1,0:T(8,128)S(1)} %copy-done, f32[16]{0:T(128)S(1)} %get-tuple-element.567, f32[16]{0:T(128)S(1)} %get-tuple-element.568, f32[16]{0:T(128)S(1)} %get-tuple-element.569, f32[16]{0:T(128)S(1)} %get-tuple-element.570, ...), kind=kLoop, calls=%fused_computation.5829 | loop fusion | flops 13041664 | bytes 1126784 | tf_op jit(solution)/shard_map/convert_element_type | solution.py:81
  541.4 21.5 %broadcast_select_fusion = bf16[16,16,128]{2,1,0:T(8,128)(2,1)S(1)} fusion(pred[]{:T(512)} %bitcast.190, f32[48,16,128]{2,1,0:T(8,128)S(1)} %fusion.760, f32[]{:T(128)} %bitcast.225, f32[]{:T(128)} %bitcast.224, f32[]{:T(128)} %bitcast.223, f32[]{:T(128)} %bitcast.222, f32[]{:T(128)} %bitcast.221, f32[]{:T(128)} %bitcast.220, f32[]{:T(128)} %bitcast.219, ...), kind=kLoop, calls=%fused_computation.4961 | loop fusion | flops 2228224 | bytes 4522117 | tf_op jit(solution)/shard_map/jit(_where)/select_n | solution.py:88
  570.0 21.7 %broadcast_select_fusion.2 = bf16[16,16,128]{2,1,0:T(8,128)(2,1)S(1)} fusion(pred[]{:T(512)} %bitcast.153, f32[48,16,128]{2,1,0:T(8,128)S(1)} %fusion.696, f32[]{:T(128)} %bitcast.188, f32[]{:T(128)} %bitcast.187, f32[]{:T(128)} %bitcast.186, f32[]{:T(128)} %bitcast.185, f32[]{:T(128)} %bitcast.184, f32[]{:T(128)} %bitcast.183, f32[]{:T(128)} %bitcast.182, ...), kind=kLoop, calls=%fused_computation.4963 | loop fusion | flops 2228224 | bytes 4522117 | tf_op jit(solution)/shard_map/jit(_where)/select_n | solution.py:88
  598.8 21.5 %broadcast_select_fusion.4 = bf16[16,16,128]{2,1,0:T(8,128)(2,1)S(1)} fusion(pred[]{:T(512)} %bitcast.116, f32[48,16,128]{2,1,0:T(8,128)S(1)} %fusion.632, f32[]{:T(128)} %bitcast.151, f32[]{:T(128)} %bitcast.150, f32[]{:T(128)} %bitcast.149, f32[]{:T(128)} %bitcast.148, f32[]{:T(128)} %bitcast.147, f32[]{:T(128)} %bitcast.146, f32[]{:T(128)} %bitcast.145, ...), kind=kLoop, calls=%fused_computation.4965 | loop fusion | flops 2228224 | bytes 4522117 | tf_op jit(solution)/shard_map/jit(_where)/select_n | solution.py:88
  627.5 21.8 %broadcast_select_fusion.6 = bf16[16,16,128]{2,1,0:T(8,128)(2,1)S(1)} fusion(pred[]{:T(512)} %bitcast.79, f32[48,16,128]{2,1,0:T(8,128)S(1)} %fusion.568, f32[]{:T(128)} %bitcast.114, f32[]{:T(128)} %bitcast.113, f32[]{:T(128)} %bitcast.112, f32[]{:T(128)} %bitcast.111, f32[]{:T(128)} %bitcast.110, f32[]{:T(128)} %bitcast.109, f32[]{:T(128)} %bitcast.108, ...), kind=kLoop, calls=%fused_computation.4967 | loop fusion | flops 2228224 | bytes 4522117 | tf_op jit(solution)/shard_map/jit(_where)/select_n | solution.py:88
  649.2 7.4 fusion.504
  656.6 21.6 %broadcast_select_fusion.8 = bf16[16,16,128]{2,1,0:T(8,128)(2,1)S(1)} fusion(pred[]{:T(512)} %bitcast.42, f32[48,16,128]{2,1,0:T(8,128)S(1)} %fusion.504, f32[]{:T(128)} %bitcast.77, f32[]{:T(128)} %bitcast.76, f32[]{:T(128)} %bitcast.75, f32[]{:T(128)} %bitcast.74, f32[]{:T(128)} %bitcast.73, f32[]{:T(128)} %bitcast.72, f32[]{:T(128)} %bitcast.71, ...), kind=kLoop, calls=%fused_computation.4969 | loop fusion | flops 2228224 | bytes 4522117 | tf_op jit(solution)/shard_map/jit(_where)/select_n | solution.py:88
  685.4 21.7 %broadcast_select_fusion.10 = bf16[16,16,128]{2,1,0:T(8,128)(2,1)S(1)} fusion(pred[]{:T(512)} %bitcast.4, f32[48,16,128]{2,1,0:T(8,128)S(1)} %fusion.440, f32[]{:T(128)} %bitcast.40, f32[]{:T(128)} %bitcast.39, f32[]{:T(128)} %bitcast.38, f32[]{:T(128)} %bitcast.37, f32[]{:T(128)} %bitcast.36, f32[]{:T(128)} %bitcast.35, f32[]{:T(128)} %bitcast.34, ...), kind=kLoop, calls=%fused_computation.4971 | loop fusion | flops 2228224 | bytes 4522117 | tf_op jit(solution)/shard_map/jit(_where)/select_n | solution.py:88
  714.9 11.5 %collective-permute-done.12 = bf16[6,16,16,128]{3,2,1,0:T(8,128)(2,1)S(1)} collective-permute-done((bf16[6,16,16,128]{3,2,1,0:T(8,128)(2,1)S(1)}, bf16[6,16,16,128]{3,2,1,0:T(8,128)(2,1)S(1)}, u32[]{:S(2)}, u32[]{:S(2)}) %collective-permute-start.12) | collective-permute-done | bytes 393248 | tf_op jit(solution)/shard_map/ppermute | solution.py:18
  734.3 23.8 %collective-permute-done.14 = bf16[6,16,48,128]{3,2,1,0:T(8,128)(2,1)S(1)} collective-permute-done((bf16[6,16,48,128]{3,2,1,0:T(8,128)(2,1)S(1)}, bf16[6,16,48,128]{3,2,1,0:T(8,128)(2,1)S(1)}, u32[]{:S(2)}, u32[]{:S(2)}) %collective-permute-start.14) | collective-permute-done | bytes 1179680 | tf_op jit(solution)/shard_map/ppermute | solution.py:18
  760.4 21.7 %fusion.1026 = f32[16,48,128]{2,1,0:T(8,128)S(1)} fusion(f32[1,48,48,128]{3,2,1,0:T(8,128)S(1)} %get-tuple-element.799, f32[]{:T(128)} %bitcast.40, f32[]{:T(128)} %bitcast.39, f32[]{:T(128)} %bitcast.38, f32[]{:T(128)} %bitcast.37, f32[]{:T(128)} %bitcast.36, f32[]{:T(128)} %bitcast.35, f32[]{:T(128)} %bitcast.34, f32[]{:T(128)} %bitcast.33, f32[]{:T(128)} %bitcast.32, ...), kind=kLoop, calls=%fused_computation.1979 | loop fusion | flops 6389760 | bytes 13369476 | tf_op jit(solution)/shard_map/add | solution.py:30
  783.0 21.5 %fusion.975 = f32[16,48,128]{2,1,0:T(8,128)S(1)} fusion(f32[1,48,48,128]{3,2,1,0:T(8,128)S(1)} %get-tuple-element.804, f32[]{:T(128)} %bitcast.77, f32[]{:T(128)} %bitcast.76, f32[]{:T(128)} %bitcast.75, f32[]{:T(128)} %bitcast.74, f32[]{:T(128)} %bitcast.73, f32[]{:T(128)} %bitcast.72, f32[]{:T(128)} %bitcast.71, f32[]{:T(128)} %bitcast.70, f32[]{:T(128)} %bitcast.69, ...), kind=kLoop, calls=%fused_computation.1895 | loop fusion | flops 6389760 | bytes 13369476 | tf_op jit(solution)/shard_map/add | solution.py:30
  805.3 21.7 %fusion.924 = f32[16,48,128]{2,1,0:T(8,128)S(1)} fusion(f32[1,48,48,128]{3,2,1,0:T(8,128)S(1)} %get-tuple-element.803, f32[]{:T(128)} %bitcast.114, f32[]{:T(128)} %bitcast.113, f32[]{:T(128)} %bitcast.112, f32[]{:T(128)} %bitcast.111, f32[]{:T(128)} %bitcast.110, f32[]{:T(128)} %bitcast.109, f32[]{:T(128)} %bitcast.108, f32[]{:T(128)} %bitcast.107, ...), kind=kLoop, calls=%fused_computation.1811 | loop fusion | flops 6389760 | bytes 13369476 | tf_op jit(solution)/shard_map/add | solution.py:30
  827.9 21.4 %fusion.873 = f32[16,48,128]{2,1,0:T(8,128)S(1)} fusion(f32[1,48,48,128]{3,2,1,0:T(8,128)S(1)} %get-tuple-element.802, f32[]{:T(128)} %bitcast.151, f32[]{:T(128)} %bitcast.150, f32[]{:T(128)} %bitcast.149, f32[]{:T(128)} %bitcast.148, f32[]{:T(128)} %bitcast.147, f32[]{:T(128)} %bitcast.146, f32[]{:T(128)} %bitcast.145, f32[]{:T(128)} %bitcast.144, ...), kind=kLoop, calls=%fused_computation.1727 | loop fusion | flops 6389760 | bytes 13369476 | tf_op jit(solution)/shard_map/add | solution.py:30
  850.1 21.6 %fusion.822 = f32[16,48,128]{2,1,0:T(8,128)S(1)} fusion(f32[1,48,48,128]{3,2,1,0:T(8,128)S(1)} %get-tuple-element.801, f32[]{:T(128)} %bitcast.188, f32[]{:T(128)} %bitcast.187, f32[]{:T(128)} %bitcast.186, f32[]{:T(128)} %bitcast.185, f32[]{:T(128)} %bitcast.184, f32[]{:T(128)} %bitcast.183, f32[]{:T(128)} %bitcast.182, f32[]{:T(128)} %bitcast.181, ...), kind=kLoop, calls=%fused_computation.1643 | loop fusion | flops 6389760 | bytes 13369476 | tf_op jit(solution)/shard_map/add | solution.py:30
  872.6 21.4 %fusion.771 = f32[16,48,128]{2,1,0:T(8,128)S(1)} fusion(f32[1,48,48,128]{3,2,1,0:T(8,128)S(1)} %get-tuple-element.800, f32[]{:T(128)} %bitcast.225, f32[]{:T(128)} %bitcast.224, f32[]{:T(128)} %bitcast.223, f32[]{:T(128)} %bitcast.222, f32[]{:T(128)} %bitcast.221, f32[]{:T(128)} %bitcast.220, f32[]{:T(128)} %bitcast.219, f32[]{:T(128)} %bitcast.218, ...), kind=kLoop, calls=%fused_computation.1559 | loop fusion | flops 6389760 | bytes 13369476 | tf_op jit(solution)/shard_map/add | solution.py:30
  894.8 17.3 %multiply_multiply_fusion = f32[16,16,128]{2,1,0:T(8,128)} fusion(f32[16,16,128]{2,1,0:T(8,128)S(1)} %get-tuple-element.798, f32[16,16,128]{2,1,0:T(8,128)S(1)} %fusion.2172, f32[16,16,128]{2,1,0:T(8,128)S(1)} %fusion.2204, f32[16,16,128]{2,1,0:T(8,128)S(1)} %fusion.2236, f32[16,16,128]{2,1,0:T(8,128)S(1)} %fusion.2268, f32[16,16,128]{2,1,0:T(8,128)S(1)} %fusion.2300, ...), kind=kLoop, calls=%fused_computation.4947 | loop fusion | flops 13008896 | bytes 1061248 | tf_op jit(solution)/shard_map/mul | solution.py:100
  (593 shorter events, 271.7 us)
Async XLA Ops:
  0.9 67.8 %collective-permute-start = (bf16[16,16,128]{2,1,0:T(8,128)(2,1)S(1)}, bf16[16,16,128]{2,1,0:T(8,128)(2,1)S(1)}, u32[]{:S(2)}, u32[]{:S(2)}) collective-permute-start(bf16[16,16,128]{2,1,0:T(8,128)(2,1)S(1)} %convert_element_type.200), channel_id=1, source_target_pairs={{0,16},{16,32},{32,48},{48,64},{64,80},{80,96},{96,112},{1,17},{17... | collective-permute-start | bytes 196616 | tf_op jit(solution)/shard_map/ppermute | solution.py:18
  6.4 62.3 %collective-permute-start.1 = (bf16[16,16,128]{2,1,0:T(8,128)(2,1)S(1)}, bf16[16,16,128]{2,1,0:T(8,128)(2,1)S(1)}, u32[]{:S(2)}, u32[]{:S(2)}) collective-permute-start(bf16[16,16,128]{2,1,0:T(8,128)(2,1)S(1)} %convert_element_type.200), channel_id=1, source_target_pairs={{16,0},{32,16},{48,32},{64,48},{80,64},{96,80},{112,96},{17,1},{33... | collective-permute-start | bytes 196616 | tf_op jit(solution)/shard_map/ppermute | solution.py:19
  12.4 132.5 %all-to-all-start = ((bf16[128,2,1024]{2,1,0:T(2,128)(2,1)}), bf16[128,2,1024]{2,1,0:T(2,128)(2,1)}, u32[]{:S(2)}, u32[]{:S(2)}) async-start(bf16[128,2,1024]{2,1,0:T(2,128)(2,1)} %reshape.4970), calls=%async_computation | async-start | bytes 1048576 | tf_op jit(solution)/shard_map/all_to_all | solution.py:65
  26.9 76.4 %copy-start.119 = (f32[48]{0:T(128)}, f32[48]{0:T(128)S(1)}, u32[]{:S(2)}) copy-start(f32[48]{0:T(128)S(1)} %get-tuple-element.6) | copy-start | bytes 580
  26.9 76.4 %copy-start.121 = (f32[48]{0:T(128)}, f32[48]{0:T(128)S(1)}, u32[]{:S(2)}) copy-start(f32[48]{0:T(128)S(1)} %get-tuple-element.7) | copy-start | bytes 580
  26.9 76.4 %copy-start.123 = (f32[48]{0:T(128)}, f32[48]{0:T(128)S(1)}, u32[]{:S(2)}) copy-start(f32[48]{0:T(128)S(1)} %get-tuple-element.8) | copy-start | bytes 580
  26.9 76.4 %copy-start.125 = (f32[48]{0:T(128)}, f32[48]{0:T(128)S(1)}, u32[]{:S(2)}) copy-start(f32[48]{0:T(128)S(1)} %get-tuple-element.9) | copy-start | bytes 580
  26.9 76.4 %copy-start.127 = (f32[48]{0:T(128)}, f32[48]{0:T(128)S(1)}, u32[]{:S(2)}) copy-start(f32[48]{0:T(128)S(1)} %get-tuple-element.10) | copy-start | bytes 580
  26.9 76.4 %copy-start.129 = (f32[48]{0:T(128)}, f32[48]{0:T(128)S(1)}, u32[]{:S(2)}) copy-start(f32[48]{0:T(128)S(1)} %get-tuple-element.11) | copy-start | bytes 580
  26.9 76.4 %copy-start.131 = (f32[48]{0:T(128)}, f32[48]{0:T(128)S(1)}, u32[]{:S(2)}) copy-start(f32[48]{0:T(128)S(1)} %get-tuple-element.12) | copy-start | bytes 580
  26.9 76.4 %copy-start.133 = (f32[48]{0:T(128)}, f32[48]{0:T(128)S(1)}, u32[]{:S(2)}) copy-start(f32[48]{0:T(128)S(1)} %get-tuple-element.13) | copy-start | bytes 580
  26.9 76.4 %copy-start.135 = (f32[48]{0:T(128)}, f32[48]{0:T(128)S(1)}, u32[]{:S(2)}) copy-start(f32[48]{0:T(128)S(1)} %get-tuple-element.14) | copy-start | bytes 580
  26.9 76.4 %copy-start.137 = (f32[48]{0:T(128)}, f32[48]{0:T(128)S(1)}, u32[]{:S(2)}) copy-start(f32[48]{0:T(128)S(1)} %get-tuple-element.15) | copy-start | bytes 580
  27.0 76.4 %copy-start.139 = (f32[48]{0:T(128)}, f32[48]{0:T(128)S(1)}, u32[]{:S(2)}) copy-start(f32[48]{0:T(128)S(1)} %get-tuple-element.16) | copy-start | bytes 580
  27.0 76.4 %copy-start.141 = (f32[48]{0:T(128)}, f32[48]{0:T(128)S(1)}, u32[]{:S(2)}) copy-start(f32[48]{0:T(128)S(1)} %get-tuple-element.17) | copy-start | bytes 580
  27.0 76.4 %copy-start.143 = (f32[48]{0:T(128)}, f32[48]{0:T(128)S(1)}, u32[]{:S(2)}) copy-start(f32[48]{0:T(128)S(1)} %get-tuple-element.18) | copy-start | bytes 580
  27.0 76.4 %copy-start.145 = (f32[48]{0:T(128)}, f32[48]{0:T(128)S(1)}, u32[]{:S(2)}) copy-start(f32[48]{0:T(128)S(1)} %get-tuple-element.19) | copy-start | bytes 580
  27.0 76.4 %copy-start.147 = (f32[48]{0:T(128)}, f32[48]{0:T(128)S(1)}, u32[]{:S(2)}) copy-start(f32[48]{0:T(128)S(1)} %get-tuple-element.20) | copy-start | bytes 580
  68.7 7.5 collective-permute-start.2
  72.3 7.2 collective-permute-start.3
  279.9 22.0 %collective-permute-start.4 = (bf16[6,16,16,128]{3,2,1,0:T(8,128)(2,1)S(1)}, bf16[6,16,16,128]{3,2,1,0:T(8,128)(2,1)S(1)}, u32[]{:S(2)}, u32[]{:S(2)}) collective-permute-start(bf16[6,16,16,128]{3,2,1,0:T(8,128)(2,1)S(1)} %bitcast_dynamic-update-slice_fusion.6), channel_id=1, source_target_pairs={{0,16},{16,32},{32,48},{48,64},{64,80},{80,96},{96,112},{1,17},{17... | collective-permute-start | bytes 1179656 | tf_op jit(solution)/shard_map/ppermute | solution.py:18
  284.7 18.9 %collective-permute-start.5 = (bf16[6,16,16,128]{3,2,1,0:T(8,128)(2,1)S(1)}, bf16[6,16,16,128]{3,2,1,0:T(8,128)(2,1)S(1)}, u32[]{:S(2)}, u32[]{:S(2)}) collective-permute-start(bf16[6,16,16,128]{3,2,1,0:T(8,128)(2,1)S(1)} %bitcast_dynamic-update-slice_fusion.6), channel_id=1, source_target_pairs={{16,0},{32,16},{48,32},{64,48},{80,64},{96,80},{112,96},{17,1},{33... | collective-permute-start | bytes 1179656 | tf_op jit(solution)/shard_map/ppermute | solution.py:19
  303.7 28.4 %collective-permute-start.6 = (bf16[6,16,48,128]{3,2,1,0:T(8,128)(2,1)S(1)}, bf16[6,16,48,128]{3,2,1,0:T(8,128)(2,1)S(1)}, u32[]{:S(2)}, u32[]{:S(2)}) collective-permute-start(bf16[6,16,48,128]{3,2,1,0:T(8,128)(2,1)S(1)} %pad_maximum_fusion.2), channel_id=1, source_target_pairs={{0,1},{1,2},{2,3},{3,4},{4,5},{5,6},{6,7},{7,8},{8,9},{9,10},{10,1... | collective-permute-start | bytes 3538952 | tf_op jit(solution)/shard_map/ppermute | solution.py:18
  306.3 28.2 %collective-permute-start.7 = (bf16[6,16,48,128]{3,2,1,0:T(8,128)(2,1)S(1)}, bf16[6,16,48,128]{3,2,1,0:T(8,128)(2,1)S(1)}, u32[]{:S(2)}, u32[]{:S(2)}) collective-permute-start(bf16[6,16,48,128]{3,2,1,0:T(8,128)(2,1)S(1)} %pad_maximum_fusion.2), channel_id=1, source_target_pairs={{1,0},{2,1},{3,2},{4,3},{5,4},{6,5},{7,6},{8,7},{9,8},{10,9},{11,1... | collective-permute-start | bytes 3538952 | tf_op jit(solution)/shard_map/ppermute | solution.py:19
  490.1 7.7 collective-permute-start.8
  494.1 6.5 collective-permute-start.9
  500.6 8.4 collective-permute-start.10
  504.4 7.0 collective-permute-start.11
  707.2 19.2 %collective-permute-start.12 = (bf16[6,16,16,128]{3,2,1,0:T(8,128)(2,1)S(1)}, bf16[6,16,16,128]{3,2,1,0:T(8,128)(2,1)S(1)}, u32[]{:S(2)}, u32[]{:S(2)}) collective-permute-start(bf16[6,16,16,128]{3,2,1,0:T(8,128)(2,1)S(1)} %bitcast_dynamic-update-slice_fusion), channel_id=1, source_target_pairs={{0,16},{16,32},{32,48},{48,64},{64,80},{80,96},{96,112},{1,17},{17... | collective-permute-start | bytes 1179656 | tf_op jit(solution)/shard_map/ppermute | solution.py:18
  712.2 16.1 %collective-permute-start.13 = (bf16[6,16,16,128]{3,2,1,0:T(8,128)(2,1)S(1)}, bf16[6,16,16,128]{3,2,1,0:T(8,128)(2,1)S(1)}, u32[]{:S(2)}, u32[]{:S(2)}) collective-permute-start(bf16[6,16,16,128]{3,2,1,0:T(8,128)(2,1)S(1)} %bitcast_dynamic-update-slice_fusion), channel_id=1, source_target_pairs={{16,0},{32,16},{48,32},{64,48},{80,64},{96,80},{112,96},{17,1},{33... | collective-permute-start | bytes 1179656 | tf_op jit(solution)/shard_map/ppermute | solution.py:19
  728.4 29.8 %collective-permute-start.14 = (bf16[6,16,48,128]{3,2,1,0:T(8,128)(2,1)S(1)}, bf16[6,16,48,128]{3,2,1,0:T(8,128)(2,1)S(1)}, u32[]{:S(2)}, u32[]{:S(2)}) collective-permute-start(bf16[6,16,48,128]{3,2,1,0:T(8,128)(2,1)S(1)} %pad_maximum_fusion.3), channel_id=1, source_target_pairs={{0,1},{1,2},{2,3},{3,4},{4,5},{5,6},{6,7},{7,8},{8,9},{9,10},{10,1... | collective-permute-start | bytes 3538952 | tf_op jit(solution)/shard_map/ppermute | solution.py:18
  732.4 26.7 %collective-permute-start.15 = (bf16[6,16,48,128]{3,2,1,0:T(8,128)(2,1)S(1)}, bf16[6,16,48,128]{3,2,1,0:T(8,128)(2,1)S(1)}, u32[]{:S(2)}, u32[]{:S(2)}) collective-permute-start(bf16[6,16,48,128]{3,2,1,0:T(8,128)(2,1)S(1)} %pad_maximum_fusion.3), channel_id=1, source_target_pairs={{1,0},{2,1},{3,2},{4,3},{5,4},{6,5},{7,6},{8,7},{9,8},{10,9},{11,1... | collective-permute-start | bytes 3538952 | tf_op jit(solution)/shard_map/ppermute | solution.py:19
  (182 other events, 2663.5 us)
where the time goes:
time: 930 us; the launch traced here: 913 us
  other arithmetic  700 us (75%)
  waiting for transfers between devices  84.4 us (9%)
  starting transfers between devices  63.4 us (7%)
  local copies, waits for them, and re-layouts  57.6 us (6%)
    add x48, other arithmetic, shifted_sum(): total = term if total is None else total + term  399 us
    select_n x12, other arithmetic, shards(): jnp.where(covered[view], (data[view].astype(jnp.float32) / blurred).astyp...  259 us
    ppermute x8, waiting for transfers between devices, extended(): before = lax.ppermute(last, axis, up)  69.1 us
    slice x59, local copies, waits for them, and re-layouts, shifted_sum(): term = weights[tap] * piece  48.7 us
    ppermute x8, starting transfers between devices, extended(): before = lax.ppermute(last, axis, up)  33.2 us
    ppermute x8, starting transfers between devices, extended(): after = lax.ppermute(leading, axis, down)  19.3 us
  transfers between devices with their start and end apart: 17, of which 12 were waited for; matrix products, arithmetic and copies ran while one was open for 13% of the time, Pallas kernels for 0%

commit v1 on v0

v1 whole, which is shorter than its diff:
```python
import jax
import jax.numpy as jnp
from jax import lax
from jax.experimental import pallas as pl
from jax.experimental.pallas import tpu as pltpu
from jax.sharding import PartitionSpec as P

TAPS = 33
ITERS = 2
HALO = 16
VIEWS = 6
KERNELS = 16
BLK = 16
NEAR = 48
LINE = 128
F32 = jnp.float32
BF = jnp.bfloat16
HI = lax.Precision.HIGHEST


def iota(shape, dim):
    return lax.broadcasted_iota(jnp.int32, shape, dim)


def build_bands(kx_ref, ky_ref, fwd_y, bwd_y, fwd_x, bwd_x):
    inside = jnp.abs(iota((LINE, LINE), 0) - iota((LINE, LINE), 1)) <= HALO

    @pl.loop(0, KERNELS)
    def _(k):
        kx = kx_ref[k]
        ky = ky_ref[k]
        rows = []
        for v in range(VIEWS):
            band = pltpu.roll(jnp.broadcast_to(ky[v : v + 1], (LINE, LINE)), LINE - HALO, 1, stride=1, stride_axis=0)
            band = jnp.where(inside, band, 0.0)
            bwd_y[k, v] = band.astype(BF)
            fwd_y[k, v] = band.T.astype(BF)
            rows.append(pltpu.roll(jnp.broadcast_to(kx[v : v + 1], (BLK, LINE)), 0, 1, stride=1, stride_axis=0))
        across = jnp.concatenate(rows, 0)
        fwd_x[k] = across.astype(BF)
        bwd_x[k] = across.T.astype(BF)


def ones_response(index_ref, ax_ref, kx_ref, ky_ref, col0, depth0, edge_x, edge_y, base_ref, cols, depths):
    tap = iota((LINE, LINE), 0)
    pos = iota((LINE, LINE), 1)
    at_x = col0 + pos - tap + HALO
    at_y = pos - tap + HALO
    ok_x = jnp.where((at_x >= 0) & (at_x < cols), 1.0, 0.0)
    ok_y = jnp.where((at_y >= 0) & (at_y < LINE), 1.0, 0.0)
    kx = kx_ref[...].reshape(KERNELS * 8, LINE)
    ky = ky_ref[...].reshape(KERNELS * 8, LINE)
    edge_x[...] = jnp.dot(kx, ok_x, precision=HI, preferred_element_type=F32).reshape(KERNELS, 8, LINE)
    edge_y[...] = jnp.dot(ky, ok_y, precision=HI, preferred_element_type=F32).reshape(KERNELS, 8, LINE)
    axial = ax_ref[...]
    lane = iota((8, LINE), 1)
    for z in range(BLK):
        k = index_ref[HALO + z]
        at_z = depth0 + z - lane + HALO
        part = jnp.sum(jnp.where((at_z >= 0) & (at_z < depths), axial, 0.0), axis=1, keepdims=True)
        left = edge_x[k][:, :BLK] * part
        base_ref[z] = lax.dot_general(
            left, edge_y[k], (((0,), (0,)), ((), ())), precision=HI, preferred_element_type=F32
        )


def lateral_forward(index_ref, fwd_x, fwd_y, wide_ref, mid, grown, first, last, unroll):
    @pl.loop(first // unroll, last // unroll)
    def _(s):
        for u in range(unroll):
            z = s * unroll + u
            k = index_ref[z]
            mid[z] = jnp.dot(fwd_x[k][:, :NEAR], wide_ref[z], preferred_element_type=F32).astype(BF)

    @pl.loop(first // unroll, last // unroll)
    def _(s):
        for u in range(unroll):
            z = s * unroll + u
            k = index_ref[z]
            for v in range(VIEWS):
                grown[v, z] = jnp.dot(mid[z, v * BLK : (v + 1) * BLK, :], fwd_y[k, v], preferred_element_type=F32)


def lateral_backward(index_ref, bwd_x, bwd_y, spread, mid, out_ref, first, last, unroll):
    @pl.loop(first // unroll, last // unroll)
    def _(s):
        for u in range(unroll):
            z = s * unroll + u
            k = index_ref[z]
            for v in range(VIEWS):
                mid[z, v * BLK : (v + 1) * BLK, :] = jnp.dot(
                    spread[v, z], bwd_y[k, v], preferred_element_type=F32
                ).astype(BF)

    @pl.loop(first // unroll, last // unroll)
    def _(s):
        for u in range(unroll):
            z = s * unroll + u
            k = index_ref[z]
            out_ref[z] = jnp.dot(bwd_x[k][:NEAR], mid[z], preferred_element_type=F32).astype(out_ref.dtype)


def taps_over(zi):
    return range(max(0, zi - 2 * HALO), min(BLK - 1, zi) + 1)


def axial_and_ratio(axial_ref, slot_ref, cover_ref, grown, tiles, spread):
    @pl.loop(0, VIEWS)
    def _(v):
        weights = [axial_ref[v, t] for t in range(TAPS)]
        seen = jnp.full((8, LINE), cover_ref[v], jnp.int32) > 0
        for half in range(2):
            rows = slice(half * 8, half * 8 + 8)
            total = [None] * BLK
            for zi in range(NEAR):
                g = grown[v, zi, rows, :]
                for zo in taps_over(zi):
                    term = weights[zi - zo] * g
                    total[zo] = term if total[zo] is None else total[zo] + term
            excess = []
            for zo in range(BLK):
                tile = tiles[slot_ref[v * BLK + zo]][rows].astype(F32)
                ratio = (tile / total[zo]).astype(BF).astype(F32)
                excess.append(jnp.where(seen, ratio - 1.0, 0.0))
            for zi in range(NEAR):
                acc = None
                for zo in taps_over(zi):
                    term = weights[zi - zo] * excess[zo]
                    acc = term if acc is None else acc + term
                spread[v, zi, rows, :] = acc.astype(BF)


def sweep_kernel(depths, cols):
    def body(index_ref, slot_ref, cover_ref, axial_ref, ax_ref, kx_ref, ky_ref, wide_ref, tiles,
             out_ref, base_ref, fwd_y, bwd_y, fwd_x, bwd_x, edge_x, edge_y, mid, grown, spread):
        col0 = lax.axis_index("gx") * BLK
        depth0 = lax.axis_index("gz") * BLK
        build_bands(kx_ref, ky_ref, fwd_y, bwd_y, fwd_x, bwd_x)
        ones_response(index_ref, ax_ref, kx_ref, ky_ref, col0, depth0, edge_x, edge_y, base_ref, cols, depths)
        lateral_forward(index_ref, fwd_x, fwd_y, wide_ref, mid, grown, 0, NEAR, 4)
        axial_and_ratio(axial_ref, slot_ref, cover_ref, grown, tiles, spread)
        lateral_backward(index_ref, bwd_x, bwd_y, spread, mid, out_ref, 0, NEAR, 4)

    smem = pl.BlockSpec(memory_space=pltpu.SMEM)
    vmem = pl.BlockSpec(memory_space=pltpu.VMEM)
    return pl.pallas_call(
        body,
        name="sweep",
        out_shape=(
            jax.ShapeDtypeStruct((NEAR, NEAR, LINE), F32),
            jax.ShapeDtypeStruct((BLK, BLK, LINE), F32),
        ),
        in_specs=[smem] * 4 + [vmem] * 5,
        out_specs=(vmem, vmem),
        scratch_shapes=[
            pltpu.VMEM((KERNELS, VIEWS, LINE, LINE), BF),
            pltpu.VMEM((KERNELS, VIEWS, LINE, LINE), BF),
            pltpu.VMEM((KERNELS, VIEWS * BLK, LINE), BF),
            pltpu.VMEM((KERNELS, LINE, VIEWS * BLK), BF),
            pltpu.VMEM((KERNELS, 8, LINE), F32),
            pltpu.VMEM((KERNELS, 8, LINE), F32),
            pltpu.VMEM((NEAR, VIEWS * BLK, LINE), BF),
            pltpu.VMEM((VIEWS, NEAR, BLK, LINE), F32),
            pltpu.VMEM((VIEWS, NEAR, BLK, LINE), BF),
        ],
        compiler_params=pltpu.CompilerParams(vmem_limit_bytes=48 << 20),
    )


def pairs(axis):
    up = [(i, i + 1) for i in range(lax.axis_size(axis) - 1)]
    return up, [(j, i) for i, j in up]


def extended(x, axis, dim):
    up, down = pairs(axis)
    return jnp.concatenate([lax.ppermute(x, axis, up), x, lax.ppermute(x, axis, down)], axis=dim)


def gathered(x, axis, dim):
    up, down = pairs(axis)
    low, own, high = (lax.slice_in_dim(x, i * BLK, (i + 1) * BLK, axis=dim) for i in range(3))
    return own + lax.ppermute(high, axis, up) + lax.ppermute(low, axis, down)


def small_tables(incoming_label, lateral_bank, axial_kernel, kernel_index):
    bank = lateral_bank / jnp.sum(lateral_bank, axis=-1, keepdims=True)
    axial = axial_kernel / jnp.sum(axial_kernel, axis=-1, keepdims=True)
    taps = jnp.pad(bank.transpose(1, 0, 2, 3), ((0, 0), (0, 8 - VIEWS), (0, 0), (0, LINE - TAPS)))
    ax = jnp.pad(axial, ((0, 8 - VIEWS), (0, LINE - TAPS)))
    near = lax.dynamic_slice_in_dim(
        jnp.pad(kernel_index, (HALO, HALO)), lax.axis_index("gz") * BLK, NEAR
    )
    labels = incoming_label[0]
    match = labels[None, :] == jnp.arange(VIEWS * BLK, dtype=jnp.int32)[:, None]
    slot = jnp.sum(jnp.where(match, jnp.arange(labels.shape[0], dtype=jnp.int32)[None, :], 0), axis=1)
    cover = jnp.sum(match.astype(jnp.int32).reshape(VIEWS, -1), axis=1)
    return axial, ax, taps[:, :, 0], taps[:, :, 1], near, slot, cover


def shards(estimate, view_tiles, incoming_label, lateral_bank, axial_kernel, kernel_index):
    depths = lax.axis_size("gz") * BLK
    cols = lax.axis_size("gx") * BLK
    axial, ax, kx, ky, near, slot, cover = small_tables(incoming_label, lateral_bank, axial_kernel, kernel_index)
    outgoing = view_tiles[0].reshape(-1, BLK, LINE)
    tiles = lax.all_to_all(outgoing, ("gx", "gz"), split_axis=0, concat_axis=0, tiled=True)
    sweep = sweep_kernel(depths, cols)
    joined = estimate
    for _ in range(ITERS):
        wide = extended(extended(joined.astype(BF), "gx", 1), "gz", 0)
        part, base = sweep(near, slot, cover, axial, ax, kx, ky, wide, tiles)
        part = gathered(part, "gz", 0)
        joined = joined * ((base + gathered(part, "gx", 1)) / VIEWS)
    return joined


def solution(mesh):
    return jax.shard_map(
        shards,
        mesh=mesh,
        in_specs=(P("gz", "gx", None), P(("gx", "gz"), None, None), P(("gx", "gz"), None), P(), P(), P()),
        out_specs=P("gz", "gx", None),
        check_vma=False,
    )
```

time: 930 us -> 154 us (0.17)
  the two profiles are of different devices: /device:TPU:13 before, /device:TPU:71 now
where the time goes in v1:
time: 154 us; the launch traced here: 153 us
  starting transfers between devices  64.4 us (42%)
  Pallas kernels  42.1 us (27%)
  waiting for transfers between devices  41.1 us (27%)
  other arithmetic  2.79 us (2%)
  local copies, waits for them, and re-layouts  2.46 us (2%)
    pallas_call x2, Pallas kernels, shards(): part, base = sweep(near, slot, cover, axial, ax, kx, ky, wide, tiles)  42.1 us
    ppermute x8, waiting for transfers between devices, gathered(): return own + lax.ppermute(high, axis, up) + lax.ppermute(low, axis, down)  30.2 us
    ppermute x8, starting transfers between devices, gathered(): return own + lax.ppermute(high, axis, up) + lax.ppermute(low, axis, down)  25.7 us
    ppermute x4, starting transfers between devices, extended(): lax.ppermute(x, axis, up)  19.7 us
    all_to_all x1, starting transfers between devices, shards(): lax.all_to_all(outgoing, ('gx', 'gz'), split_axis=0, concat_axis=0, tiled...  10.9 us
    ppermute x4, waiting for transfers between devices, extended(): lax.ppermute(x, axis, down)  9.49 us
    ppermute x4, starting transfers between devices, extended(): lax.ppermute(x, axis, down)  8.03 us
  transfers between devices with their start and end apart: 17, of which 10 were waited for; matrix products, arithmetic and copies ran while one was open for 2% of the time, Pallas kernels for 0%

profile of v1, /device:TPU:71, one launch (start us, length us, event | category | flops | bytes accessed | tf_op | source)
XLA Modules:
  0.0 153.2 jit_solution(13352400400600469717)
XLA Ops:
  0.0 0.9 convert_element_type.16
  1.0 1.9 %collective-permute-start.1 = (bf16[16,16,128]{2,1,0:T(8,128)(2,1)S(1)}, bf16[16,16,128]{2,1,0:T(8,128)(2,1)S(1)}, u32[]{:S(2)}, u32[]{:S(2)}) collective-permute-start(bf16[16,16,128]{2,1,0:T(8,128)(2,1)S(1)} %convert_element_type.16), channel_id=1, source_target_pairs={{16,0},{32,16},{48,32},{64,48},{80,64},{96,80},{112,96},{17,1},{33... | collective-permute-start | bytes 196616 | tf_op jit(solution)/shard_map/ppermute | solution.py:177
  2.9 5.8 %collective-permute-start = (bf16[16,16,128]{2,1,0:T(8,128)(2,1)S(1)}, bf16[16,16,128]{2,1,0:T(8,128)(2,1)S(1)}, u32[]{:S(2)}, u32[]{:S(2)}) collective-permute-start(bf16[16,16,128]{2,1,0:T(8,128)(2,1)S(1)} %convert_element_type.16), channel_id=1, source_target_pairs={{0,16},{16,32},{32,48},{48,64},{64,80},{80,96},{96,112},{1,17},{17... | collective-permute-start | bytes 196616 | tf_op jit(solution)/shard_map/ppermute | solution.py:177
  8.7 2.0 %copy.12 = bf16[16,8,16,128]{3,2,1,0:T(8,128)(2,1)} copy(bf16[16,8,16,128]{3,1,2,0:T(8,128)(2,1)} %bitcast.10) | data formatting | bytes 1048576
  10.6 10.9 %all-to-all-start = ((bf16[128,16,128]{2,1,0:T(8,128)(2,1)}), bf16[128,16,128]{2,1,0:T(8,128)(2,1)S(1)}, u32[]{:S(2)}, u32[]{:S(2)}) async-start(bf16[128,16,128]{2,1,0:T(8,128)(2,1)} %bitcast.6), calls=%async_computation | async-start | bytes 1048576 | tf_op jit(solution)/shard_map/all_to_all | solution.py:206
  22.3 0.3 convert_reduce_fusion.cover_ref
  22.7 2.3 %collective-permute-start.3 = (bf16[16,48,128]{2,1,0:T(8,128)(2,1)S(1)}, bf16[16,48,128]{2,1,0:T(8,128)(2,1)S(1)}, u32[]{:S(2)}, u32[]{:S(2)}) collective-permute-start(bf16[16,48,128]{2,1,0:T(8,128)(2,1)S(1)} %pad_maximum_fusion.2), channel_id=1, source_target_pairs={{1,0},{2,1},{3,2},{4,3},{5,4},{6,5},{7,6},{8,7},{9,8},{10,9},{11,1... | collective-permute-start | bytes 589832 | tf_op jit(solution)/shard_map/ppermute | solution.py:177
  25.0 3.3 %collective-permute-start.2 = (bf16[16,48,128]{2,1,0:T(8,128)(2,1)S(1)}, bf16[16,48,128]{2,1,0:T(8,128)(2,1)S(1)}, u32[]{:S(2)}, u32[]{:S(2)}) collective-permute-start(bf16[16,48,128]{2,1,0:T(8,128)(2,1)S(1)} %pad_maximum_fusion.2), channel_id=1, source_target_pairs={{0,1},{1,2},{2,3},{3,4},{4,5},{5,6},{6,7},{7,8},{8,9},{9,10},{10,1... | collective-permute-start | bytes 589832 | tf_op jit(solution)/shard_map/ppermute | solution.py:177
  28.4 6.0 %collective-permute-done.3 = bf16[16,48,128]{2,1,0:T(8,128)(2,1)S(1)} collective-permute-done((bf16[16,48,128]{2,1,0:T(8,128)(2,1)S(1)}, bf16[16,48,128]{2,1,0:T(8,128)(2,1)S(1)}, u32[]{:S(2)}, u32[]{:S(2)}) %collective-permute-start.3) | collective-permute-done | bytes 196640 | tf_op jit(solution)/shard_map/ppermute | solution.py:177
  34.4 21.1 %sweep.2 = (f32[48,48,128]{2,1,0:T(8,128)S(1)}, f32[16,16,128]{2,1,0:T(8,128)S(1)}) custom-call(s32[48]{0:T(128)S(1)} %pad_dynamic-slice_fusion.index_ref, s32[96]{0:T(128)S(1)} %select_reduce_fusion.slot_ref, s32[6]{0:T(128)S(1)} %convert_reduce_fusion.cover_ref, f32[6,33]{1,0:T(8,128)S(1)} %broadcast_divide_fusion.axial_ref, f32[8,128]{1,0:T(8,128)S(1)} %pad.13.ax_ref, ...), custom_call_target="tpu_custom_call" | custom-call | tf_op jit(solution)/shard_map/sweep/pallas_call | solution.py:211
  55.6 2.1 %collective-permute-start.4 = (f32[16,48,128]{2,1,0:T(8,128)S(1)}, f32[16,48,128]{2,1,0:T(8,128)S(1)}, u32[]{:S(2)}, u32[]{:S(2)}) collective-permute-start(f32[16,48,128]{2,1,0:T(8,128)S(1)} %get-tuple-element.17), channel_id=1, source_target_pairs={{0,1},{1,2},{2,3},{3,4},{4,5},{5,6},{6,7},{7,8},{8,9},{9,10},{10,1... | collective-permute-start | bytes 1179656 | tf_op jit(solution)/shard_map/ppermute | solution.py:183
  57.6 2.4 %collective-permute-start.5 = (f32[16,48,128]{2,1,0:T(8,128)S(1)}, f32[16,48,128]{2,1,0:T(8,128)S(1)}, u32[]{:S(2)}, u32[]{:S(2)}) collective-permute-start(f32[16,48,128]{2,1,0:T(8,128)S(1)} %get-tuple-element.18), channel_id=1, source_target_pairs={{1,0},{2,1},{3,2},{4,3},{5,4},{6,5},{7,6},{8,7},{9,8},{10,9},{11,1... | collective-permute-start | bytes 1179656 | tf_op jit(solution)/shard_map/ppermute | solution.py:183
  60.1 2.3 %collective-permute-done.4 = f32[16,48,128]{2,1,0:T(8,128)S(1)} collective-permute-done((f32[16,48,128]{2,1,0:T(8,128)S(1)}, f32[16,48,128]{2,1,0:T(8,128)S(1)}, u32[]{:S(2)}, u32[]{:S(2)}) %collective-permute-start.4) | collective-permute-done | bytes 393248 | tf_op jit(solution)/shard_map/ppermute | solution.py:183
  62.3 7.4 %collective-permute-done.5 = f32[16,48,128]{2,1,0:T(8,128)S(1)} collective-permute-done((f32[16,48,128]{2,1,0:T(8,128)S(1)}, f32[16,48,128]{2,1,0:T(8,128)S(1)}, u32[]{:S(2)}, u32[]{:S(2)}) %collective-permute-start.5) | collective-permute-done | bytes 393248 | tf_op jit(solution)/shard_map/ppermute | solution.py:183
  69.9 5.1 %collective-permute-start.6 = (f32[16,16,128]{2,1,0:T(8,128)S(1)}, f32[16,16,128]{2,1,0:T(8,128)S(1)}, u32[]{:S(2)}, u32[]{:S(2)}) collective-permute-start(f32[16,16,128]{2,1,0:T(8,128)S(1)} %get-tuple-element.21), channel_id=1, source_target_pairs={{0,16},{16,32},{32,48},{48,64},{64,80},{80,96},{96,112},{1,17},{17... | collective-permute-start | bytes 393224 | tf_op jit(solution)/shard_map/ppermute | solution.py:183
  75.0 1.9 %collective-permute-start.7 = (f32[16,16,128]{2,1,0:T(8,128)S(1)}, f32[16,16,128]{2,1,0:T(8,128)S(1)}, u32[]{:S(2)}, u32[]{:S(2)}) collective-permute-start(f32[16,16,128]{2,1,0:T(8,128)S(1)} %get-tuple-element.22), channel_id=1, source_target_pairs={{16,0},{32,16},{48,32},{64,48},{80,64},{96,80},{112,96},{17,1},{33... | collective-permute-start | bytes 393224 | tf_op jit(solution)/shard_map/ppermute | solution.py:183
  77.1 6.0 %collective-permute-done.7 = f32[16,16,128]{2,1,0:T(8,128)S(1)} collective-permute-done((f32[16,16,128]{2,1,0:T(8,128)S(1)}, f32[16,16,128]{2,1,0:T(8,128)S(1)}, u32[]{:S(2)}, u32[]{:S(2)}) %collective-permute-start.7) | collective-permute-done | bytes 131104 | tf_op jit(solution)/shard_map/ppermute | solution.py:183
  83.2 1.9 %collective-permute-start.9 = (bf16[16,16,128]{2,1,0:T(8,128)(2,1)S(1)}, bf16[16,16,128]{2,1,0:T(8,128)(2,1)S(1)}, u32[]{:S(2)}, u32[]{:S(2)}) collective-permute-start(bf16[16,16,128]{2,1,0:T(8,128)(2,1)S(1)} %get-tuple-element.13), channel_id=1, source_target_pairs={{16,0},{32,16},{48,32},{64,48},{80,64},{96,80},{112,96},{17,1},{33... | collective-permute-start | bytes 196616 | tf_op jit(solution)/shard_map/ppermute | solution.py:177
  85.1 5.8 %collective-permute-start.8 = (bf16[16,16,128]{2,1,0:T(8,128)(2,1)S(1)}, bf16[16,16,128]{2,1,0:T(8,128)(2,1)S(1)}, u32[]{:S(2)}, u32[]{:S(2)}) collective-permute-start(bf16[16,16,128]{2,1,0:T(8,128)(2,1)S(1)} %get-tuple-element.13), channel_id=1, source_target_pairs={{0,16},{16,32},{32,48},{48,64},{64,80},{80,96},{96,112},{1,17},{17... | collective-permute-start | bytes 196616 | tf_op jit(solution)/shard_map/ppermute | solution.py:177
  90.9 1.3 collective-permute-done.8
  92.2 1.9 %collective-permute-start.11 = (bf16[16,48,128]{2,1,0:T(8,128)(2,1)S(1)}, bf16[16,48,128]{2,1,0:T(8,128)(2,1)S(1)}, u32[]{:S(2)}, u32[]{:S(2)}) collective-permute-start(bf16[16,48,128]{2,1,0:T(8,128)(2,1)S(1)} %pad_maximum_fusion.3), channel_id=1, source_target_pairs={{1,0},{2,1},{3,2},{4,3},{5,4},{6,5},{7,6},{8,7},{9,8},{10,9},{11,1... | collective-permute-start | bytes 589832 | tf_op jit(solution)/shard_map/ppermute | solution.py:177
  94.2 4.9 %collective-permute-start.10 = (bf16[16,48,128]{2,1,0:T(8,128)(2,1)S(1)}, bf16[16,48,128]{2,1,0:T(8,128)(2,1)S(1)}, u32[]{:S(2)}, u32[]{:S(2)}) collective-permute-start(bf16[16,48,128]{2,1,0:T(8,128)(2,1)S(1)} %pad_maximum_fusion.3), channel_id=1, source_target_pairs={{0,1},{1,2},{2,3},{3,4},{4,5},{5,6},{6,7},{7,8},{8,9},{9,10},{10,1... | collective-permute-start | bytes 589832 | tf_op jit(solution)/shard_map/ppermute | solution.py:177
  99.1 3.5 %collective-permute-done.11 = bf16[16,48,128]{2,1,0:T(8,128)(2,1)S(1)} collective-permute-done((bf16[16,48,128]{2,1,0:T(8,128)(2,1)S(1)}, bf16[16,48,128]{2,1,0:T(8,128)(2,1)S(1)}, u32[]{:S(2)}, u32[]{:S(2)}) %collective-permute-start.11) | collective-permute-done | bytes 196640 | tf_op jit(solution)/shard_map/ppermute | solution.py:177
  102.6 21.1 %sweep.3 = (f32[48,48,128]{2,1,0:T(8,128)S(1)}, f32[16,16,128]{2,1,0:T(8,128)S(1)}) custom-call(s32[48]{0:T(128)S(1)} %pad_dynamic-slice_fusion.index_ref, s32[96]{0:T(128)S(1)} %select_reduce_fusion.slot_ref, s32[6]{0:T(128)S(1)} %convert_reduce_fusion.cover_ref, f32[6,33]{1,0:T(8,128)S(1)} %broadcast_divide_fusion.axial_ref, f32[8,128]{1,0:T(8,128)S(1)} %pad.13.ax_ref, ...), custom_call_target="tpu_custom_call" | custom-call | tf_op jit(solution)/shard_map/sweep/pallas_call | solution.py:211
  123.8 3.5 %collective-permute-start.12 = (f32[16,48,128]{2,1,0:T(8,128)S(1)}, f32[16,48,128]{2,1,0:T(8,128)S(1)}, u32[]{:S(2)}, u32[]{:S(2)}) collective-permute-start(f32[16,48,128]{2,1,0:T(8,128)S(1)} %get-tuple-element.15), channel_id=1, source_target_pairs={{0,1},{1,2},{2,3},{3,4},{4,5},{5,6},{6,7},{7,8},{8,9},{9,10},{10,1... | collective-permute-start | bytes 1179656 | tf_op jit(solution)/shard_map/ppermute | solution.py:183
  127.3 1.9 %collective-permute-start.13 = (f32[16,48,128]{2,1,0:T(8,128)S(1)}, f32[16,48,128]{2,1,0:T(8,128)S(1)}, u32[]{:S(2)}, u32[]{:S(2)}) collective-permute-start(f32[16,48,128]{2,1,0:T(8,128)S(1)} %get-tuple-element.16), channel_id=1, source_target_pairs={{1,0},{2,1},{3,2},{4,3},{5,4},{6,5},{7,6},{8,7},{9,8},{10,9},{11,1... | collective-permute-start | bytes 1179656 | tf_op jit(solution)/shard_map/ppermute | solution.py:183
  129.2 2.8 %collective-permute-done.12 = f32[16,48,128]{2,1,0:T(8,128)S(1)} collective-permute-done((f32[16,48,128]{2,1,0:T(8,128)S(1)}, f32[16,48,128]{2,1,0:T(8,128)S(1)}, u32[]{:S(2)}, u32[]{:S(2)}) %collective-permute-start.12) | collective-permute-done | bytes 393248 | tf_op jit(solution)/shard_map/ppermute | solution.py:183
  132.0 5.4 %collective-permute-done.13 = f32[16,48,128]{2,1,0:T(8,128)S(1)} collective-permute-done((f32[16,48,128]{2,1,0:T(8,128)S(1)}, f32[16,48,128]{2,1,0:T(8,128)S(1)}, u32[]{:S(2)}, u32[]{:S(2)}) %collective-permute-start.13) | collective-permute-done | bytes 393248 | tf_op jit(solution)/shard_map/ppermute | solution.py:183
  137.4 6.9 %collective-permute-start.14 = (f32[16,16,128]{2,1,0:T(8,128)S(1)}, f32[16,16,128]{2,1,0:T(8,128)S(1)}, u32[]{:S(2)}, u32[]{:S(2)}) collective-permute-start(f32[16,16,128]{2,1,0:T(8,128)S(1)} %get-tuple-element.19), channel_id=1, source_target_pairs={{0,16},{16,32},{32,48},{48,64},{64,80},{80,96},{96,112},{1,17},{17... | collective-permute-start | bytes 393224 | tf_op jit(solution)/shard_map/ppermute | solution.py:183
  144.4 1.9 %collective-permute-start.15 = (f32[16,16,128]{2,1,0:T(8,128)S(1)}, f32[16,16,128]{2,1,0:T(8,128)S(1)}, u32[]{:S(2)}, u32[]{:S(2)}) collective-permute-start(f32[16,16,128]{2,1,0:T(8,128)S(1)} %get-tuple-element.20), channel_id=1, source_target_pairs={{16,0},{32,16},{48,32},{64,48},{80,64},{96,80},{112,96},{17,1},{33... | collective-permute-start | bytes 393224 | tf_op jit(solution)/shard_map/ppermute | solution.py:183
  146.3 6.2 %collective-permute-done.15 = f32[16,16,128]{2,1,0:T(8,128)S(1)} collective-permute-done((f32[16,16,128]{2,1,0:T(8,128)S(1)}, f32[16,16,128]{2,1,0:T(8,128)S(1)}, u32[]{:S(2)}, u32[]{:S(2)}) %collective-permute-start.15) | collective-permute-done | bytes 131104 | tf_op jit(solution)/shard_map/ppermute | solution.py:183
  152.5 0.7 fusion.3
  (39 shorter events, 1.5 us)
Async XLA Ops:
  0.0 21.5 %copy-start.2 = (f32[6,33]{1,0:T(8,128)S(1)}, f32[6,33]{1,0:T(8,128)}, u32[]{:S(2)}) copy-start(f32[6,33]{1,0:T(8,128)} %param.10) | copy-start | bytes 2380
  0.0 21.7 %copy-start.1 = (f32[6,16,2,33]{3,2,1,0:T(2,128)S(1)}, f32[6,16,2,33]{3,2,1,0:T(2,128)}, u32[]{:S(2)}) copy-start(f32[6,16,2,33]{3,2,1,0:T(2,128)} %param.9) | copy-start | bytes 76036
  1.0 21.7 %collective-permute-start.1 = (bf16[16,16,128]{2,1,0:T(8,128)(2,1)S(1)}, bf16[16,16,128]{2,1,0:T(8,128)(2,1)S(1)}, u32[]{:S(2)}, u32[]{:S(2)}) collective-permute-start(bf16[16,16,128]{2,1,0:T(8,128)(2,1)S(1)} %convert_element_type.16), channel_id=1, source_target_pairs={{16,0},{32,16},{48,32},{64,48},{80,64},{96,80},{112,96},{17,1},{33... | collective-permute-start | bytes 196616 | tf_op jit(solution)/shard_map/ppermute | solution.py:177
  2.9 19.8 %collective-permute-start = (bf16[16,16,128]{2,1,0:T(8,128)(2,1)S(1)}, bf16[16,16,128]{2,1,0:T(8,128)(2,1)S(1)}, u32[]{:S(2)}, u32[]{:S(2)}) collective-permute-start(bf16[16,16,128]{2,1,0:T(8,128)(2,1)S(1)} %convert_element_type.16), channel_id=1, source_target_pairs={{0,16},{16,32},{32,48},{48,64},{64,80},{80,96},{96,112},{1,17},{17... | collective-permute-start | bytes 196616 | tf_op jit(solution)/shard_map/ppermute | solution.py:177
  8.7 13.6 %copy-start.4 = (s32[1,128]{1,0:T(1,128)S(1)}, s32[1,128]{1,0:T(1,128)}, u32[]{:S(2)}) copy-start(s32[1,128]{1,0:T(1,128)} %param.8) | copy-start | bytes 1540
  10.6 17.6 %copy-start.3 = (s32[256]{0:T(256)S(1)}, s32[256]{0:T(256)}, u32[]{:S(2)}) copy-start(s32[256]{0:T(256)} %param.11) | copy-start | bytes 3076
  10.6 23.8 %all-to-all-start = ((bf16[128,16,128]{2,1,0:T(8,128)(2,1)}), bf16[128,16,128]{2,1,0:T(8,128)(2,1)S(1)}, u32[]{:S(2)}, u32[]{:S(2)}) async-start(bf16[128,16,128]{2,1,0:T(8,128)(2,1)} %bitcast.6), calls=%async_computation | async-start | bytes 1048576 | tf_op jit(solution)/shard_map/all_to_all | solution.py:206
  22.7 11.7 %collective-permute-start.3 = (bf16[16,48,128]{2,1,0:T(8,128)(2,1)S(1)}, bf16[16,48,128]{2,1,0:T(8,128)(2,1)S(1)}, u32[]{:S(2)}, u32[]{:S(2)}) collective-permute-start(bf16[16,48,128]{2,1,0:T(8,128)(2,1)S(1)} %pad_maximum_fusion.2), channel_id=1, source_target_pairs={{1,0},{2,1},{3,2},{4,3},{5,4},{6,5},{7,6},{8,7},{9,8},{10,9},{11,1... | collective-permute-start | bytes 589832 | tf_op jit(solution)/shard_map/ppermute | solution.py:177
  25.0 9.4 %collective-permute-start.2 = (bf16[16,48,128]{2,1,0:T(8,128)(2,1)S(1)}, bf16[16,48,128]{2,1,0:T(8,128)(2,1)S(1)}, u32[]{:S(2)}, u32[]{:S(2)}) collective-permute-start(bf16[16,48,128]{2,1,0:T(8,128)(2,1)S(1)} %pad_maximum_fusion.2), channel_id=1, source_target_pairs={{0,1},{1,2},{2,3},{3,4},{4,5},{5,6},{6,7},{7,8},{8,9},{9,10},{10,1... | collective-permute-start | bytes 589832 | tf_op jit(solution)/shard_map/ppermute | solution.py:177
  55.6 27.6 %copy-start = (f32[16,16,128]{2,1,0:T(8,128)S(1)}, f32[16,16,128]{2,1,0:T(8,128)}, u32[]{:S(2)}) copy-start(f32[16,16,128]{2,1,0:T(8,128)} %param.6) | copy-start | bytes 393220
  55.6 6.8 %collective-permute-start.4 = (f32[16,48,128]{2,1,0:T(8,128)S(1)}, f32[16,48,128]{2,1,0:T(8,128)S(1)}, u32[]{:S(2)}, u32[]{:S(2)}) collective-permute-start(f32[16,48,128]{2,1,0:T(8,128)S(1)} %get-tuple-element.17), channel_id=1, source_target_pairs={{0,1},{1,2},{2,3},{3,4},{4,5},{5,6},{6,7},{7,8},{8,9},{9,10},{10,1... | collective-permute-start | bytes 1179656 | tf_op jit(solution)/shard_map/ppermute | solution.py:183
  57.6 12.1 %collective-permute-start.5 = (f32[16,48,128]{2,1,0:T(8,128)S(1)}, f32[16,48,128]{2,1,0:T(8,128)S(1)}, u32[]{:S(2)}, u32[]{:S(2)}) collective-permute-start(f32[16,48,128]{2,1,0:T(8,128)S(1)} %get-tuple-element.18), channel_id=1, source_target_pairs={{1,0},{2,1},{3,2},{4,3},{5,4},{6,5},{7,6},{8,7},{9,8},{10,9},{11,1... | collective-permute-start | bytes 1179656 | tf_op jit(solution)/shard_map/ppermute | solution.py:183
  69.9 7.2 %collective-permute-start.6 = (f32[16,16,128]{2,1,0:T(8,128)S(1)}, f32[16,16,128]{2,1,0:T(8,128)S(1)}, u32[]{:S(2)}, u32[]{:S(2)}) collective-permute-start(f32[16,16,128]{2,1,0:T(8,128)S(1)} %get-tuple-element.21), channel_id=1, source_target_pairs={{0,16},{16,32},{32,48},{48,64},{64,80},{80,96},{96,112},{1,17},{17... | collective-permute-start | bytes 393224 | tf_op jit(solution)/shard_map/ppermute | solution.py:183
  75.0 8.1 %collective-permute-start.7 = (f32[16,16,128]{2,1,0:T(8,128)S(1)}, f32[16,16,128]{2,1,0:T(8,128)S(1)}, u32[]{:S(2)}, u32[]{:S(2)}) collective-permute-start(f32[16,16,128]{2,1,0:T(8,128)S(1)} %get-tuple-element.22), channel_id=1, source_target_pairs={{16,0},{32,16},{48,32},{64,48},{80,64},{96,80},{112,96},{17,1},{33... | collective-permute-start | bytes 393224 | tf_op jit(solution)/shard_map/ppermute | solution.py:183
  83.2 7.7 %collective-permute-start.9 = (bf16[16,16,128]{2,1,0:T(8,128)(2,1)S(1)}, bf16[16,16,128]{2,1,0:T(8,128)(2,1)S(1)}, u32[]{:S(2)}, u32[]{:S(2)}) collective-permute-start(bf16[16,16,128]{2,1,0:T(8,128)(2,1)S(1)} %get-tuple-element.13), channel_id=1, source_target_pairs={{16,0},{32,16},{48,32},{64,48},{80,64},{96,80},{112,96},{17,1},{33... | collective-permute-start | bytes 196616 | tf_op jit(solution)/shard_map/ppermute | solution.py:177
  85.1 7.1 %collective-permute-start.8 = (bf16[16,16,128]{2,1,0:T(8,128)(2,1)S(1)}, bf16[16,16,128]{2,1,0:T(8,128)(2,1)S(1)}, u32[]{:S(2)}, u32[]{:S(2)}) collective-permute-start(bf16[16,16,128]{2,1,0:T(8,128)(2,1)S(1)} %get-tuple-element.13), channel_id=1, source_target_pairs={{0,16},{16,32},{32,48},{48,64},{64,80},{80,96},{96,112},{1,17},{17... | collective-permute-start | bytes 196616 | tf_op jit(solution)/shard_map/ppermute | solution.py:177
  92.2 10.4 %collective-permute-start.11 = (bf16[16,48,128]{2,1,0:T(8,128)(2,1)S(1)}, bf16[16,48,128]{2,1,0:T(8,128)(2,1)S(1)}, u32[]{:S(2)}, u32[]{:S(2)}) collective-permute-start(bf16[16,48,128]{2,1,0:T(8,128)(2,1)S(1)} %pad_maximum_fusion.3), channel_id=1, source_target_pairs={{1,0},{2,1},{3,2},{4,3},{5,4},{6,5},{7,6},{8,7},{9,8},{10,9},{11,1... | collective-permute-start | bytes 589832 | tf_op jit(solution)/shard_map/ppermute | solution.py:177
  94.2 8.4 %collective-permute-start.10 = (bf16[16,48,128]{2,1,0:T(8,128)(2,1)S(1)}, bf16[16,48,128]{2,1,0:T(8,128)(2,1)S(1)}, u32[]{:S(2)}, u32[]{:S(2)}) collective-permute-start(bf16[16,48,128]{2,1,0:T(8,128)(2,1)S(1)} %pad_maximum_fusion.3), channel_id=1, source_target_pairs={{0,1},{1,2},{2,3},{3,4},{4,5},{5,6},{6,7},{7,8},{8,9},{9,10},{10,1... | collective-permute-start | bytes 589832 | tf_op jit(solution)/shard_map/ppermute | solution.py:177
  123.8 8.2 %collective-permute-start.12 = (f32[16,48,128]{2,1,0:T(8,128)S(1)}, f32[16,48,128]{2,1,0:T(8,128)S(1)}, u32[]{:S(2)}, u32[]{:S(2)}) collective-permute-start(f32[16,48,128]{2,1,0:T(8,128)S(1)} %get-tuple-element.15), channel_id=1, source_target_pairs={{0,1},{1,2},{2,3},{3,4},{4,5},{5,6},{6,7},{7,8},{8,9},{9,10},{10,1... | collective-permute-start | bytes 1179656 | tf_op jit(solution)/shard_map/ppermute | solution.py:183
  127.3 10.1 %collective-permute-start.13 = (f32[16,48,128]{2,1,0:T(8,128)S(1)}, f32[16,48,128]{2,1,0:T(8,128)S(1)}, u32[]{:S(2)}, u32[]{:S(2)}) collective-permute-start(f32[16,48,128]{2,1,0:T(8,128)S(1)} %get-tuple-element.16), channel_id=1, source_target_pairs={{1,0},{2,1},{3,2},{4,3},{5,4},{6,5},{7,6},{8,7},{9,8},{10,9},{11,1... | collective-permute-start | bytes 1179656 | tf_op jit(solution)/shard_map/ppermute | solution.py:183
  137.4 8.9 %collective-permute-start.14 = (f32[16,16,128]{2,1,0:T(8,128)S(1)}, f32[16,16,128]{2,1,0:T(8,128)S(1)}, u32[]{:S(2)}, u32[]{:S(2)}) collective-permute-start(f32[16,16,128]{2,1,0:T(8,128)S(1)} %get-tuple-element.19), channel_id=1, source_target_pairs={{0,16},{16,32},{32,48},{48,64},{64,80},{80,96},{96,112},{1,17},{17... | collective-permute-start | bytes 393224 | tf_op jit(solution)/shard_map/ppermute | solution.py:183
  144.4 8.1 %collective-permute-start.15 = (f32[16,16,128]{2,1,0:T(8,128)S(1)}, f32[16,16,128]{2,1,0:T(8,128)S(1)}, u32[]{:S(2)}, u32[]{:S(2)}) collective-permute-start(f32[16,16,128]{2,1,0:T(8,128)S(1)} %get-tuple-element.20), channel_id=1, source_target_pairs={{16,0},{32,16},{48,32},{64,48},{80,64},{96,80},{112,96},{17,1},{33... | collective-permute-start | bytes 393224 | tf_op jit(solution)/shard_map/ppermute | solution.py:183

commit v2 on v1

--- a/solution.py
+++ b/solution.py
@@ -104,7 +104,7 @@
     return range(max(0, zi - 2 * HALO), min(BLK - 1, zi) + 1)
 
 
-def axial_and_ratio(axial_ref, slot_ref, cover_ref, grown, tiles, spread):
+def axial_and_ratio(axial_ref, slot_ref, cover_ref, grown, tile_of, spread):
     @pl.loop(0, VIEWS)
     def _(v):
         weights = [axial_ref[v, t] for t in range(TAPS)]
@@ -119,7 +119,7 @@
                     total[zo] = term if total[zo] is None else total[zo] + term
             excess = []
             for zo in range(BLK):
-                tile = tiles[slot_ref[v * BLK + zo]][rows].astype(F32)
+                tile = tile_of(slot_ref[v * BLK + zo])[rows].astype(F32)
                 ratio = (tile / total[zo]).astype(BF).astype(F32)
                 excess.append(jnp.where(seen, ratio - 1.0, 0.0))
             for zi in range(NEAR):
@@ -130,28 +130,168 @@
                 spread[v, zi, rows, :] = acc.astype(BF)
 
 
-def sweep_kernel(depths, cols):
-    def body(index_ref, slot_ref, cover_ref, axial_ref, ax_ref, kx_ref, ky_ref, wide_ref, tiles,
-             out_ref, base_ref, fwd_y, bwd_y, fwd_x, bwd_x, edge_x, edge_y, mid, grown, spread):
-        col0 = lax.axis_index("gx") * BLK
-        depth0 = lax.axis_index("gz") * BLK
-        build_bands(kx_ref, ky_ref, fwd_y, bwd_y, fwd_x, bwd_x)
-        ones_response(index_ref, ax_ref, kx_ref, ky_ref, col0, depth0, edge_x, edge_y, base_ref, cols, depths)
-        lateral_forward(index_ref, fwd_x, fwd_y, wide_ref, mid, grown, 0, NEAR, 4)
-        axial_and_ratio(axial_ref, slot_ref, cover_ref, grown, tiles, spread)
-        lateral_backward(index_ref, bwd_x, bwd_y, spread, mid, out_ref, 0, NEAR, 4)
+LOW, OWN, HIGH = slice(0, BLK), slice(BLK, 2 * BLK), slice(2 * BLK, NEAR)
+
+
+class Copy:
+    def __init__(self, src, dst, sems, slot, device, sends, receives):
+        self.sends, self.receives = sends, receives
+        self.copy = pltpu.make_async_remote_copy(
+            src_ref=src, dst_ref=dst, send_sem=sems[0].at[slot], recv_sem=sems[1].at[slot],
+            device_id=device, device_id_type=pl.DeviceIdType.MESH,
+        )
+
+    def start(self):
+        pl.when(self.sends)(self.copy.start)
+
+    def wait_recv(self):
+        pl.when(self.receives)(self.copy.wait_recv)
+
+    def wait_send(self):
+        pl.when(self.sends)(self.copy.wait_send)
+
+
+def joint_kernel(nx, nz):
+    def body(index_ref, slot_ref, cover_ref, axial_ref, ax_ref, kx_ref, ky_ref, estimate_ref, outgoing,
+             out_ref, fwd_y, bwd_y, fwd_x, bwd_x, edge_x, edge_y, base, mid, grown, spread, total,
+             wide, part_z, side, part_x, passing, arrived,
+             halo_sems, sum_sems, first_send, first_recv, second_send, second_recv, local_sems):
+        gx, gz = lax.axis_index("gx"), lax.axis_index("gz")
+        has_l, has_r, has_d, has_u = gx > 0, gx < nx - 1, gz > 0, gz < nz - 1
+        left, right = (lax.rem(gx + nx - 1, nx), gz), (lax.rem(gx + 1, nx), gz)
+        down, up = (gx, lax.rem(gz + nz - 1, nz)), (gx, lax.rem(gz + 1, nz))
+        halo_s, halo_r = halo_sems
+        sum_s, sum_r = sum_sems
+
+        for it in range(ITERS):
+            wide[it] = jnp.zeros_like(wide[it])
+        part_z[...] = jnp.zeros_like(part_z)
+        part_x[...] = jnp.zeros_like(part_x)
+        wide[0, OWN, OWN] = estimate_ref[...].astype(BF)
+
+        barrier = pltpu.get_barrier_semaphore()
+        for d in range(1, nz):
+            pl.semaphore_signal(barrier, inc=1, device_id=(gx, lax.rem(gz + d, nz)), device_id_type=pl.DeviceIdType.MESH)
+        for d in range(1, nx):
+            pl.semaphore_signal(barrier, inc=1, device_id=(lax.rem(gx + d, nx), gz), device_id_type=pl.DeviceIdType.MESH)
+        pl.semaphore_wait(barrier, nx + nz - 2)
+
+        def halo(it):
+            w = wide.at[it]
+            sems = (halo_s.at[it], halo_r.at[it])
+            own = w.at[OWN, OWN]
+            near = [
+                Copy(own, w.at[OWN, LOW], sems, 0, right, has_r, has_l),
+                Copy(own, w.at[OWN, HIGH], sems, 1, left, has_l, has_r),
+            ]
+            far = [
+                Copy(own, w.at[LOW, OWN], sems, 2, up, has_u, has_d),
+                Copy(own, w.at[HIGH, OWN], sems, 3, down, has_d, has_u),
+            ]
+            corner = [
+                Copy(w.at[OWN, LOW], w.at[LOW, LOW], sems, 4, up, has_u & has_l, has_d & has_l),
+                Copy(w.at[OWN, LOW], w.at[HIGH, LOW], sems, 5, down, has_d & has_l, has_u & has_l),
+                Copy(w.at[OWN, HIGH], w.at[LOW, HIGH], sems, 6, up, has_u & has_r, has_d & has_r),
+                Copy(w.at[OWN, HIGH], w.at[HIGH, HIGH], sems, 7, down, has_d & has_r, has_u & has_r),
+            ]
+            return near, far, corner
+
+        def sums(it):
+            sems = (sum_s.at[it], sum_r.at[it])
+            return (
+                Copy(total.at[LOW], part_z.at[it, 1], sems, 0, down, has_d, has_u),
+                Copy(total.at[HIGH], part_z.at[it, 0], sems, 1, up, has_u, has_d),
+                Copy(side.at[0], part_x.at[it, 1], sems, 2, left, has_l, has_r),
+                Copy(side.at[1], part_x.at[it, 0], sems, 3, right, has_r, has_l),
+            )
+
+        def along_gz(d):
+            return pltpu.make_async_remote_copy(
+                src_ref=outgoing.at[:, lax.rem(gz + d, nz)], dst_ref=passing.at[:, gz],
+                send_sem=first_send.at[d], recv_sem=first_recv.at[d],
+                device_id=(gx, lax.rem(gz + d, nz)), device_id_type=pl.DeviceIdType.MESH,
+            )
+
+        def along_gx(d):
+            return pltpu.make_async_remote_copy(
+                src_ref=passing.at[lax.rem(gx + d, nx)], dst_ref=arrived.at[gx],
+                send_sem=second_send.at[d], recv_sem=second_recv.at[d],
+                device_id=(lax.rem(gx + d, nx), gz), device_id_type=pl.DeviceIdType.MESH,
+            )
+
+        for it in range(ITERS):
+            near, far, corner = halo(it)
+            for copy in near + far:
+                copy.start()
+            if it == 0:
+                keep = pltpu.make_async_copy(outgoing.at[:, gz], passing.at[:, gz], local_sems.at[0])
+                keep.start()
+                for d in range(1, nz):
+                    along_gz(d).start()
+                build_bands(kx_ref, ky_ref, fwd_y, bwd_y, fwd_x, bwd_x)
+            for copy in near:
+                copy.wait_recv()
+            for copy in corner:
+                copy.start()
+            lateral_forward(index_ref, fwd_x, fwd_y, wide.at[it], mid, grown, BLK, 2 * BLK, 4)
+            if it == 0:
+                keep.wait()
+                for d in range(1, nz):
+                    along_gz(d).wait_recv()
+                for d in range(1, nx):
+                    along_gx(d).start()
+                stay = pltpu.make_async_copy(passing.at[gx], arrived.at[gx], local_sems.at[1])
+                stay.start()
+            for copy in far + corner:
+                copy.wait_recv()
+            lateral_forward(index_ref, fwd_x, fwd_y, wide.at[it], mid, grown, 0, BLK, 4)
+            lateral_forward(index_ref, fwd_x, fwd_y, wide.at[it], mid, grown, 2 * BLK, NEAR, 4)
+            if it == 0:
+                ones_response(index_ref, ax_ref, kx_ref, ky_ref, gx * BLK, gz * BLK, edge_x, edge_y, base,
+                              nx * BLK, nz * BLK)
+                for d in range(1, nz):
+                    along_gz(d).wait_send()
+                for d in range(1, nx):
+                    along_gx(d).wait()
+                stay.wait()
+            for copy in near + far + corner:
+                copy.wait_send()
+
+            axial_and_ratio(axial_ref, slot_ref, cover_ref, grown,
+                            lambda s: arrived[s // nz, lax.rem(s, nz)], spread)
+            below, above, to_left, to_right = sums(it)
+            lateral_backward(index_ref, bwd_x, bwd_y, spread, mid, total, 0, BLK, 4)
+            below.start()
+            lateral_backward(index_ref, bwd_x, bwd_y, spread, mid, total, 2 * BLK, NEAR, 4)
+            above.start()
+            lateral_backward(index_ref, bwd_x, bwd_y, spread, mid, total, BLK, 2 * BLK, 4)
+            below.wait_recv()
+            above.wait_recv()
+            reach = total[OWN] + part_z[it, 0] + part_z[it, 1]
+            side[0] = reach[:, LOW]
+            side[1] = reach[:, HIGH]
+            to_left.start()
+            to_right.start()
+            inner = base[...] + reach[:, OWN]
+            before = estimate_ref if it == 0 else out_ref
+            to_left.wait_recv()
+            to_right.wait_recv()
+            after = before[...] * ((inner + part_x[it, 0] + part_x[it, 1]) / VIEWS)
+            out_ref[...] = after
+            if it + 1 < ITERS:
+                wide[it + 1, OWN, OWN] = after.astype(BF)
+            for copy in (below, above, to_left, to_right):
+                copy.wait_send()
 
     smem = pl.BlockSpec(memory_space=pltpu.SMEM)
     vmem = pl.BlockSpec(memory_space=pltpu.VMEM)
+    dma = pltpu.SemaphoreType.DMA
     return pl.pallas_call(
         body,
-        name="sweep",
-        out_shape=(
-            jax.ShapeDtypeStruct((NEAR, NEAR, LINE), F32),
-            jax.ShapeDtypeStruct((BLK, BLK, LINE), F32),
-        ),
-        in_specs=[smem] * 4 + [vmem] * 5,
-        out_specs=(vmem, vmem),
+        name="joint",
+        out_shape=jax.ShapeDtypeStruct((BLK, BLK, LINE), F32),
+        in_specs=[smem] * 4 + [vmem] * 4 + [pl.BlockSpec(memory_space=pl.ANY)],
+        out_specs=vmem,
         scratch_shapes=[
             pltpu.VMEM((KERNELS, VIEWS, LINE, LINE), BF),
             pltpu.VMEM((KERNELS, VIEWS, LINE, LINE), BF),
@@ -159,28 +299,25 @@
             pltpu.VMEM((KERNELS, LINE, VIEWS * BLK), BF),
             pltpu.VMEM((KERNELS, 8, LINE), F32),
             pltpu.VMEM((KERNELS, 8, LINE), F32),
+            pltpu.VMEM((BLK, BLK, LINE), F32),
             pltpu.VMEM((NEAR, VIEWS * BLK, LINE), BF),
             pltpu.VMEM((VIEWS, NEAR, BLK, LINE), F32),
             pltpu.VMEM((VIEWS, NEAR, BLK, LINE), BF),
+            pltpu.VMEM((NEAR, NEAR, LINE), F32),
+            pltpu.VMEM((ITERS, NEAR, NEAR, LINE), BF),
+            pltpu.VMEM((ITERS, 2, BLK, NEAR, LINE), F32),
+            pltpu.VMEM((2, BLK, BLK, LINE), F32),
+            pltpu.VMEM((ITERS, 2, BLK, BLK, LINE), F32),
+            pltpu.VMEM((nx, nz, BLK, LINE), BF),
+            pltpu.VMEM((nx, nz, BLK, LINE), BF),
+            (dma((ITERS, 8)), dma((ITERS, 8))),
+            (dma((ITERS, 4)), dma((ITERS, 4))),
+            dma((nz,)), dma((nz,)), dma((nx,)), dma((nx,)), dma((2,)),
         ],
-        compiler_params=pltpu.CompilerParams(vmem_limit_bytes=48 << 20),
+        compiler_params=pltpu.CompilerParams(
+            vmem_limit_bytes=48 << 20, collective_id=0, has_side_effects=True
+        ),
     )
-
-
-def pairs(axis):
-    up = [(i, i + 1) for i in range(lax.axis_size(axis) - 1)]
-    return up, [(j, i) for i, j in up]
-
-
-def extended(x, axis, dim):
-    up, down = pairs(axis)
-    return jnp.concatenate([lax.ppermute(x, axis, up), x, lax.ppermute(x, axis, down)], axis=dim)
-
-
-def gathered(x, axis, dim):
-    up, down = pairs(axis)
-    low, own, high = (lax.slice_in_dim(x, i * BLK, (i + 1) * BLK, axis=dim) for i in range(3))
-    return own + lax.ppermute(high, axis, up) + lax.ppermute(low, axis, down)
 
 
 def small_tables(incoming_label, lateral_bank, axial_kernel, kernel_index):
@@ -199,19 +336,11 @@
 
 
 def shards(estimate, view_tiles, incoming_label, lateral_bank, axial_kernel, kernel_index):
-    depths = lax.axis_size("gz") * BLK
-    cols = lax.axis_size("gx") * BLK
-    axial, ax, kx, ky, near, slot, cover = small_tables(incoming_label, lateral_bank, axial_kernel, kernel_index)
-    outgoing = view_tiles[0].reshape(-1, BLK, LINE)
-    tiles = lax.all_to_all(outgoing, ("gx", "gz"), split_axis=0, concat_axis=0, tiled=True)
-    sweep = sweep_kernel(depths, cols)
-    joined = estimate
-    for _ in range(ITERS):
-        wide = extended(extended(joined.astype(BF), "gx", 1), "gz", 0)
-        part, base = sweep(near, slot, cover, axial, ax, kx, ky, wide, tiles)
-        part = gathered(part, "gz", 0)
-        joined = joined * ((base + gathered(part, "gx", 1)) / VIEWS)
-    return joined
+    nx, nz = lax.axis_size("gx"), lax.axis_size("gz")
+    tables = small_tables(incoming_label, lateral_bank, axial_kernel, kernel_index)
+    axial, ax, kx, ky, near, slot, cover = tables
+    outgoing = view_tiles[0].reshape(nx, nz, BLK, LINE)
+    return joint_kernel(nx, nz)(near, slot, cover, axial, ax, kx, ky, estimate, outgoing)
 
 
 def solution(mesh):

time: 154 us -> 101 us (0.66)
  the two profiles are of different devices: /device:TPU:71 before, /device:TPU:19 now
where the time goes in v2:
time: 101 us
  Pallas kernels  93.2 us (92%)
  other arithmetic  5.34 us (5%)
  local copies, waits for them, and re-layouts  2.59 us (3%)
    pallas_call x1, Pallas kernels, shards(): joint_kernel(nx, nz)  93.2 us

profile of v2, /device:TPU:19, one launch (start us, length us, event | category | flops | bytes accessed | tf_op | source)
XLA Modules:
  0.0 101.2 jit_solution(14475365026259320831)
XLA Ops:
  0.0 0.0 copy-start.1
  0.0 0.8 pad_dynamic-slice_fusion.index_ref
  0.8 0.8 select_reduce_fusion.slot_ref
  1.6 0.8 reduce_sum.38
  2.4 0.8 broadcast_divide_fusion.axial_ref
  3.2 0.9 convert_reduce_fusion.cover_ref
  4.1 1.1 %reduce_sum.39 = f32[6,16,2]{2,1,0:T(8,128)S(1)} reduce(f32[6,16,2,33]{3,2,1,0:T(2,128)} %param.9, f32[]{:T(128)} %constant.13.clone.1), dimensions={3}, to_apply=%region_3.4 | reduce | flops 6144 | bytes 26116 | tf_op jit(solution)/shard_map/reduce_sum | solution.py:324
  5.2 0.2 copy.10
  5.4 1.0 fusion
  6.4 0.0 copy-done.1
  6.4 0.0 copy-start
  6.4 0.1 copy.12
  6.5 0.8 copy-done
  7.3 93.2 %joint.1 = f32[16,16,128]{2,1,0:T(8,128)S(1)} custom-call(s32[48]{0:T(128)S(1)} %pad_dynamic-slice_fusion.index_ref, s32[96]{0:T(128)S(1)} %select_reduce_fusion.slot_ref, s32[6]{0:T(128)S(1)} %convert_reduce_fusion.cover_ref, f32[6,33]{1,0:T(8,128)S(1)} %broadcast_divide_fusion.axial_ref, f32[8,128]{1,0:T(8,128)S(1)} %pad.13.ax_ref, ...), custom_call_target="tpu_custom_call" | custom-call | tf_op jit(solution)/shard_map/joint/pallas_call | solution.py:343
  100.5 0.7 copy.17
  (3 shorter events, 0.0 us)
Async XLA Ops:
  0.0 6.4 %copy-start.1 = (bf16[1,128,2048]{2,1,0:T(8,128)(2,1)S(1)}, bf16[1,128,2048]{2,1,0:T(8,128)(2,1)}, u32[]{:S(2)}) copy-start(bf16[1,128,2048]{2,1,0:T(8,128)(2,1)} %param.7) | copy-start | bytes 1572868
  6.4 0.9 copy-start

commit v3 on v2

v3 whole, which is shorter than its diff:
```python
import jax
import jax.numpy as jnp
from jax import lax
from jax.experimental import pallas as pl
from jax.experimental.pallas import tpu as pltpu
from jax.sharding import PartitionSpec as P

TAPS = 33
ITERS = 2
HALO = 16
VIEWS = 6
KERNELS = 16
BLK = 16
NEAR = 48
LINE = 128
F32 = jnp.float32
BF = jnp.bfloat16
HI = lax.Precision.HIGHEST


def iota(shape, dim):
    return lax.broadcasted_iota(jnp.int32, shape, dim)


def load_taps(bank_ref, axial_in, kx, ky, ax):
    ax[...] = jnp.zeros_like(ax)
    ax[:VIEWS, :TAPS] = axial_in[...]
    for dim, taps in ((0, kx), (1, ky)):
        taps[...] = jnp.zeros_like(taps)
        for v in range(VIEWS):
            taps[:, v, :TAPS] = bank_ref[v, :, dim, :]
        raw = taps[...]
        total = jnp.sum(raw, axis=-1, keepdims=True)
        taps[...] = raw / jnp.where(total > 0.0, total, 1.0)


def build_bands(kx_ref, ky_ref, ax, fwd_y, bwd_y, fwd_x, bwd_x, first, last):
    inside = jnp.abs(iota((LINE, LINE), 0) - iota((LINE, LINE), 1)) <= HALO
    axial = jnp.sum(ax[...], axis=1, keepdims=True)
    scale = jnp.broadcast_to(1.0 / jnp.where(axial > 0.0, axial, 1.0), (8, LINE))

    @pl.loop(first, last)
    def _(k):
        kx = kx_ref[k]
        ky = ky_ref[k] * scale
        rows = []
        for v in range(VIEWS):
            band = pltpu.roll(jnp.broadcast_to(ky[v : v + 1], (LINE, LINE)), LINE - HALO, 1, stride=1, stride_axis=0)
            band = jnp.where(inside, band, 0.0)
            bwd_y[k, v] = band.astype(BF)
            fwd_y[k, v] = band.T.astype(BF)
            rows.append(pltpu.roll(jnp.broadcast_to(kx[v : v + 1], (BLK, LINE)), 0, 1, stride=1, stride_axis=0))
        across = jnp.concatenate(rows, 0)
        fwd_x[k] = across.astype(BF)
        bwd_x[k] = across.T.astype(BF)


def ones_response(index_of, ax, kx_ref, ky_ref, col0, depth0, edge_x, edge_y, base_ref, cols, depths):
    tap = iota((LINE, LINE), 0)
    pos = iota((LINE, LINE), 1)
    at_x = col0 + pos - tap + HALO
    at_y = pos - tap + HALO
    ok_x = jnp.where((at_x >= 0) & (at_x < cols), 1.0, 0.0)
    ok_y = jnp.where((at_y >= 0) & (at_y < LINE), 1.0, 0.0)
    kx = kx_ref[...].reshape(KERNELS * 8, LINE)
    ky = ky_ref[...].reshape(KERNELS * 8, LINE)
    edge_x[...] = jnp.dot(kx, ok_x, precision=HI, preferred_element_type=F32).reshape(KERNELS, 8, LINE)
    edge_y[...] = jnp.dot(ky, ok_y, precision=HI, preferred_element_type=F32).reshape(KERNELS, 8, LINE)
    axial = ax[...]
    total = jnp.sum(axial, axis=1, keepdims=True)
    axial = axial / jnp.where(total > 0.0, total, 1.0)
    lane = iota((8, LINE), 1)
    for z in range(BLK):
        k = index_of(HALO + z)
        at_z = depth0 + z - lane + HALO
        part = jnp.sum(jnp.where((at_z >= 0) & (at_z < depths), axial, 0.0), axis=1, keepdims=True)
        left = edge_x[k][:, :BLK] * part
        base_ref[z] = lax.dot_general(
            left, edge_y[k], (((0,), (0,)), ((), ())), precision=HI, preferred_element_type=F32
        )


def slots_of(labels, slots):
    column = jnp.broadcast_to(labels, (LINE, LINE)).T
    hit = column == iota((LINE, LINE), 1)
    slots[...] = jnp.max(jnp.where(hit, iota((LINE, LINE), 0), -1), axis=0, keepdims=True)


def lateral_forward(index_of, fwd_x, fwd_y, wide_ref, mid, grown, first, last, unroll):
    @pl.loop(first // unroll, last // unroll)
    def _(s):
        for u in range(unroll):
            z = s * unroll + u
            k = index_of(z)
            mid[z] = jnp.dot(fwd_x[k][:, :NEAR], wide_ref[z], preferred_element_type=F32).astype(BF)

    @pl.loop(first // unroll, last // unroll)
    def _(s):
        for u in range(unroll):
            z = s * unroll + u
            k = index_of(z)
            for v in range(VIEWS):
                grown[v, z] = jnp.dot(mid[z, v * BLK : (v + 1) * BLK, :], fwd_y[k, v], preferred_element_type=F32)


def lateral_backward(index_of, bwd_x, bwd_y, spread, mid, out_ref, first, last, unroll):
    @pl.loop(first // unroll, last // unroll)
    def _(s):
        for u in range(unroll):
            z = s * unroll + u
            k = index_of(z)
            for v in range(VIEWS):
                mid[z, v * BLK : (v + 1) * BLK, :] = jnp.dot(
                    spread[v, z], bwd_y[k, v], preferred_element_type=F32
                ).astype(BF)

    @pl.loop(first // unroll, last // unroll)
    def _(s):
        for u in range(unroll):
            z = s * unroll + u
            k = index_of(z)
            out_ref[z] = jnp.dot(bwd_x[k][:NEAR], mid[z], preferred_element_type=F32).astype(out_ref.dtype)


def taps_over(zi):
    return range(max(0, zi - 2 * HALO), min(BLK - 1, zi) + 1)


def axial_and_ratio(axial_ref, slot_ref, grown, tile_of, spread):
    @pl.loop(0, VIEWS)
    def _(v):
        weights = [axial_ref[v, t] for t in range(TAPS)]
        seen = jnp.full((8, LINE), slot_ref[0, v * BLK], jnp.int32) >= 0
        for half in range(2):
            rows = slice(half * 8, half * 8 + 8)
            total = [None] * BLK
            for zi in range(NEAR):
                g = grown[v, zi, rows, :]
                for zo in taps_over(zi):
                    term = weights[zi - zo] * g
                    total[zo] = term if total[zo] is None else total[zo] + term
            excess = []
            for zo in range(BLK):
                tile = tile_of(jnp.maximum(slot_ref[0, v * BLK + zo], 0))[rows].astype(F32)
                ratio = (tile / total[zo]).astype(BF).astype(F32)
                excess.append(jnp.where(seen, ratio - 1.0, 0.0))
            for zi in range(NEAR):
                acc = None
                for zo in taps_over(zi):
                    term = weights[zi - zo] * excess[zo]
                    acc = term if acc is None else acc + term
                spread[v, zi, rows, :] = acc.astype(BF)


LOW, OWN, HIGH = slice(0, BLK), slice(BLK, 2 * BLK), slice(2 * BLK, NEAR)
MESH = pl.DeviceIdType.MESH


def worker_of(bx, bz):
    turn_x = bx // 4
    y = bx + turn_x * (7 - 2 * bx)
    chip = bz // 2
    turn_z = chip // 4
    x = chip + turn_z * (7 - 2 * chip)
    return 2 * y + turn_x, 4 * x + 2 * ((turn_x + turn_z) % 2) + bz % 2


def column_turn(gz, turn_x):
    x = gz // 4
    turn_z = (turn_x + (gz // 2) % 2) % 2
    return 2 * (x + turn_z * (7 - 2 * x)) + gz % 2


def row_of(gx):
    y = gx // 2
    return y + (gx % 2) * (7 - 2 * y)


class Copy:
    def __init__(self, src, dst, sems, slot, device, sends, receives):
        self.sends, self.receives = sends, receives
        self.copy = pltpu.make_async_remote_copy(
            src_ref=src, dst_ref=dst, send_sem=sems[0].at[slot], recv_sem=sems[1].at[slot],
            device_id=device, device_id_type=MESH,
        )

    def start(self):
        pl.when(self.sends)(self.copy.start)

    def wait_recv(self):
        pl.when(self.receives)(self.copy.wait_recv)

    def wait_send(self):
        pl.when(self.sends)(self.copy.wait_send)


def joint_kernel(nx, nz):
    def body(index_ref, axial_ref, axial_in, bank_ref, labels_ref, estimate_ref, outgoing,
             out_ref, kx, ky, ax, fwd_y, bwd_y, fwd_x, bwd_x, edge_x, edge_y, base, mid, grown, spread, total,
             staged, wide, part_z, part_x, product, back, passing, arrived, labels, slots, slot_ref,
             move_sems, halo_sems, sum_sems, first_sems, second_sems, local_sems):
        gx, gz = lax.axis_index("gx"), lax.axis_index("gz")
        bx = row_of(gx)
        bz = column_turn(gz, gx % 2)
        has_l, has_r, has_d, has_u = bx > 0, bx < nx - 1, bz > 0, bz < nz - 1
        left, right = worker_of((bx + nx - 1) % nx, bz), worker_of((bx + 1) % nx, bz)
        down, up = worker_of(bx, (bz + nz - 1) % nz), worker_of(bx, (bz + 1) % nz)
        worker = worker_of(gx, gz)
        owner = (bx, bz)
        moved = (bx != gx) | (bz != gz)

        def index_of(z):
            return index_ref[jnp.clip(bz * BLK - HALO + z, 0, nz * BLK - 1)]

        staged[...] = estimate_ref[...].astype(BF)
        for it in range(ITERS):
            for missing, rows, columns in (
                (bx == 0, slice(0, NEAR), LOW), (bx == nx - 1, slice(0, NEAR), HIGH),
                (bz == 0, LOW, slice(0, NEAR)), (bz == nz - 1, HIGH, slice(0, NEAR)),
            ):
                @pl.when(missing)
                def _():
                    region = wide.at[it, rows, columns]
                    region[...] = jnp.zeros(region.shape, BF)

        barrier = pltpu.get_barrier_semaphore()

        def greet(device):
            pl.semaphore_signal(barrier, inc=1, device_id=device, device_id_type=MESH)

        for d in range(1, nz):
            greet((gx, (gz + d) % nz))
        for d in range(1, nx):
            greet(((gx + d) % nx, gz))
        for there, device in ((has_l, left), (has_r, right), (has_d, down), (has_u, up), (moved, worker), (moved, owner)):
            pl.when(there)(lambda device=device: greet(device))
        extra = sum(there.astype(jnp.int32) for there in (has_l, has_r, has_d, has_u, moved, moved))
        pl.semaphore_wait(barrier, nx + nz - 2 + extra)

        own_0 = wide.at[0, OWN, OWN]
        moves = [
            Copy(staged, own_0, move_sems, 0, worker, moved, moved),
            Copy(labels_ref, labels, move_sems, 1, worker, moved, moved),
        ]
        bring = Copy(product, back, move_sems, 2, owner, moved, moved)

        def halo(it):
            w = wide.at[it]
            sems = (halo_sems[0].at[it], halo_sems[1].at[it])
            own = w.at[OWN, OWN]
            near = [
                Copy(own, w.at[OWN, LOW], sems, 0, right, has_r, has_l),
                Copy(own, w.at[OWN, HIGH], sems, 1, left, has_l, has_r),
            ]
            far = [
                Copy(own, w.at[LOW, OWN], sems, 2, up, has_u, has_d),
                Copy(own, w.at[HIGH, OWN], sems, 3, down, has_d, has_u),
            ]
            corner = [
                Copy(w.at[OWN, LOW], w.at[LOW, LOW], sems, 4, up, has_u & has_l, has_d & has_l),
                Copy(w.at[OWN, LOW], w.at[HIGH, LOW], sems, 5, down, has_d & has_l, has_u & has_l),
                Copy(w.at[OWN, HIGH], w.at[LOW, HIGH], sems, 6, up, has_u & has_r, has_d & has_r),
                Copy(w.at[OWN, HIGH], w.at[HIGH, HIGH], sems, 7, down, has_d & has_r, has_u & has_r),
            ]
            return near, far, corner

        def sums(it):
            sems = (sum_sems[0].at[it], sum_sems[1].at[it])
            return (
                Copy(total.at[LOW], part_z.at[it, 1], sems, 0, down, has_d, has_u),
                Copy(total.at[HIGH], part_z.at[it, 0], sems, 1, up, has_u, has_d),
                Copy(total.at[OWN, LOW], part_x.at[it, 1], sems, 2, left, has_l, has_r),
                Copy(total.at[OWN, HIGH], part_x.at[it, 0], sems, 3, right, has_r, has_l),
            )

        def quarter(turn, device_gz):
            return slice(4 * turn, 4 * turn + 4), column_turn(device_gz, turn)

        def along_gz(d, turn):
            target = (gz + d) % nz
            rows, column = quarter(turn, target)
            return pltpu.make_async_remote_copy(
                src_ref=outgoing.at[rows, column], dst_ref=passing.at[rows, gz],
                send_sem=first_sems[0].at[d, turn], recv_sem=first_sems[1].at[d, turn],
                device_id=(gx, target), device_id_type=MESH,
            )

        def stay_gz(turn):
            rows, column = quarter(turn, gz)
            return pltpu.make_async_copy(outgoing.at[rows, column], passing.at[rows, gz], local_sems.at[turn])

        def along_gx(d):
            target = (gx + d) % nx
            return pltpu.make_async_remote_copy(
                src_ref=passing.at[row_of(target)], dst_ref=arrived.at[gx],
                send_sem=second_sems[0].at[d], recv_sem=second_sems[1].at[d],
                device_id=(target, gz), device_id_type=MESH,
            )

        stay_gx = pltpu.make_async_copy(passing.at[bx], arrived.at[gx], local_sems.at[2])
        slot_copy = pltpu.make_async_copy(slots, slot_ref, local_sems.at[3])
        ends = [(d, turn) for d in range(1, nz) for turn in range(2)]

        for copy in moves:
            copy.start()

        @pl.when(jnp.logical_not(moved))
        def _():
            wide[0, OWN, OWN] = staged[...]
            labels[...] = labels_ref[...]

        for turn in range(2):
            stay_gz(turn).start()
        for d, turn in ends:
            along_gz(d, turn).start()
        load_taps(bank_ref, axial_in, kx, ky, ax)
        build_bands(kx, ky, ax, fwd_y, bwd_y, fwd_x, bwd_x, 0, KERNELS // 2)
        for copy in moves:
            copy.wait_recv()

        for it in range(ITERS):
            near, far, corner = halo(it)
            for copy in near + far:
                copy.start()
            if it == 0:
                build_bands(kx, ky, ax, fwd_y, bwd_y, fwd_x, bwd_x, KERNELS // 2, KERNELS)
            for copy in near:
                copy.wait_recv()
            for copy in corner:
                copy.start()
            if it == 0:
                slots_of(labels[...], slots)
                slot_copy.start()
                ones_response(index_of, ax, kx, ky, bx * BLK, bz * BLK, edge_x, edge_y, base, nx * BLK, nz * BLK)
            lateral_forward(index_of, fwd_x, fwd_y, wide.at[it], mid, grown, BLK, 2 * BLK, 4)
            if it == 0:
                for turn in range(2):
                    stay_gz(turn).wait()
                for d, turn in ends:
                    along_gz(d, turn).wait_recv()
                for d in range(1, nx):
                    along_gx(d).start()
                stay_gx.start()
            for copy in far + corner:
                copy.wait_recv()
            lateral_forward(index_of, fwd_x, fwd_y, wide.at[it], mid, grown, 0, BLK, 4)
            lateral_forward(index_of, fwd_x, fwd_y, wide.at[it], mid, grown, 2 * BLK, NEAR, 4)
            if it == 0:
                for d, turn in ends:
                    along_gz(d, turn).wait_send()
                for d in range(1, nx):
                    along_gx(d).wait()
                stay_gx.wait()
                slot_copy.wait()
                for copy in moves:
                    copy.wait_send()
            for copy in near + far + corner:
                copy.wait_send()

            axial_and_ratio(axial_ref, slot_ref, grown, lambda s: arrived[s // nz, s % nz], spread)
            below, above, to_left, to_right = sums(it)
            lateral_backward(index_of, bwd_x, bwd_y, spread, mid, total, 0, BLK, 4)
            below.start()
            lateral_backward(index_of, bwd_x, bwd_y, spread, mid, total, 2 * BLK, NEAR, 4)
            above.start()
            lateral_backward(index_of, bwd_x, bwd_y, spread, mid, total, BLK, 2 * BLK, 4)
            below.wait_recv()
            above.wait_recv()
            for there, which in ((has_d, 0), (has_u, 1)):
                @pl.when(there)
                def _():
                    total[OWN] += part_z[it, which]
            to_left.start()
            to_right.start()
            base_now = base[...] + total[OWN, OWN]
            gain = (1.0 / VIEWS) if it == 0 else product[...] * (1.0 / VIEWS)
            to_left.wait_recv()
            to_right.wait_recv()
            left_part = jnp.where(has_l, part_x[it, 0], 0.0)
            right_part = jnp.where(has_r, part_x[it, 1], 0.0)
            product[...] = (base_now + left_part + right_part) * gain
            if it + 1 < ITERS:
                wide[it + 1, OWN, OWN] = (wide[it, OWN, OWN].astype(F32) * product[...]).astype(BF)
            else:
                bring.start()
            for copy in (below, above, to_left, to_right):
                copy.wait_send()

        @pl.when(jnp.logical_not(moved))
        def _():
            back[...] = product[...]

        bring.wait_recv()
        out_ref[...] = estimate_ref[...] * back[...]
        bring.wait_send()

    smem = pl.BlockSpec(memory_space=pltpu.SMEM)
    vmem = pl.BlockSpec(memory_space=pltpu.VMEM)
    dma = pltpu.SemaphoreType.DMA
    block = (BLK, BLK, LINE)
    return pl.pallas_call(
        body,
        name="joint",
        out_shape=jax.ShapeDtypeStruct(block, F32),
        in_specs=[smem] * 2 + [vmem] * 4 + [pl.BlockSpec(memory_space=pl.ANY)],
        out_specs=vmem,
        scratch_shapes=[
            pltpu.VMEM((KERNELS, 8, LINE), F32),
            pltpu.VMEM((KERNELS, 8, LINE), F32),
            pltpu.VMEM((8, LINE), F32),
            pltpu.VMEM((KERNELS, VIEWS, LINE, LINE), BF),
            pltpu.VMEM((KERNELS, VIEWS, LINE, LINE), BF),
            pltpu.VMEM((KERNELS, VIEWS * BLK, LINE), BF),
            pltpu.VMEM((KERNELS, LINE, VIEWS * BLK), BF),
            pltpu.VMEM((KERNELS, 8, LINE), F32),
            pltpu.VMEM((KERNELS, 8, LINE), F32),
            pltpu.VMEM(block, F32),
            pltpu.VMEM((NEAR, VIEWS * BLK, LINE), BF),
            pltpu.VMEM((VIEWS, NEAR, BLK, LINE), F32),
            pltpu.VMEM((VIEWS, NEAR, BLK, LINE), BF),
            pltpu.VMEM((NEAR, NEAR, LINE), F32),
            pltpu.VMEM(block, BF),
            pltpu.VMEM((ITERS, NEAR, NEAR, LINE), BF),
            pltpu.VMEM((ITERS, 2, BLK, NEAR, LINE), F32),
            pltpu.VMEM((ITERS, 2) + block, F32),
            pltpu.VMEM(block, F32),
            pltpu.VMEM(block, F32),
            pltpu.VMEM((nx, nz, BLK, LINE), BF),
            pltpu.VMEM((nx, nz, BLK, LINE), BF),
            pltpu.VMEM((1, LINE), jnp.int32),
            pltpu.VMEM((1, LINE), jnp.int32),
            pltpu.SMEM((1, LINE), jnp.int32),
            (dma((3,)), dma((3,))),
            (dma((ITERS, 8)), dma((ITERS, 8))),
            (dma((ITERS, 4)), dma((ITERS, 4))),
            (dma((nz, 2)), dma((nz, 2))),
            (dma((nx,)), dma((nx,))),
            dma((4,)),
        ],
        compiler_params=pltpu.CompilerParams(
            vmem_limit_bytes=48 << 20, collective_id=0, has_side_effects=True
        ),
    )


def shards(estimate, view_tiles, incoming_label, lateral_bank, axial_kernel, kernel_index):
    nx, nz = lax.axis_size("gx"), lax.axis_size("gz")
    outgoing = view_tiles[0].reshape(nx, nz, BLK, LINE)
    return joint_kernel(nx, nz)(
        kernel_index, axial_kernel, axial_kernel, lateral_bank, incoming_label, estimate, outgoing
    )


def solution(mesh):
    return jax.shard_map(
        shards,
        mesh=mesh,
        in_specs=(P("gz", "gx", None), P(("gx", "gz"), None, None), P(("gx", "gz"), None), P(), P(), P()),
        out_specs=P("gz", "gx", None),
        check_vma=False,
    )
```

time: 101 us -> 91.9 us (0.910)
  the two profiles are of different devices: /device:TPU:19 before, /device:TPU:68 now
where the time goes in v3:
time: 91.9 us; the launch traced here: 91.8 us
  Pallas kernels  89.2 us (97%)
  local copies, waits for them, and re-layouts  2.49 us (3%)
    pallas_call x1, Pallas kernels, shards(): joint_kernel(nx, nz)  89.2 us
    unnamed x12, local copies, waits for them, and re-layouts  2.49 us

profile of v3, /device:TPU:68, one launch (start us, length us, event | category | flops | bytes accessed | tf_op | source)
XLA Modules:
  0.0 91.8 jit_solution(14771869800809199928)
XLA Ops:
  0.0 0.0 copy-start
  0.0 0.0 copy-start.1
  0.0 0.0 copy-start.2
  0.0 1.2 %copy.7 = bf16[16,8,16,128]{3,2,1,0:T(8,128)(2,1)S(1)} copy(bf16[16,8,16,128]{3,1,2,0:T(8,128)(2,1)} %bitcast.5) | data formatting | bytes 1048576
  1.2 0.0 copy-start.3
  1.2 0.0 copy-start.4
  1.2 0.0 copy-done
  1.2 0.0 copy-done.1
  1.2 0.0 copy-done.2
  1.3 0.6 copy-done.3
  1.9 0.0 copy-done.4
  1.9 89.2 %joint.1 = f32[16,16,128]{2,1,0:T(8,128)S(1)} custom-call(s32[256]{0:T(256)S(1)} %copy-done.3, f32[6,33]{1,0:T(8,128)S(1)} %copy-done.2, f32[6,33]{1,0:T(8,128)S(1)} %copy-done.2, f32[6,16,2,33]{3,2,1,0:T(2,128)S(1)} %copy-done.1, s32[1,128]{1,0:T(1,128)S(1)} %copy-done.4, f32[16,16,128]{2,1,0:T(8,128)S(1)} %copy-done, bf16[8,16,16,128]{3,2,1,0:T(8,128)(2,1)S(1)} %bitcast.4), custom_call_target="tpu_custom_call" | custom-call | tf_op jit(solution)/shard_map/joint/pallas_call | solution.py:449
  91.1 0.7 copy.9
Async XLA Ops:
  0.0 1.2 %copy-start = (f32[16,16,128]{2,1,0:T(8,128)S(1)}, f32[16,16,128]{2,1,0:T(8,128)}, u32[]{:S(2)}) copy-start(f32[16,16,128]{2,1,0:T(8,128)} %estimate_ref.1) | copy-start | bytes 393220
  0.0 1.2 %copy-start.1 = (f32[6,16,2,33]{3,2,1,0:T(2,128)S(1)}, f32[6,16,2,33]{3,2,1,0:T(2,128)}, u32[]{:S(2)}) copy-start(f32[6,16,2,33]{3,2,1,0:T(2,128)} %bank_ref.1) | copy-start | bytes 76036
  0.0 1.2 %copy-start.2 = (f32[6,33]{1,0:T(8,128)S(1)}, f32[6,33]{1,0:T(8,128)}, u32[]{:S(2)}) copy-start(f32[6,33]{1,0:T(8,128)} %axial_in.1) | copy-start | bytes 2380
  1.2 0.7 copy-start.3
  1.2 0.7 copy-start.4

commit v4 on v3

v4 whole, which is shorter than its diff:
```python
import jax
import jax.numpy as jnp
from jax import lax
from jax.experimental import pallas as pl
from jax.experimental.pallas import tpu as pltpu
from jax.sharding import PartitionSpec as P

TAPS = 33
ITERS = 2
HALO = 16
VIEWS = 6
KERNELS = 16
BLK = 16
NEAR = 48
UNROLL = 8
LINE = 128
F32 = jnp.float32
BF = jnp.bfloat16
HI = lax.Precision.HIGHEST


def iota(shape, dim):
    return lax.broadcasted_iota(jnp.int32, shape, dim)


def load_taps(bank_ref, axial_in, kx, ky, ax):
    ax[...] = jnp.zeros_like(ax)
    ax[:VIEWS, :TAPS] = axial_in[...]
    for dim, taps in ((0, kx), (1, ky)):
        taps[...] = jnp.zeros_like(taps)
        for v in range(VIEWS):
            taps[:, v, :TAPS] = bank_ref[v, :, dim, :]
        raw = taps[...]
        total = jnp.sum(raw, axis=-1, keepdims=True)
        taps[...] = raw / jnp.where(total > 0.0, total, 1.0)


def build_bands(kx_ref, ky_ref, ax, fwd_y, bwd_y, fwd_x, bwd_x, first, last):
    inside = jnp.abs(iota((LINE, LINE), 0) - iota((LINE, LINE), 1)) <= HALO
    axial = jnp.sum(ax[...], axis=1, keepdims=True)
    scale = jnp.broadcast_to(1.0 / jnp.where(axial > 0.0, axial, 1.0), (8, LINE))

    @pl.loop(first, last)
    def _(k):
        kx = kx_ref[k]
        ky = ky_ref[k] * scale
        rows = []
        for v in range(VIEWS):
            band = pltpu.roll(jnp.broadcast_to(ky[v : v + 1], (LINE, LINE)), LINE - HALO, 1, stride=1, stride_axis=0)
            band = jnp.where(inside, band, 0.0)
            bwd_y[k, v] = band.astype(BF)
            fwd_y[k, v] = band.T.astype(BF)
            rows.append(pltpu.roll(jnp.broadcast_to(kx[v : v + 1], (BLK, LINE)), 0, 1, stride=1, stride_axis=0))
        across = jnp.concatenate(rows, 0)
        fwd_x[k] = across.astype(BF)
        bwd_x[k] = across.T.astype(BF)


def ones_response(index_of, ax, kx_ref, ky_ref, col0, depth0, edge_x, edge_y, base_ref, cols, depths):
    tap = iota((LINE, LINE), 0)
    pos = iota((LINE, LINE), 1)
    at_x = col0 + pos - tap + HALO
    at_y = pos - tap + HALO
    ok_x = jnp.where((at_x >= 0) & (at_x < cols), 1.0, 0.0)
    ok_y = jnp.where((at_y >= 0) & (at_y < LINE), 1.0, 0.0)
    kx = kx_ref[...].reshape(KERNELS * 8, LINE)
    ky = ky_ref[...].reshape(KERNELS * 8, LINE)
    edge_x[...] = jnp.dot(kx, ok_x, precision=HI, preferred_element_type=F32).reshape(KERNELS, 8, LINE)
    edge_y[...] = jnp.dot(ky, ok_y, precision=HI, preferred_element_type=F32).reshape(KERNELS, 8, LINE)
    axial = ax[...]
    total = jnp.sum(axial, axis=1, keepdims=True)
    axial = axial / jnp.where(total > 0.0, total, 1.0)
    lane = iota((8, LINE), 1)
    for z in range(BLK):
        k = index_of(HALO + z)
        at_z = depth0 + z - lane + HALO
        part = jnp.sum(jnp.where((at_z >= 0) & (at_z < depths), axial, 0.0), axis=1, keepdims=True)
        left = edge_x[k][:, :BLK] * part
        base_ref[z] = lax.dot_general(
            left, edge_y[k], (((0,), (0,)), ((), ())), precision=HI, preferred_element_type=F32
        )


def slots_of(labels, slots):
    column = jnp.broadcast_to(labels, (LINE, LINE)).T
    hit = column == iota((LINE, LINE), 1)
    slots[...] = jnp.max(jnp.where(hit, iota((LINE, LINE), 0), -1), axis=0, keepdims=True)


def lateral_forward(index_of, fwd_x, fwd_y, wide, mid, grown, first, count, unroll):
    @pl.loop(0, count // unroll)
    def _(s):
        start = first + s * unroll
        kernels = [index_of(start + u) for u in range(unroll)]
        for u, k in enumerate(kernels):
            mid[start + u] = jnp.dot(fwd_x[k][:, :NEAR], wide[start + u], preferred_element_type=F32).astype(BF)
        for u, k in enumerate(kernels):
            for v in range(VIEWS):
                grown[v, start + u] = jnp.dot(
                    mid[start + u, v * BLK : (v + 1) * BLK, :], fwd_y[k, v], preferred_element_type=F32
                )


def lateral_backward(index_of, bwd_x, bwd_y, spread, mid, total, first, count, unroll):
    @pl.loop(0, count // unroll)
    def _(s):
        start = first + s * unroll
        kernels = [index_of(start + u) for u in range(unroll)]
        for u, k in enumerate(kernels):
            for v in range(VIEWS):
                mid[start + u, v * BLK : (v + 1) * BLK, :] = jnp.dot(
                    spread[v, start + u], bwd_y[k, v], preferred_element_type=F32
                ).astype(BF)
        for u, k in enumerate(kernels):
            total[start + u] = jnp.dot(bwd_x[k][:NEAR], mid[start + u], preferred_element_type=F32)


def taps_over(zi):
    return range(max(0, zi - 2 * HALO), min(BLK - 1, zi) + 1)


def axial_and_ratio(axial_ref, slot_ref, grown, tile_of, spread):
    @pl.loop(0, VIEWS)
    def _(v):
        weights = [axial_ref[v, t] for t in range(TAPS)]
        seen = jnp.full((8, LINE), slot_ref[0, v * BLK], jnp.int32) >= 0
        for half in range(2):
            rows = slice(half * 8, half * 8 + 8)
            total = [None] * BLK
            for zi in range(NEAR):
                g = grown[v, zi, rows, :]
                for zo in taps_over(zi):
                    term = weights[zi - zo] * g
                    total[zo] = term if total[zo] is None else total[zo] + term
            excess = []
            for zo in range(BLK):
                tile = tile_of(jnp.maximum(slot_ref[0, v * BLK + zo], 0))[rows].astype(F32)
                ratio = (tile / total[zo]).astype(BF).astype(F32)
                excess.append(jnp.where(seen, ratio - 1.0, 0.0))
            for zi in range(NEAR):
                acc = None
                for zo in taps_over(zi):
                    term = weights[zi - zo] * excess[zo]
                    acc = term if acc is None else acc + term
                spread[v, zi, rows, :] = acc.astype(BF)


LOW, OWN, HIGH = slice(0, BLK), slice(BLK, 2 * BLK), slice(2 * BLK, NEAR)
MESH = pl.DeviceIdType.MESH


class Copy:
    def __init__(self, src, dst, sems, slot, device, sends, receives):
        self.src, self.sems, self.slot = src, sems, slot
        self.sends, self.receives = sends, receives
        self.out = self.back = self.make(dst, device)
        self.device = device

    def make(self, dst, device):
        return pltpu.make_async_remote_copy(
            src_ref=self.src, dst_ref=dst, send_sem=self.sems[0].at[self.slot], recv_sem=self.sems[1].at[self.slot],
            device_id=device, device_id_type=MESH,
        )

    def lands_in(self, region):
        self.back = self.make(region, self.device)

    def start(self):
        pl.when(self.sends)(self.out.start)

    def wait_recv(self):
        pl.when(self.receives)(self.back.wait_recv)

    def wait_send(self):
        pl.when(self.sends)(self.out.wait_send)


def joint_kernel(nx, nz):
    def body(index_ref, axial_ref, axial_in, bank_ref, labels_ref, estimate_ref, outgoing,
             out_ref, kx, ky, ax, fwd_y, bwd_y, fwd_x, bwd_x, edge_x, edge_y, base, mid, grown, spread, total,
             wide, part_mate, part, passing, arrived, slots, slot_ref,
             halo_sems, sum_sems, first_sems, second_sems, local_sems):
        gx, gz = lax.axis_index("gx"), lax.axis_index("gz")
        core = gz % 2
        has_l, has_r = gx > 0, gx < nx - 1
        across = gz - 1 + 2 * core
        has_c = (across >= 0) & (across < nz)
        across = (across + nz) % nz
        gl, gr = (gx + nx - 1) % nx, (gx + 1) % nx
        mate = (gx, gz + 1 - 2 * core)
        mate_rows, cross_rows = pl.ds(2 * BLK * (1 - core), BLK), pl.ds(2 * BLK * core, BLK)
        at_mate, at_cross = cross_rows, mate_rows

        def index_of(z):
            return index_ref[jnp.clip(gz * BLK - HALO + z, 0, nz * BLK - 1)]

        wide[0, OWN, OWN] = estimate_ref[...].astype(BF)
        for it in range(ITERS):
            for missing, rows, columns in (
                (gx == 0, slice(0, NEAR), LOW), (gx == nx - 1, slice(0, NEAR), HIGH),
                (gz == 0, LOW, slice(0, NEAR)), (gz == nz - 1, HIGH, slice(0, NEAR)),
            ):
                @pl.when(missing)
                def _():
                    region = wide.at[it, rows, columns]
                    region[...] = jnp.zeros(region.shape, BF)

        barrier = pltpu.get_barrier_semaphore()

        def greet(device):
            pl.semaphore_signal(barrier, inc=1, device_id=device, device_id_type=MESH)

        for d in range(1, nz):
            greet((gx, (gz + d) % nz))
        for d in range(1, nx):
            greet(((gx + d) % nx, gz))
        pl.when(has_c & has_l)(lambda: greet((gl, across)))
        pl.when(has_c & has_r)(lambda: greet((gr, across)))
        extra = (has_c & has_l).astype(jnp.int32) + (has_c & has_r).astype(jnp.int32)
        pl.semaphore_wait(barrier, nx + nz - 2 + extra)

        def halo(it):
            w = wide.at[it]
            sems = (halo_sems[0].at[it], halo_sems[1].at[it])
            own = w.at[OWN, OWN]
            near = [
                Copy(own, w.at[OWN, LOW], sems, 0, (gr, gz), has_r, has_l),
                Copy(own, w.at[OWN, HIGH], sems, 1, (gl, gz), has_l, has_r),
            ]
            far = [
                Copy(own, w.at[at_mate, OWN], sems, 2, mate, True, True),
                Copy(own, w.at[at_cross, LOW], sems, 3, (gr, across), has_c & has_r, has_c & has_l),
                Copy(own, w.at[at_cross, HIGH], sems, 4, (gl, across), has_c & has_l, has_c & has_r),
                Copy(own, w.at[at_cross, OWN], sems, 5, (gx, across), has_c, has_c),
            ]
            relay = [
                Copy(w.at[OWN, LOW], w.at[at_mate, LOW], sems, 6, mate, has_l, has_l),
                Copy(w.at[OWN, HIGH], w.at[at_mate, HIGH], sems, 7, mate, has_r, has_r),
            ]
            for copy, rows, columns in (
                (far[0], mate_rows, OWN), (far[1], cross_rows, LOW), (far[2], cross_rows, HIGH),
                (far[3], cross_rows, OWN), (relay[0], mate_rows, LOW), (relay[1], mate_rows, HIGH),
            ):
                copy.lands_in(w.at[rows, columns])
            return near, far, relay

        def sums(it):
            sems = (sum_sems[0].at[it], sum_sems[1].at[it])
            p = part.at[it]
            to_mate = Copy(total.at[mate_rows], part_mate.at[it], sems, 0, mate, True, True)
            to_cross = [
                Copy(total.at[cross_rows, LOW], p.at[2], sems, 1, (gl, across), has_c & has_l, has_c & has_r),
                Copy(total.at[cross_rows, HIGH], p.at[1], sems, 2, (gr, across), has_c & has_r, has_c & has_l),
                Copy(total.at[cross_rows, OWN], p.at[0], sems, 3, (gx, across), has_c, has_c),
            ]
            aside = []
            for half in range(2):
                rows = slice(BLK + 8 * half, BLK + 8 * half + 8)
                there = slice(8 * half, 8 * half + 8)
                aside.append([
                    Copy(total.at[rows, LOW], p.at[4, there], sems, 4 + 2 * half, (gl, gz), has_l, has_r),
                    Copy(total.at[rows, HIGH], p.at[3, there], sems, 5 + 2 * half, (gr, gz), has_r, has_l),
                ])
            return to_mate, to_cross, aside

        def along_gz(d):
            target = (gz + d) % nz
            return pltpu.make_async_remote_copy(
                src_ref=outgoing.at[:, target], dst_ref=passing.at[:, gz],
                send_sem=first_sems[0].at[d], recv_sem=first_sems[1].at[d],
                device_id=(gx, target), device_id_type=MESH,
            )

        def along_gx(d):
            target = (gx + d) % nx
            return pltpu.make_async_remote_copy(
                src_ref=passing.at[target], dst_ref=arrived.at[gx],
                send_sem=second_sems[0].at[d], recv_sem=second_sems[1].at[d],
                device_id=(target, gz), device_id_type=MESH,
            )

        stay_gz = pltpu.make_async_copy(outgoing.at[:, gz], passing.at[:, gz], local_sems.at[0])
        stay_gx = pltpu.make_async_copy(passing.at[gx], arrived.at[gx], local_sems.at[1])
        slot_copy = pltpu.make_async_copy(slots, slot_ref, local_sems.at[2])

        for it in range(ITERS):
            w = wide.at[it]
            near, far, relay = halo(it)
            for copy in near + far:
                copy.start()
            if it == 0:
                stay_gz.start()
                for d in range(1, nz):
                    along_gz(d).start()
                slots_of(labels_ref[...], slots)
                slot_copy.start()
                load_taps(bank_ref, axial_in, kx, ky, ax)
                build_bands(kx, ky, ax, fwd_y, bwd_y, fwd_x, bwd_x, 0, KERNELS)
            for copy in near:
                copy.wait_recv()
            for copy in relay:
                copy.start()
            lateral_forward(index_of, fwd_x, fwd_y, w, mid, grown, BLK, BLK, UNROLL)
            if it == 0:
                stay_gz.wait()
                for d in range(1, nz):
                    along_gz(d).wait_recv()
                for d in range(1, nx):
                    along_gx(d).start()
                stay_gx.start()
            for copy in [far[0]] + relay:
                copy.wait_recv()
            lateral_forward(index_of, fwd_x, fwd_y, w, mid, grown, 2 * BLK * (1 - core), BLK, UNROLL)
            for copy in far[1:]:
                copy.wait_recv()
            lateral_forward(index_of, fwd_x, fwd_y, w, mid, grown, 2 * BLK * core, BLK, UNROLL)
            if it == 0:
                ones_response(index_of, ax, kx, ky, gx * BLK, gz * BLK, edge_x, edge_y, base, nx * BLK, nz * BLK)
                for d in range(1, nz):
                    along_gz(d).wait_send()
                for d in range(1, nx):
                    along_gx(d).wait()
                stay_gx.wait()
                slot_copy.wait()
            for copy in near + far + relay:
                copy.wait_send()

            axial_and_ratio(axial_ref, slot_ref, grown, lambda s: arrived[s // nz, s % nz], spread)
            to_mate, to_cross, aside = sums(it)
            lateral_backward(index_of, bwd_x, bwd_y, spread, mid, total, 2 * BLK * core, BLK, UNROLL)
            for copy in to_cross:
                copy.start()
            lateral_backward(index_of, bwd_x, bwd_y, spread, mid, total, 2 * BLK * (1 - core), BLK, UNROLL)
            to_mate.start()
            for half in range(2):
                first = BLK + 8 * half
                lateral_backward(index_of, bwd_x, bwd_y, spread, mid, total, first, 8, UNROLL)
                if half == 0:
                    to_mate.wait_recv()
                total[first : first + 8] += part_mate[it, 8 * half : 8 * half + 8]
                for copy in aside[half]:
                    copy.start()
            inner = base[...] + total[OWN, OWN]
            for copy in to_cross:
                copy.wait_recv()
            for there, which in ((has_c, 0), (has_c & has_l, 1), (has_c & has_r, 2)):
                inner = inner + jnp.where(there, part[it, which], 0.0)
            before = estimate_ref if it == 0 else out_ref
            scaled = before[...] * (1.0 / VIEWS)
            for pair in aside:
                for copy in pair:
                    copy.wait_recv()
            for there, which in ((has_l, 3), (has_r, 4)):
                inner = inner + jnp.where(there, part[it, which], 0.0)
            after = scaled * inner
            out_ref[...] = after
            if it + 1 < ITERS:
                wide[it + 1, OWN, OWN] = after.astype(BF)
            for copy in [to_mate] + to_cross + aside[0] + aside[1]:
                copy.wait_send()

    smem = pl.BlockSpec(memory_space=pltpu.SMEM)
    vmem = pl.BlockSpec(memory_space=pltpu.VMEM)
    dma = pltpu.SemaphoreType.DMA
    block = (BLK, BLK, LINE)
    return pl.pallas_call(
        body,
        name="joint",
        out_shape=jax.ShapeDtypeStruct(block, F32),
        in_specs=[smem] * 2 + [vmem] * 4 + [pl.BlockSpec(memory_space=pl.ANY)],
        out_specs=vmem,
        scratch_shapes=[
            pltpu.VMEM((KERNELS, 8, LINE), F32),
            pltpu.VMEM((KERNELS, 8, LINE), F32),
            pltpu.VMEM((8, LINE), F32),
            pltpu.VMEM((KERNELS, VIEWS, LINE, LINE), BF),
            pltpu.VMEM((KERNELS, VIEWS, LINE, LINE), BF),
            pltpu.VMEM((KERNELS, VIEWS * BLK, LINE), BF),
            pltpu.VMEM((KERNELS, LINE, VIEWS * BLK), BF),
            pltpu.VMEM((KERNELS, 8, LINE), F32),
            pltpu.VMEM((KERNELS, 8, LINE), F32),
            pltpu.VMEM(block, F32),
            pltpu.VMEM((NEAR, VIEWS * BLK, LINE), BF),
            pltpu.VMEM((VIEWS, NEAR, BLK, LINE), F32),
            pltpu.VMEM((VIEWS, NEAR, BLK, LINE), BF),
            pltpu.VMEM((NEAR, NEAR, LINE), F32),
            pltpu.VMEM((ITERS, NEAR, NEAR, LINE), BF),
            pltpu.VMEM((ITERS, BLK, NEAR, LINE), F32),
            pltpu.VMEM((ITERS, 5) + block, F32),
            pltpu.VMEM((nx, nz, BLK, LINE), BF),
            pltpu.VMEM((nx, nz, BLK, LINE), BF),
            pltpu.VMEM((1, LINE), jnp.int32),
            pltpu.SMEM((1, LINE), jnp.int32),
            (dma((ITERS, 8)), dma((ITERS, 8))),
            (dma((ITERS, 8)), dma((ITERS, 8))),
            (dma((nz,)), dma((nz,))),
            (dma((nx,)), dma((nx,))),
            dma((3,)),
        ],
        compiler_params=pltpu.CompilerParams(
            vmem_limit_bytes=48 << 20, collective_id=0, has_side_effects=True
        ),
    )


def shards(estimate, view_tiles, incoming_label, lateral_bank, axial_kernel, kernel_index):
    nx, nz = lax.axis_size("gx"), lax.axis_size("gz")
    outgoing = view_tiles[0].reshape(nx, nz, BLK, LINE)
    return joint_kernel(nx, nz)(
        kernel_index, axial_kernel, axial_kernel, lateral_bank, incoming_label, estimate, outgoing
    )


def solution(mesh):
    return jax.shard_map(
        shards,
        mesh=mesh,
        in_specs=(P("gz", "gx", None), P(("gx", "gz"), None, None), P(("gx", "gz"), None), P(), P(), P()),
        out_specs=P("gz", "gx", None),
        check_vma=False,
    )
```

time: 91.9 us -> 80.2 us (0.87)
  the two profiles are of different devices: /device:TPU:68 before, /device:TPU:19 now
where the time goes in v4:
time: 80.2 us; the launch traced here: 80.1 us
  Pallas kernels  77.5 us (97%)
  local copies, waits for them, and re-layouts  2.49 us (3%)
    pallas_call x1, Pallas kernels, shards(): joint_kernel(nx, nz)  77.5 us
    unnamed x12, local copies, waits for them, and re-layouts  2.49 us

profile of v4, /device:TPU:19, one launch (start us, length us, event | category | flops | bytes accessed | tf_op | source)
XLA Modules:
  0.0 80.1 jit_solution(7565160308618137911)
XLA Ops:
  0.0 0.0 copy-start
  0.0 0.0 copy-start.1
  0.0 0.0 copy-start.2
  0.0 1.2 %copy.7 = bf16[16,8,16,128]{3,2,1,0:T(8,128)(2,1)S(1)} copy(bf16[16,8,16,128]{3,1,2,0:T(8,128)(2,1)} %bitcast.5) | data formatting | bytes 1048576
  1.2 0.0 copy-start.3
  1.2 0.0 copy-start.4
  1.2 0.0 copy-done
  1.2 0.0 copy-done.1
  1.2 0.0 copy-done.2
  1.3 0.6 copy-done.3
  1.9 0.0 copy-done.4
  1.9 77.5 %joint.1 = f32[16,16,128]{2,1,0:T(8,128)S(1)} custom-call(s32[256]{0:T(256)S(1)} %copy-done.3, f32[6,33]{1,0:T(8,128)S(1)} %copy-done.2, f32[6,33]{1,0:T(8,128)S(1)} %copy-done.2, f32[6,16,2,33]{3,2,1,0:T(2,128)S(1)} %copy-done.1, s32[1,128]{1,0:T(1,128)S(1)} %copy-done.4, f32[16,16,128]{2,1,0:T(8,128)S(1)} %copy-done, bf16[8,16,16,128]{3,2,1,0:T(8,128)(2,1)S(1)} %bitcast.4), custom_call_target="tpu_custom_call" | custom-call | tf_op jit(solution)/shard_map/joint/pallas_call | solution.py:409
  79.4 0.7 copy.9
Async XLA Ops:
  0.0 1.2 %copy-start = (f32[16,16,128]{2,1,0:T(8,128)S(1)}, f32[16,16,128]{2,1,0:T(8,128)}, u32[]{:S(2)}) copy-start(f32[16,16,128]{2,1,0:T(8,128)} %estimate_ref.1) | copy-start | bytes 393220
  0.0 1.2 %copy-start.1 = (f32[6,16,2,33]{3,2,1,0:T(2,128)S(1)}, f32[6,16,2,33]{3,2,1,0:T(2,128)}, u32[]{:S(2)}) copy-start(f32[6,16,2,33]{3,2,1,0:T(2,128)} %bank_ref.1) | copy-start | bytes 76036
  0.0 1.2 %copy-start.2 = (f32[6,33]{1,0:T(8,128)S(1)}, f32[6,33]{1,0:T(8,128)}, u32[]{:S(2)}) copy-start(f32[6,33]{1,0:T(8,128)} %axial_in.1) | copy-start | bytes 2380
  1.2 0.7 copy-start.3
  1.2 0.7 copy-start.4

commit v5 on v4

--- a/solution.py
+++ b/solution.py
@@ -35,25 +35,33 @@
         taps[...] = raw / jnp.where(total > 0.0, total, 1.0)
 
 
-def build_bands(kx_ref, ky_ref, ax, fwd_y, bwd_y, fwd_x, bwd_x, first, last):
+def line_scale(ax):
+    axial = jnp.sum(ax[...], axis=1, keepdims=True)
+    return jnp.broadcast_to(1.0 / jnp.where(axial > 0.0, axial, 1.0), (8, LINE))
+
+
+def reverse_taps(ky, ky_back):
+    flip = jnp.where(iota((LINE, LINE), 0) + iota((LINE, LINE), 1) == TAPS - 1, 1.0, 0.0)
+    taps = ky[...].reshape(KERNELS * 8, LINE)
+    ky_back[...] = jnp.dot(taps, flip, precision=HI, preferred_element_type=F32).reshape(KERNELS, 8, LINE)
+
+
+def build_bands(ky, kx, ax, bands_y, bands_x, spread_out):
     inside = jnp.abs(iota((LINE, LINE), 0) - iota((LINE, LINE), 1)) <= HALO
-    axial = jnp.sum(ax[...], axis=1, keepdims=True)
-    scale = jnp.broadcast_to(1.0 / jnp.where(axial > 0.0, axial, 1.0), (8, LINE))
-
-    @pl.loop(first, last)
+    scale = line_scale(ax)
+
+    @pl.loop(0, KERNELS)
     def _(k):
-        kx = kx_ref[k]
-        ky = ky_ref[k] * scale
+        taps_x = kx[k]
+        taps_y = ky[k] * scale
         rows = []
         for v in range(VIEWS):
-            band = pltpu.roll(jnp.broadcast_to(ky[v : v + 1], (LINE, LINE)), LINE - HALO, 1, stride=1, stride_axis=0)
-            band = jnp.where(inside, band, 0.0)
-            bwd_y[k, v] = band.astype(BF)
-            fwd_y[k, v] = band.T.astype(BF)
-            rows.append(pltpu.roll(jnp.broadcast_to(kx[v : v + 1], (BLK, LINE)), 0, 1, stride=1, stride_axis=0))
+            band = jnp.broadcast_to(taps_y[v : v + 1], (LINE, LINE))
+            band = pltpu.roll(band, LINE - HALO, 1, stride=1, stride_axis=0)
+            bands_y[k, v] = jnp.where(inside, band, 0.0).astype(BF)
+            rows.append(pltpu.roll(jnp.broadcast_to(taps_x[v : v + 1], (BLK, LINE)), 0, 1, stride=1, stride_axis=0))
         across = jnp.concatenate(rows, 0)
-        fwd_x[k] = across.astype(BF)
-        bwd_x[k] = across.T.astype(BF)
+        bands_x[k] = (across.T if spread_out else across).astype(BF)
 
 
 def ones_response(index_of, ax, kx_ref, ky_ref, col0, depth0, edge_x, edge_y, base_ref, cols, depths):
@@ -101,7 +109,7 @@
                 )
 
 
-def lateral_backward(index_of, bwd_x, bwd_y, spread, mid, total, first, count, unroll):
+def lateral_backward(index_of, bwd_x, bwd_y, spread, mid, total, shift, first, count, unroll):
     @pl.loop(0, count // unroll)
     def _(s):
         start = first + s * unroll
@@ -112,7 +120,7 @@
                     spread[v, start + u], bwd_y[k, v], preferred_element_type=F32
                 ).astype(BF)
         for u, k in enumerate(kernels):
-            total[start + u] = jnp.dot(bwd_x[k][:NEAR], mid[start + u], preferred_element_type=F32)
+            total[start + u - shift] = jnp.dot(bwd_x[k][:NEAR], mid[start + u], preferred_element_type=F32).astype(total.dtype)
 
 
 def taps_over(zi):
@@ -177,8 +185,8 @@
 
 def joint_kernel(nx, nz):
     def body(index_ref, axial_ref, axial_in, bank_ref, labels_ref, estimate_ref, outgoing,
-             out_ref, kx, ky, ax, fwd_y, bwd_y, fwd_x, bwd_x, edge_x, edge_y, base, mid, grown, spread, total,
-             wide, part_mate, part, passing, arrived, slots, slot_ref,
+             out_ref, kx, ky, ky_back, ax, fwd_y, bwd_y, fwd_x, bwd_x, edge_x, edge_y, base, mid, grown, spread, total,
+             to_far, to_side, wide, part_mate, part, passing, arrived, slots, slot_ref,
              halo_sems, sum_sems, first_sems, second_sems, local_sems):
         gx, gz = lax.axis_index("gx"), lax.axis_index("gz")
         core = gz % 2
@@ -210,14 +218,18 @@
         def greet(device):
             pl.semaphore_signal(barrier, inc=1, device_id=device, device_id_type=MESH)
 
-        for d in range(1, nz):
-            greet((gx, (gz + d) % nz))
-        for d in range(1, nx):
-            greet(((gx + d) % nx, gz))
-        pl.when(has_c & has_l)(lambda: greet((gl, across)))
-        pl.when(has_c & has_r)(lambda: greet((gr, across)))
-        extra = (has_c & has_l).astype(jnp.int32) + (has_c & has_r).astype(jnp.int32)
-        pl.semaphore_wait(barrier, nx + nz - 2 + extra)
+        for d in range(1, 16):
+            greet((2 * ((gx // 2 + d // 4) % 4) + gx % 2, 4 * ((gz // 4 + d % 4) % 4) + gz % 4))
+        for d in range(1, 8):
+            greet((gx - gx % 2 + (gx % 2 + d // 4) % 2, gz - gz % 4 + (gz % 4 + d % 4) % 4))
+        extra = 0
+        for there, device in (
+            (has_l, (gl, gz)), (has_r, (gr, gz)), (has_c, (gx, across)),
+            (has_c & has_l, (gl, across)), (has_c & has_r, (gr, across)),
+        ):
+            pl.when(there)(lambda device=device: greet(device))
+            extra = extra + there.astype(jnp.int32)
+        pl.semaphore_wait(barrier, 22 + extra)
 
         def halo(it):
             w = wide.at[it]
@@ -249,65 +261,70 @@
             p = part.at[it]
             to_mate = Copy(total.at[mate_rows], part_mate.at[it], sems, 0, mate, True, True)
             to_cross = [
-                Copy(total.at[cross_rows, LOW], p.at[2], sems, 1, (gl, across), has_c & has_l, has_c & has_r),
-                Copy(total.at[cross_rows, HIGH], p.at[1], sems, 2, (gr, across), has_c & has_r, has_c & has_l),
-                Copy(total.at[cross_rows, OWN], p.at[0], sems, 3, (gx, across), has_c, has_c),
+                Copy(to_far.at[:, LOW], p.at[2], sems, 1, (gl, across), has_c & has_l, has_c & has_r),
+                Copy(to_far.at[:, HIGH], p.at[1], sems, 2, (gr, across), has_c & has_r, has_c & has_l),
+                Copy(to_far.at[:, OWN], p.at[0], sems, 3, (gx, across), has_c, has_c),
             ]
             aside = []
             for half in range(2):
-                rows = slice(BLK + 8 * half, BLK + 8 * half + 8)
                 there = slice(8 * half, 8 * half + 8)
                 aside.append([
-                    Copy(total.at[rows, LOW], p.at[4, there], sems, 4 + 2 * half, (gl, gz), has_l, has_r),
-                    Copy(total.at[rows, HIGH], p.at[3, there], sems, 5 + 2 * half, (gr, gz), has_r, has_l),
+                    Copy(to_side.at[0, there], p.at[4, there], sems, 4 + 2 * half, (gl, gz), has_l, has_r),
+                    Copy(to_side.at[1, there], p.at[3, there], sems, 5 + 2 * half, (gr, gz), has_r, has_l),
                 ])
             return to_mate, to_cross, aside
 
-        def along_gz(d):
-            target = (gz + d) % nz
+        def first_stage(d):
+            y, x = (gx // 2 + d // 4) % 4, (gz // 4 + d % 4) % 4
             return pltpu.make_async_remote_copy(
-                src_ref=outgoing.at[:, target], dst_ref=passing.at[:, gz],
+                src_ref=outgoing.at[y, :, x], dst_ref=passing.at[gx // 2, gz // 4],
                 send_sem=first_sems[0].at[d], recv_sem=first_sems[1].at[d],
-                device_id=(gx, target), device_id_type=MESH,
+                device_id=(2 * y + gx % 2, 4 * x + gz % 4), device_id_type=MESH,
             )
 
-        def along_gx(d):
-            target = (gx + d) % nx
+        def second_stage(d):
+            high, low = (gx % 2 + d // 4) % 2, (gz % 4 + d % 4) % 4
             return pltpu.make_async_remote_copy(
-                src_ref=passing.at[target], dst_ref=arrived.at[gx],
+                src_ref=passing.at[:, :, high, low], dst_ref=arrived.at[:, gx % 2, :, gz % 4],
                 send_sem=second_sems[0].at[d], recv_sem=second_sems[1].at[d],
-                device_id=(target, gz), device_id_type=MESH,
+                device_id=(gx - gx % 2 + high, gz - gz % 4 + low), device_id_type=MESH,
             )
 
-        stay_gz = pltpu.make_async_copy(outgoing.at[:, gz], passing.at[:, gz], local_sems.at[0])
-        stay_gx = pltpu.make_async_copy(passing.at[gx], arrived.at[gx], local_sems.at[1])
+        stay_first = pltpu.make_async_copy(
+            outgoing.at[gx // 2, :, gz // 4], passing.at[gx // 2, gz // 4], local_sems.at[0]
+        )
+        stay_second = pltpu.make_async_copy(
+            passing.at[:, :, gx % 2, gz % 4], arrived.at[:, gx % 2, :, gz % 4], local_sems.at[1]
+        )
         slot_copy = pltpu.make_async_copy(slots, slot_ref, local_sems.at[2])
 
         for it in range(ITERS):
             w = wide.at[it]
             near, far, relay = halo(it)
+            if it == 0:
+                stay_first.start()
+                for d in range(1, 16):
+                    first_stage(d).start()
             for copy in near + far:
                 copy.start()
             if it == 0:
-                stay_gz.start()
-                for d in range(1, nz):
-                    along_gz(d).start()
                 slots_of(labels_ref[...], slots)
                 slot_copy.start()
                 load_taps(bank_ref, axial_in, kx, ky, ax)
-                build_bands(kx, ky, ax, fwd_y, bwd_y, fwd_x, bwd_x, 0, KERNELS)
+                reverse_taps(ky, ky_back)
+                build_bands(ky_back, kx, ax, fwd_y, fwd_x, False)
             for copy in near:
                 copy.wait_recv()
             for copy in relay:
                 copy.start()
             lateral_forward(index_of, fwd_x, fwd_y, w, mid, grown, BLK, BLK, UNROLL)
             if it == 0:
-                stay_gz.wait()
-                for d in range(1, nz):
-                    along_gz(d).wait_recv()
-                for d in range(1, nx):
-                    along_gx(d).start()
-                stay_gx.start()
+                stay_first.wait()
+                for d in range(1, 16):
+                    first_stage(d).wait_recv()
+                for d in range(1, 8):
+                    second_stage(d).start()
+                stay_second.start()
             for copy in [far[0]] + relay:
                 copy.wait_recv()
             lateral_forward(index_of, fwd_x, fwd_y, w, mid, grown, 2 * BLK * (1 - core), BLK, UNROLL)
@@ -316,42 +333,47 @@
             lateral_forward(index_of, fwd_x, fwd_y, w, mid, grown, 2 * BLK * core, BLK, UNROLL)
             if it == 0:
                 ones_response(index_of, ax, kx, ky, gx * BLK, gz * BLK, edge_x, edge_y, base, nx * BLK, nz * BLK)
-                for d in range(1, nz):
-                    along_gz(d).wait_send()
-                for d in range(1, nx):
-                    along_gx(d).wait()
-                stay_gx.wait()
+                build_bands(ky, kx, ax, bwd_y, bwd_x, True)
+                for d in range(1, 16):
+                    first_stage(d).wait_send()
+                for d in range(1, 8):
+                    second_stage(d).wait()
+                stay_second.wait()
                 slot_copy.wait()
             for copy in near + far + relay:
                 copy.wait_send()
 
-            axial_and_ratio(axial_ref, slot_ref, grown, lambda s: arrived[s // nz, s % nz], spread)
+            axial_and_ratio(axial_ref, slot_ref, grown, lambda s: arrived[s // 32, (s // 16) % 2, (s // 4) % 4, s % 4], spread)
             to_mate, to_cross, aside = sums(it)
-            lateral_backward(index_of, bwd_x, bwd_y, spread, mid, total, 2 * BLK * core, BLK, UNROLL)
+            lateral_backward(index_of, bwd_x, bwd_y, spread, mid, to_far, 2 * BLK * core, 2 * BLK * core, BLK, UNROLL)
             for copy in to_cross:
                 copy.start()
-            lateral_backward(index_of, bwd_x, bwd_y, spread, mid, total, 2 * BLK * (1 - core), BLK, UNROLL)
+            lateral_backward(index_of, bwd_x, bwd_y, spread, mid, total, 0, 2 * BLK * (1 - core), BLK, UNROLL)
             to_mate.start()
             for half in range(2):
                 first = BLK + 8 * half
-                lateral_backward(index_of, bwd_x, bwd_y, spread, mid, total, first, 8, UNROLL)
+                lateral_backward(index_of, bwd_x, bwd_y, spread, mid, total, 0, first, 8, UNROLL)
                 if half == 0:
                     to_mate.wait_recv()
-                total[first : first + 8] += part_mate[it, 8 * half : 8 * half + 8]
+                there = slice(8 * half, 8 * half + 8)
+                both = total[first : first + 8] + part_mate[it, there]
+                total[first : first + 8, OWN] = both[:, OWN]
+                to_side[0, there] = both[:, LOW].astype(BF)
+                to_side[1, there] = both[:, HIGH].astype(BF)
                 for copy in aside[half]:
                     copy.start()
             inner = base[...] + total[OWN, OWN]
             for copy in to_cross:
                 copy.wait_recv()
             for there, which in ((has_c, 0), (has_c & has_l, 1), (has_c & has_r, 2)):
-                inner = inner + jnp.where(there, part[it, which], 0.0)
+                inner = inner + jnp.where(there, part[it, which].astype(F32), 0.0)
             before = estimate_ref if it == 0 else out_ref
             scaled = before[...] * (1.0 / VIEWS)
             for pair in aside:
                 for copy in pair:
                     copy.wait_recv()
             for there, which in ((has_l, 3), (has_r, 4)):
-                inner = inner + jnp.where(there, part[it, which], 0.0)
+                inner = inner + jnp.where(there, part[it, which].astype(F32), 0.0)
             after = scaled * inner
             out_ref[...] = after
             if it + 1 < ITERS:
@@ -370,6 +392,7 @@
         in_specs=[smem] * 2 + [vmem] * 4 + [pl.BlockSpec(memory_space=pl.ANY)],
         out_specs=vmem,
         scratch_shapes=[
+            pltpu.VMEM((KERNELS, 8, LINE), F32),
             pltpu.VMEM((KERNELS, 8, LINE), F32),
             pltpu.VMEM((KERNELS, 8, LINE), F32),
             pltpu.VMEM((8, LINE), F32),
@@ -384,17 +407,19 @@
             pltpu.VMEM((VIEWS, NEAR, BLK, LINE), F32),
             pltpu.VMEM((VIEWS, NEAR, BLK, LINE), BF),
             pltpu.VMEM((NEAR, NEAR, LINE), F32),
+            pltpu.VMEM((BLK, NEAR, LINE), BF),
+            pltpu.VMEM((2,) + block, BF),
             pltpu.VMEM((ITERS, NEAR, NEAR, LINE), BF),
             pltpu.VMEM((ITERS, BLK, NEAR, LINE), F32),
-            pltpu.VMEM((ITERS, 5) + block, F32),
-            pltpu.VMEM((nx, nz, BLK, LINE), BF),
-            pltpu.VMEM((nx, nz, BLK, LINE), BF),
+            pltpu.VMEM((ITERS, 5) + block, BF),
+            pltpu.VMEM((4, 4, 2, 4, BLK, LINE), BF),
+            pltpu.VMEM((4, 2, 4, 4, BLK, LINE), BF),
             pltpu.VMEM((1, LINE), jnp.int32),
             pltpu.SMEM((1, LINE), jnp.int32),
             (dma((ITERS, 8)), dma((ITERS, 8))),
             (dma((ITERS, 8)), dma((ITERS, 8))),
-            (dma((nz,)), dma((nz,))),
-            (dma((nx,)), dma((nx,))),
+            (dma((16,)), dma((16,))),
+            (dma((8,)), dma((8,))),
             dma((3,)),
         ],
         compiler_params=pltpu.CompilerParams(
@@ -405,7 +430,7 @@
 
 def shards(estimate, view_tiles, incoming_label, lateral_bank, axial_kernel, kernel_index):
     nx, nz = lax.axis_size("gx"), lax.axis_size("gz")
-    outgoing = view_tiles[0].reshape(nx, nz, BLK, LINE)
+    outgoing = view_tiles[0].reshape(4, 2, 4, 4, BLK, LINE)
     return joint_kernel(nx, nz)(
         kernel_index, axial_kernel, axial_kernel, lateral_bank, incoming_label, estimate, outgoing
     )

time: 80.2 us -> 68.7 us (0.86)
  the two profiles are of different devices: /device:TPU:19 before, /device:TPU:17 now
where the time goes in v5:
time: 68.7 us; the launch traced here: 68.6 us
  Pallas kernels  66 us (96%)
  local copies, waits for them, and re-layouts  2.49 us (4%)
    pallas_call x1, Pallas kernels, shards(): joint_kernel(nx, nz)  66 us
    unnamed x12, local copies, waits for them, and re-layouts  2.49 us

profile of v5, /device:TPU:17, one launch (start us, length us, event | category | flops | bytes accessed | tf_op | source)
XLA Modules:
  0.0 68.6 jit_solution(5503423540014330184)
XLA Ops:
  0.0 0.0 copy-start
  0.0 0.0 copy-start.1
  0.0 0.0 copy-start.2
  0.0 1.2 %copy.7 = bf16[16,8,16,128]{3,2,1,0:T(8,128)(2,1)S(1)} copy(bf16[16,8,16,128]{3,1,2,0:T(8,128)(2,1)} %bitcast.5) | data formatting | bytes 1048576
  1.2 0.0 copy-start.3
  1.2 0.0 copy-start.4
  1.2 0.0 copy-done
  1.2 0.0 copy-done.1
  1.2 0.0 copy-done.2
  1.3 0.6 copy-done.3
  1.9 0.0 copy-done.4
  1.9 66.0 %joint.1 = f32[16,16,128]{2,1,0:T(8,128)S(1)} custom-call(s32[256]{0:T(256)S(1)} %copy-done.3, f32[6,33]{1,0:T(8,128)S(1)} %copy-done.2, f32[6,33]{1,0:T(8,128)S(1)} %copy-done.2, f32[6,16,2,33]{3,2,1,0:T(2,128)S(1)} %copy-done.1, s32[1,128]{1,0:T(1,128)S(1)} %copy-done.4, f32[16,16,128]{2,1,0:T(8,128)S(1)} %copy-done, ...), custom_call_target="tpu_custom_call" | custom-call | tf_op jit(solution)/shard_map/joint/pallas_call | solution.py:434
  67.9 0.7 copy.9
Async XLA Ops:
  0.0 1.2 %copy-start = (f32[16,16,128]{2,1,0:T(8,128)S(1)}, f32[16,16,128]{2,1,0:T(8,128)}, u32[]{:S(2)}) copy-start(f32[16,16,128]{2,1,0:T(8,128)} %estimate_ref.1) | copy-start | bytes 393220
  0.0 1.2 %copy-start.1 = (f32[6,16,2,33]{3,2,1,0:T(2,128)S(1)}, f32[6,16,2,33]{3,2,1,0:T(2,128)}, u32[]{:S(2)}) copy-start(f32[6,16,2,33]{3,2,1,0:T(2,128)} %bank_ref.1) | copy-start | bytes 76036
  0.0 1.2 %copy-start.2 = (f32[6,33]{1,0:T(8,128)S(1)}, f32[6,33]{1,0:T(8,128)}, u32[]{:S(2)}) copy-start(f32[6,33]{1,0:T(8,128)} %axial_in.1) | copy-start | bytes 2380
  1.2 0.7 copy-start.3
  1.2 0.7 copy-start.4

commit v6 on v5

--- a/solution.py
+++ b/solution.py
@@ -101,7 +101,9 @@
         start = first + s * unroll
         kernels = [index_of(start + u) for u in range(unroll)]
         for u, k in enumerate(kernels):
-            mid[start + u] = jnp.dot(fwd_x[k][:, :NEAR], wide[start + u], preferred_element_type=F32).astype(BF)
+            mid[start + u] = jnp.dot(
+                fwd_x[k][:, :NEAR], wide[start + u].reshape(NEAR, LINE), preferred_element_type=F32
+            ).astype(BF)
         for u, k in enumerate(kernels):
             for v in range(VIEWS):
                 grown[v, start + u] = jnp.dot(
@@ -109,7 +111,7 @@
                 )
 
 
-def lateral_backward(index_of, bwd_x, bwd_y, spread, mid, total, shift, first, count, unroll):
+def lateral_backward(index_of, bwd_x, bwd_y, spread, mid, total, first, count, unroll):
     @pl.loop(0, count // unroll)
     def _(s):
         start = first + s * unroll
@@ -120,7 +122,9 @@
                     spread[v, start + u], bwd_y[k, v], preferred_element_type=F32
                 ).astype(BF)
         for u, k in enumerate(kernels):
-            total[start + u - shift] = jnp.dot(bwd_x[k][:NEAR], mid[start + u], preferred_element_type=F32).astype(total.dtype)
+            total[start + u] = jnp.dot(
+                bwd_x[k][:NEAR], mid[start + u], preferred_element_type=F32
+            ).reshape(3, BLK, LINE)
 
 
 def taps_over(zi):
@@ -157,6 +161,10 @@
 MESH = pl.DeviceIdType.MESH
 
 
+def worker_of(bx, bz):
+    return 2 * (bx // 2) + (bz % 4) // 2, 4 * (bz // 4) + 2 * (bz % 2) + bx % 2
+
+
 class Copy:
     def __init__(self, src, dst, sems, slot, device, sends, receives):
         self.src, self.sems, self.slot = src, sems, slot
@@ -172,6 +180,7 @@
 
     def lands_in(self, region):
         self.back = self.make(region, self.device)
+        return self
 
     def start(self):
         pl.when(self.sends)(self.out.start)
@@ -186,32 +195,36 @@
 def joint_kernel(nx, nz):
     def body(index_ref, axial_ref, axial_in, bank_ref, labels_ref, estimate_ref, outgoing,
              out_ref, kx, ky, ky_back, ax, fwd_y, bwd_y, fwd_x, bwd_x, edge_x, edge_y, base, mid, grown, spread, total,
-             to_far, to_side, wide, part_mate, part, passing, arrived, slots, slot_ref,
-             halo_sems, sum_sems, first_sems, second_sems, local_sems):
+             to_far, to_corner, to_side, staged, wide, part_mate, part, product, back,
+             passing, arrived, labels, slots, slot_ref,
+             move_sems, halo_sems, sum_sems, first_sems, second_sems, local_sems):
         gx, gz = lax.axis_index("gx"), lax.axis_index("gz")
-        core = gz % 2
-        has_l, has_r = gx > 0, gx < nx - 1
-        across = gz - 1 + 2 * core
-        has_c = (across >= 0) & (across < nz)
-        across = (across + nz) % nz
-        gl, gr = (gx + nx - 1) % nx, (gx + 1) % nx
+        core, high_z = gz % 2, gx % 2
+        bx, bz = gx - high_z + core, gz - gz % 4 + 2 * high_z + (gz % 4) // 2
+        has_d, has_u = bz > 0, bz < nz - 1
+        bc = bx - 1 + 2 * core
+        has_c = (bc >= 0) & (bc < nx)
+        bc, bd, bu = (bc + nx) % nx, (bz + nz - 1) % nz, (bz + 1) % nz
         mate = (gx, gz + 1 - 2 * core)
-        mate_rows, cross_rows = pl.ds(2 * BLK * (1 - core), BLK), pl.ds(2 * BLK * core, BLK)
-        at_mate, at_cross = cross_rows, mate_rows
+        across, down, up = worker_of(bc, bz), worker_of(bx, bd), worker_of(bx, bu)
+        across_down, across_up = worker_of(bc, bd), worker_of(bc, bu)
+        worker, owner = worker_of(gx, gz), (bx, bz)
+        moved = (bx != gx) | (bz != gz)
+        far_side, mate_side = 2 * core, 2 - 2 * core
 
         def index_of(z):
-            return index_ref[jnp.clip(gz * BLK - HALO + z, 0, nz * BLK - 1)]
-
-        wide[0, OWN, OWN] = estimate_ref[...].astype(BF)
+            return index_ref[jnp.clip(bz * BLK - HALO + z, 0, nz * BLK - 1)]
+
+        staged[...] = estimate_ref[...].astype(BF)
         for it in range(ITERS):
-            for missing, rows, columns in (
-                (gx == 0, slice(0, NEAR), LOW), (gx == nx - 1, slice(0, NEAR), HIGH),
-                (gz == 0, LOW, slice(0, NEAR)), (gz == nz - 1, HIGH, slice(0, NEAR)),
-            ):
-                @pl.when(missing)
+            @pl.when(jnp.logical_not(has_c))
+            def _():
+                wide[it, :, far_side] = jnp.zeros((NEAR, BLK, LINE), BF)
+
+            for there, rows in ((has_d, LOW), (has_u, HIGH)):
+                @pl.when(jnp.logical_not(there))
                 def _():
-                    region = wide.at[it, rows, columns]
-                    region[...] = jnp.zeros(region.shape, BF)
+                    wide[it, rows] = jnp.zeros((BLK, 3, BLK, LINE), BF)
 
         barrier = pltpu.get_barrier_semaphore()
 
@@ -224,55 +237,63 @@
             greet((gx - gx % 2 + (gx % 2 + d // 4) % 2, gz - gz % 4 + (gz % 4 + d % 4) % 4))
         extra = 0
         for there, device in (
-            (has_l, (gl, gz)), (has_r, (gr, gz)), (has_c, (gx, across)),
-            (has_c & has_l, (gl, across)), (has_c & has_r, (gr, across)),
+            (has_c, across), (has_d, down), (has_u, up), (has_c & has_d, across_down), (has_c & has_u, across_up),
         ):
             pl.when(there)(lambda device=device: greet(device))
             extra = extra + there.astype(jnp.int32)
         pl.semaphore_wait(barrier, 22 + extra)
 
+        moves = [
+            Copy(staged, wide.at[0, OWN, 1], move_sems, 0, worker, moved, moved),
+            Copy(labels_ref, labels, move_sems, 1, worker, moved, moved),
+        ]
+        bring = Copy(product, back, move_sems, 2, owner, moved, moved)
+
         def halo(it):
             w = wide.at[it]
             sems = (halo_sems[0].at[it], halo_sems[1].at[it])
-            own = w.at[OWN, OWN]
+            own = w.at[OWN, 1]
             near = [
-                Copy(own, w.at[OWN, LOW], sems, 0, (gr, gz), has_r, has_l),
-                Copy(own, w.at[OWN, HIGH], sems, 1, (gl, gz), has_l, has_r),
-            ]
-            far = [
-                Copy(own, w.at[at_mate, OWN], sems, 2, mate, True, True),
-                Copy(own, w.at[at_cross, LOW], sems, 3, (gr, across), has_c & has_r, has_c & has_l),
-                Copy(own, w.at[at_cross, HIGH], sems, 4, (gl, across), has_c & has_l, has_c & has_r),
-                Copy(own, w.at[at_cross, OWN], sems, 5, (gx, across), has_c, has_c),
+                Copy(own, w.at[OWN, mate_side], sems, 1, across, has_c, has_c).lands_in(w.at[OWN, far_side]),
+                Copy(own, w.at[OWN, far_side], sems, 0, mate, True, True).lands_in(w.at[OWN, mate_side]),
+            ]
+            straight = [
+                Copy(own, w.at[LOW, 1], sems, 2, up, has_u, has_d),
+                Copy(own, w.at[HIGH, 1], sems, 3, down, has_d, has_u),
+            ]
+            corner = [
+                Copy(own, w.at[LOW, mate_side], sems, 4, across_up, has_c & has_u, has_c & has_d).lands_in(
+                    w.at[LOW, far_side]),
+                Copy(own, w.at[HIGH, mate_side], sems, 5, across_down, has_c & has_d, has_c & has_u).lands_in(
+                    w.at[HIGH, far_side]),
             ]
             relay = [
-                Copy(w.at[OWN, LOW], w.at[at_mate, LOW], sems, 6, mate, has_l, has_l),
-                Copy(w.at[OWN, HIGH], w.at[at_mate, HIGH], sems, 7, mate, has_r, has_r),
-            ]
-            for copy, rows, columns in (
-                (far[0], mate_rows, OWN), (far[1], cross_rows, LOW), (far[2], cross_rows, HIGH),
-                (far[3], cross_rows, OWN), (relay[0], mate_rows, LOW), (relay[1], mate_rows, HIGH),
-            ):
-                copy.lands_in(w.at[rows, columns])
-            return near, far, relay
+                Copy(w.at[LOW, 1], w.at[LOW, far_side], sems, 6, mate, has_d, has_d).lands_in(w.at[LOW, mate_side]),
+                Copy(w.at[HIGH, 1], w.at[HIGH, far_side], sems, 7, mate, has_u, has_u).lands_in(w.at[HIGH, mate_side]),
+            ]
+            return near, straight, corner, relay
 
         def sums(it):
             sems = (sum_sems[0].at[it], sum_sems[1].at[it])
             p = part.at[it]
-            to_mate = Copy(total.at[mate_rows], part_mate.at[it], sems, 0, mate, True, True)
-            to_cross = [
-                Copy(to_far.at[:, LOW], p.at[2], sems, 1, (gl, across), has_c & has_l, has_c & has_r),
-                Copy(to_far.at[:, HIGH], p.at[1], sems, 2, (gr, across), has_c & has_r, has_c & has_l),
-                Copy(to_far.at[:, OWN], p.at[0], sems, 3, (gx, across), has_c, has_c),
-            ]
-            aside = []
-            for half in range(2):
-                there = slice(8 * half, 8 * half + 8)
-                aside.append([
-                    Copy(to_side.at[0, there], p.at[4, there], sems, 4 + 2 * half, (gl, gz), has_l, has_r),
-                    Copy(to_side.at[1, there], p.at[3, there], sems, 5 + 2 * half, (gr, gz), has_r, has_l),
-                ])
-            return to_mate, to_cross, aside
+            halves = [slice(BLK, BLK + 8), slice(BLK + 8, 2 * BLK)]
+            to_mate = [
+                Copy(total.at[rows, mate_side], part_mate.at[it, rows], sems, i, mate, there, there)
+                for i, (rows, there) in enumerate(((LOW, has_d), (HIGH, has_u), (halves[0], True), (halves[1], True)))
+            ]
+            straight = [
+                Copy(to_far.at[0], p.at[0], sems, 4, down, has_d, has_u),
+                Copy(to_far.at[1], p.at[1], sems, 5, up, has_u, has_d),
+            ]
+            corner = [
+                Copy(to_corner.at[0], p.at[2], sems, 6, across_down, has_c & has_d, has_c & has_u),
+                Copy(to_corner.at[1], p.at[3], sems, 7, across_up, has_c & has_u, has_c & has_d),
+            ]
+            aside = [
+                Copy(to_side.at[rows], p.at[4, rows], sems, 8 + i, across, has_c, has_c)
+                for i, rows in enumerate((slice(0, 8), slice(8, 16)))
+            ]
+            return to_mate, straight, corner, aside
 
         def first_stage(d):
             y, x = (gx // 2 + d // 4) % 4, (gz // 4 + d % 4) % 4
@@ -285,7 +306,7 @@
         def second_stage(d):
             high, low = (gx % 2 + d // 4) % 2, (gz % 4 + d % 4) % 4
             return pltpu.make_async_remote_copy(
-                src_ref=passing.at[:, :, high, low], dst_ref=arrived.at[:, gx % 2, :, gz % 4],
+                src_ref=passing.at[:, :, low % 2, 2 * high + low // 2], dst_ref=arrived.at[:, gx % 2, :, gz % 4],
                 send_sem=second_sems[0].at[d], recv_sem=second_sems[1].at[d],
                 device_id=(gx - gx % 2 + high, gz - gz % 4 + low), device_id_type=MESH,
             )
@@ -294,30 +315,42 @@
             outgoing.at[gx // 2, :, gz // 4], passing.at[gx // 2, gz // 4], local_sems.at[0]
         )
         stay_second = pltpu.make_async_copy(
-            passing.at[:, :, gx % 2, gz % 4], arrived.at[:, gx % 2, :, gz % 4], local_sems.at[1]
+            passing.at[:, :, core, 2 * high_z + (gz % 4) // 2], arrived.at[:, gx % 2, :, gz % 4], local_sems.at[1]
         )
         slot_copy = pltpu.make_async_copy(slots, slot_ref, local_sems.at[2])
 
+        for copy in moves:
+            copy.start()
+
+        @pl.when(jnp.logical_not(moved))
+        def _():
+            wide[0, OWN, 1] = staged[...]
+            labels[...] = labels_ref[...]
+
+        stay_first.start()
+        for d in range(1, 16):
+            first_stage(d).start()
+        load_taps(bank_ref, axial_in, kx, ky, ax)
+        reverse_taps(ky, ky_back)
+        for copy in moves:
+            copy.wait_recv()
+
         for it in range(ITERS):
             w = wide.at[it]
-            near, far, relay = halo(it)
-            if it == 0:
-                stay_first.start()
-                for d in range(1, 16):
-                    first_stage(d).start()
-            for copy in near + far:
+            near, straight, corner, relay = halo(it)
+            for copy in near + straight + corner:
                 copy.start()
             if it == 0:
-                slots_of(labels_ref[...], slots)
+                build_bands(ky_back, kx, ax, fwd_y, fwd_x, False)
+                slots_of(labels[...], slots)
                 slot_copy.start()
-                load_taps(bank_ref, axial_in, kx, ky, ax)
-                reverse_taps(ky, ky_back)
-                build_bands(ky_back, kx, ax, fwd_y, fwd_x, False)
             for copy in near:
+                copy.wait_recv()
+            lateral_forward(index_of, fwd_x, fwd_y, w, mid, grown, BLK, BLK, UNROLL)
+            for copy in straight:
                 copy.wait_recv()
             for copy in relay:
                 copy.start()
-            lateral_forward(index_of, fwd_x, fwd_y, w, mid, grown, BLK, BLK, UNROLL)
             if it == 0:
                 stay_first.wait()
                 for d in range(1, 16):
@@ -325,14 +358,12 @@
                 for d in range(1, 8):
                     second_stage(d).start()
                 stay_second.start()
-            for copy in [far[0]] + relay:
-                copy.wait_recv()
-            lateral_forward(index_of, fwd_x, fwd_y, w, mid, grown, 2 * BLK * (1 - core), BLK, UNROLL)
-            for copy in far[1:]:
-                copy.wait_recv()
-            lateral_forward(index_of, fwd_x, fwd_y, w, mid, grown, 2 * BLK * core, BLK, UNROLL)
+            for copy in corner + relay:
+                copy.wait_recv()
+            lateral_forward(index_of, fwd_x, fwd_y, w, mid, grown, 0, BLK, UNROLL)
+            lateral_forward(index_of, fwd_x, fwd_y, w, mid, grown, 2 * BLK, BLK, UNROLL)
             if it == 0:
-                ones_response(index_of, ax, kx, ky, gx * BLK, gz * BLK, edge_x, edge_y, base, nx * BLK, nz * BLK)
+                ones_response(index_of, ax, kx, ky, bx * BLK, bz * BLK, edge_x, edge_y, base, nx * BLK, nz * BLK)
                 build_bands(ky, kx, ax, bwd_y, bwd_x, True)
                 for d in range(1, 16):
                     first_stage(d).wait_send()
@@ -340,46 +371,56 @@
                     second_stage(d).wait()
                 stay_second.wait()
                 slot_copy.wait()
-            for copy in near + far + relay:
+                for copy in moves:
+                    copy.wait_send()
+            for copy in near + straight + corner + relay:
                 copy.wait_send()
 
-            axial_and_ratio(axial_ref, slot_ref, grown, lambda s: arrived[s // 32, (s // 16) % 2, (s // 4) % 4, s % 4], spread)
-            to_mate, to_cross, aside = sums(it)
-            lateral_backward(index_of, bwd_x, bwd_y, spread, mid, to_far, 2 * BLK * core, 2 * BLK * core, BLK, UNROLL)
-            for copy in to_cross:
-                copy.start()
-            lateral_backward(index_of, bwd_x, bwd_y, spread, mid, total, 0, 2 * BLK * (1 - core), BLK, UNROLL)
-            to_mate.start()
+            axial_and_ratio(axial_ref, slot_ref, grown, lambda s: arrived[s // 32, (s // 16) % 2, (s // 4) % 4, s % 4],
+                            spread)
+            to_mate, straight, corner, aside = sums(it)
+            for i, rows in enumerate((LOW, HIGH)):
+                lateral_backward(index_of, bwd_x, bwd_y, spread, mid, total, rows.start, BLK, UNROLL)
+                to_mate[i].start()
+                to_corner[i] = total[rows, far_side].astype(BF)
+                corner[i].start()
+            for i, rows in enumerate((LOW, HIGH)):
+                to_mate[i].wait_recv()
+                to_far[i] = (total[rows, 1] + jnp.where((has_d, has_u)[i], part_mate[it, rows], 0.0)).astype(BF)
+                straight[i].start()
             for half in range(2):
                 first = BLK + 8 * half
-                lateral_backward(index_of, bwd_x, bwd_y, spread, mid, total, 0, first, 8, UNROLL)
-                if half == 0:
-                    to_mate.wait_recv()
-                there = slice(8 * half, 8 * half + 8)
-                both = total[first : first + 8] + part_mate[it, there]
-                total[first : first + 8, OWN] = both[:, OWN]
-                to_side[0, there] = both[:, LOW].astype(BF)
-                to_side[1, there] = both[:, HIGH].astype(BF)
-                for copy in aside[half]:
-                    copy.start()
-            inner = base[...] + total[OWN, OWN]
-            for copy in to_cross:
-                copy.wait_recv()
-            for there, which in ((has_c, 0), (has_c & has_l, 1), (has_c & has_r, 2)):
+                lateral_backward(index_of, bwd_x, bwd_y, spread, mid, total, first, 8, UNROLL)
+                to_side[8 * half : 8 * half + 8] = total[first : first + 8, far_side].astype(BF)
+                aside[half].start()
+                to_mate[2 + half].start()
+            inner = base[...] + total[OWN, 1]
+            gain = (1.0 / VIEWS) if it == 0 else product[...] * (1.0 / VIEWS)
+            for copy in to_mate[2:]:
+                copy.wait_recv()
+            inner = inner + part_mate[it, OWN]
+            for copy in straight + corner:
+                copy.wait_recv()
+            for there, which in ((has_u, 0), (has_d, 1), (has_c & has_u, 2), (has_c & has_d, 3)):
                 inner = inner + jnp.where(there, part[it, which].astype(F32), 0.0)
-            before = estimate_ref if it == 0 else out_ref
-            scaled = before[...] * (1.0 / VIEWS)
-            for pair in aside:
-                for copy in pair:
-                    copy.wait_recv()
-            for there, which in ((has_l, 3), (has_r, 4)):
-                inner = inner + jnp.where(there, part[it, which].astype(F32), 0.0)
-            after = scaled * inner
-            out_ref[...] = after
+            for copy in aside:
+                copy.wait_recv()
+            inner = inner + jnp.where(has_c, part[it, 4].astype(F32), 0.0)
+            product[...] = inner * gain
             if it + 1 < ITERS:
-                wide[it + 1, OWN, OWN] = after.astype(BF)
-            for copy in [to_mate] + to_cross + aside[0] + aside[1]:
+                wide[it + 1, OWN, 1] = (wide[it, OWN, 1].astype(F32) * product[...]).astype(BF)
+            else:
+                bring.start()
+            for copy in to_mate + straight + corner + aside:
                 copy.wait_send()
+
+        @pl.when(jnp.logical_not(moved))
+        def _():
+            back[...] = product[...]
+
+        bring.wait_recv()
+        out_ref[...] = estimate_ref[...] * back[...]
+        bring.wait_send()
 
     smem = pl.BlockSpec(memory_space=pltpu.SMEM)
     vmem = pl.BlockSpec(memory_space=pltpu.VMEM)
@@ -406,18 +447,24 @@
             pltpu.VMEM((NEAR, VIEWS * BLK, LINE), BF),
             pltpu.VMEM((VIEWS, NEAR, BLK, LINE), F32),
             pltpu.VMEM((VIEWS, NEAR, BLK, LINE), BF),
-            pltpu.VMEM((NEAR, NEAR, LINE), F32),
-            pltpu.VMEM((BLK, NEAR, LINE), BF),
+            pltpu.VMEM((NEAR, 3, BLK, LINE), F32),
             pltpu.VMEM((2,) + block, BF),
-            pltpu.VMEM((ITERS, NEAR, NEAR, LINE), BF),
-            pltpu.VMEM((ITERS, BLK, NEAR, LINE), F32),
+            pltpu.VMEM((2,) + block, BF),
+            pltpu.VMEM(block, BF),
+            pltpu.VMEM(block, BF),
+            pltpu.VMEM((ITERS, NEAR, 3, BLK, LINE), BF),
+            pltpu.VMEM((ITERS, NEAR, BLK, LINE), F32),
             pltpu.VMEM((ITERS, 5) + block, BF),
+            pltpu.VMEM(block, F32),
+            pltpu.VMEM(block, F32),
             pltpu.VMEM((4, 4, 2, 4, BLK, LINE), BF),
             pltpu.VMEM((4, 2, 4, 4, BLK, LINE), BF),
             pltpu.VMEM((1, LINE), jnp.int32),
+            pltpu.VMEM((1, LINE), jnp.int32),
             pltpu.SMEM((1, LINE), jnp.int32),
+            (dma((3,)), dma((3,))),
             (dma((ITERS, 8)), dma((ITERS, 8))),
-            (dma((ITERS, 8)), dma((ITERS, 8))),
+            (dma((ITERS, 10)), dma((ITERS, 10))),
             (dma((16,)), dma((16,))),
             (dma((8,)), dma((8,))),
             dma((3,)),

time: 68.7 us -> 66.6 us (0.969)
  the two profiles are of different devices: /device:TPU:17 before, /device:TPU:1 now
where the time goes in v6:
time: 66.6 us; the launch traced here: 65.8 us
  Pallas kernels  63.2 us (95%)
  local copies, waits for them, and re-layouts  2.49 us (4%)
    pallas_call x1, Pallas kernels, shards(): joint_kernel(nx, nz)  63.2 us
    unnamed x12, local copies, waits for them, and re-layouts  2.49 us

profile of v6, /device:TPU:1, one launch (start us, length us, event | category | flops | bytes accessed | tf_op | source)
XLA Modules:
  0.0 65.8 jit_solution(8707060361431630319)
XLA Ops:
  0.0 0.0 copy-start
  0.0 0.0 copy-start.1
  0.0 0.0 copy-start.2
  0.0 1.2 %copy.7 = bf16[16,8,16,128]{3,2,1,0:T(8,128)(2,1)S(1)} copy(bf16[16,8,16,128]{3,1,2,0:T(8,128)(2,1)} %bitcast.5) | data formatting | bytes 1048576
  1.2 0.0 copy-start.3
  1.2 0.0 copy-start.4
  1.2 0.0 copy-done
  1.2 0.0 copy-done.1
  1.2 0.0 copy-done.2
  1.3 0.6 copy-done.3
  1.9 0.0 copy-done.4
  1.9 63.2 %joint.1 = f32[16,16,128]{2,1,0:T(8,128)S(1)} custom-call(s32[256]{0:T(256)S(1)} %copy-done.3, f32[6,33]{1,0:T(8,128)S(1)} %copy-done.2, f32[6,33]{1,0:T(8,128)S(1)} %copy-done.2, f32[6,16,2,33]{3,2,1,0:T(2,128)S(1)} %copy-done.1, s32[1,128]{1,0:T(1,128)S(1)} %copy-done.4, f32[16,16,128]{2,1,0:T(8,128)S(1)} %copy-done, ...), custom_call_target="tpu_custom_call" | custom-call | tf_op jit(solution)/shard_map/joint/pallas_call | solution.py:481
  65.1 0.7 copy.9
Async XLA Ops:
  0.0 1.2 %copy-start = (f32[16,16,128]{2,1,0:T(8,128)S(1)}, f32[16,16,128]{2,1,0:T(8,128)}, u32[]{:S(2)}) copy-start(f32[16,16,128]{2,1,0:T(8,128)} %estimate_ref.1) | copy-start | bytes 393220
  0.0 1.2 %copy-start.1 = (f32[6,16,2,33]{3,2,1,0:T(2,128)S(1)}, f32[6,16,2,33]{3,2,1,0:T(2,128)}, u32[]{:S(2)}) copy-start(f32[6,16,2,33]{3,2,1,0:T(2,128)} %bank_ref.1) | copy-start | bytes 76036
  0.0 1.2 %copy-start.2 = (f32[6,33]{1,0:T(8,128)S(1)}, f32[6,33]{1,0:T(8,128)}, u32[]{:S(2)}) copy-start(f32[6,33]{1,0:T(8,128)} %axial_in.1) | copy-start | bytes 2380
  1.2 0.7 %copy-start.3 = (s32[256]{0:T(256)S(1)}, s32[256]{0:T(256)}, u32[]{:S(2)}) copy-start(s32[256]{0:T(256)} %index_ref.1) | copy-start | bytes 3076
  1.2 0.7 %copy-start.4 = (s32[1,128]{1,0:T(1,128)S(1)}, s32[1,128]{1,0:T(1,128)}, u32[]{:S(2)}) copy-start(s32[1,128]{1,0:T(1,128)} %labels_ref.1) | copy-start | bytes 1540

commit v7 on v6

--- a/solution.py
+++ b/solution.py
@@ -95,66 +95,91 @@
     slots[...] = jnp.max(jnp.where(hit, iota((LINE, LINE), 0), -1), axis=0, keepdims=True)
 
 
-def lateral_forward(index_of, fwd_x, fwd_y, wide, mid, grown, first, count, unroll):
-    @pl.loop(0, count // unroll)
+def by_views(body):
+    @pl.loop(0, VIEWS // 2)
     def _(s):
-        start = first + s * unroll
-        kernels = [index_of(start + u) for u in range(unroll)]
-        for u, k in enumerate(kernels):
-            mid[start + u] = jnp.dot(
-                fwd_x[k][:, :NEAR], wide[start + u].reshape(NEAR, LINE), preferred_element_type=F32
-            ).astype(BF)
-        for u, k in enumerate(kernels):
-            for v in range(VIEWS):
-                grown[v, start + u] = jnp.dot(
-                    mid[start + u, v * BLK : (v + 1) * BLK, :], fwd_y[k, v], preferred_element_type=F32
-                )
-
-
-def lateral_backward(index_of, bwd_x, bwd_y, spread, mid, total, first, count, unroll):
-    @pl.loop(0, count // unroll)
+        for u in range(2):
+            body(2 * s + u)
+
+
+def columns_forward(index_of, fwd_x, wide, mid, first):
+    @pl.loop(0, BLK // UNROLL)
     def _(s):
-        start = first + s * unroll
-        kernels = [index_of(start + u) for u in range(unroll)]
-        for u, k in enumerate(kernels):
-            for v in range(VIEWS):
-                mid[start + u, v * BLK : (v + 1) * BLK, :] = jnp.dot(
-                    spread[v, start + u], bwd_y[k, v], preferred_element_type=F32
-                ).astype(BF)
-        for u, k in enumerate(kernels):
-            total[start + u] = jnp.dot(
-                bwd_x[k][:NEAR], mid[start + u], preferred_element_type=F32
+        for u in range(UNROLL):
+            z = s * UNROLL + u
+            mid[z] = jnp.dot(
+                fwd_x[index_of(first + z)][:, :NEAR], wide[first + z].reshape(NEAR, LINE), preferred_element_type=F32
+            ).astype(BF).reshape(VIEWS, BLK, LINE)
+
+
+def line_forward(index_of, fwd_y, mid, grown, first, v):
+    for z in range(BLK):
+        grown[v, z] = jnp.dot(mid[z, v], fwd_y[index_of(first + z), v], preferred_element_type=F32)
+
+
+def line_backward(index_of, bwd_y, spread, mid, first, v):
+    for z in range(BLK):
+        mid[z, v] = jnp.dot(spread[v, z], bwd_y[index_of(first + z), v], preferred_element_type=F32).astype(BF)
+
+
+def columns_backward(index_of, bwd_x, mid, total, first, start, count):
+    @pl.loop(0, count // UNROLL)
+    def _(s):
+        for u in range(UNROLL):
+            z = start + s * UNROLL + u
+            total[first + z] = jnp.dot(
+                bwd_x[index_of(first + z)][:NEAR], mid[z].reshape(VIEWS * BLK, LINE), preferred_element_type=F32
             ).reshape(3, BLK, LINE)
 
 
-def taps_over(zi):
+HALVES = (slice(0, 8), slice(8, 16))
+
+
+def reached(zi):
     return range(max(0, zi - 2 * HALO), min(BLK - 1, zi) + 1)
 
 
-def axial_and_ratio(axial_ref, slot_ref, grown, tile_of, spread):
-    @pl.loop(0, VIEWS)
-    def _(v):
-        weights = [axial_ref[v, t] for t in range(TAPS)]
-        seen = jnp.full((8, LINE), slot_ref[0, v * BLK], jnp.int32) >= 0
-        for half in range(2):
-            rows = slice(half * 8, half * 8 + 8)
-            total = [None] * BLK
-            for zi in range(NEAR):
-                g = grown[v, zi, rows, :]
-                for zo in taps_over(zi):
-                    term = weights[zi - zo] * g
-                    total[zo] = term if total[zo] is None else total[zo] + term
-            excess = []
-            for zo in range(BLK):
-                tile = tile_of(jnp.maximum(slot_ref[0, v * BLK + zo], 0))[rows].astype(F32)
-                ratio = (tile / total[zo]).astype(BF).astype(F32)
-                excess.append(jnp.where(seen, ratio - 1.0, 0.0))
-            for zi in range(NEAR):
-                acc = None
-                for zo in taps_over(zi):
-                    term = weights[zi - zo] * excess[zo]
-                    acc = term if acc is None else acc + term
-                spread[v, zi, rows, :] = acc.astype(BF)
+def axial_forward(axial_ref, grown, first, v, rows, total):
+    for z in range(BLK):
+        g = grown[v, z, rows, :]
+        for zo in reached(first + z):
+            term = axial_ref[v, first + z - zo] * g
+            total[zo] = term if total[zo] is None else total[zo] + term
+    return total
+
+
+def axial_backward(axial_ref, excess, spread, first, v, rows):
+    for z in range(BLK):
+        acc = None
+        for zo in reached(first + z):
+            term = axial_ref[v, first + z - zo] * excess[zo]
+            acc = term if acc is None else acc + term
+        spread[v, z, rows, :] = acc.astype(BF)
+
+
+def gather_axial(axial_ref, grown, first, v, blurred):
+    for rows in HALVES:
+        total = [None if first == BLK else blurred[v, zo, rows, :] for zo in range(BLK)]
+        for zo, value in enumerate(axial_forward(axial_ref, grown, first, v, rows, total)):
+            blurred[v, zo, rows, :] = value
+
+
+def ratios(axial_ref, slot_ref, grown, blurred, tile_of, excess, spread, v):
+    seen = jnp.full((8, LINE), slot_ref[0, v * BLK], jnp.int32) >= 0
+    for rows in HALVES:
+        total = axial_forward(axial_ref, grown, 2 * BLK, v, rows, [blurred[v, zo, rows, :] for zo in range(BLK)])
+        over = []
+        for zo in range(BLK):
+            tile = tile_of(jnp.maximum(slot_ref[0, v * BLK + zo], 0))[rows].astype(F32)
+            ratio = (tile / total[zo]).astype(BF).astype(F32)
+            over.append(jnp.where(seen, ratio - 1.0, 0.0))
+            excess[v, zo, rows, :] = over[-1]
+        axial_backward(axial_ref, over, spread, 0, v, rows)
+
+
+def spread_axial(axial_ref, excess, spread, first, v):
+    for rows in HALVES:
+        axial_backward(axial_ref, [excess[v, zo, rows, :] for zo in range(BLK)], spread, first, v, rows)
 
 
 LOW, OWN, HIGH = slice(0, BLK), slice(BLK, 2 * BLK), slice(2 * BLK, NEAR)
@@ -194,7 +219,7 @@
 
 def joint_kernel(nx, nz):
     def body(index_ref, axial_ref, axial_in, bank_ref, labels_ref, estimate_ref, outgoing,
-             out_ref, kx, ky, ky_back, ax, fwd_y, bwd_y, fwd_x, bwd_x, edge_x, edge_y, base, mid, grown, spread, total,
+             out_ref, kx, ky, ky_back, ax, fwd_y, bwd_y, fwd_x, bwd_x, edge_x, edge_y, base, mid, grown, blurred, excess, spread, total,
              to_far, to_corner, to_side, staged, wide, part_mate, part, product, back,
              passing, arrived, labels, slots, slot_ref,
              move_sems, halo_sems, sum_sems, first_sems, second_sems, local_sems):
@@ -346,7 +371,8 @@
                 slot_copy.start()
             for copy in near:
                 copy.wait_recv()
-            lateral_forward(index_of, fwd_x, fwd_y, w, mid, grown, BLK, BLK, UNROLL)
+            columns_forward(index_of, fwd_x, w, mid, BLK)
+            by_views(lambda v: line_forward(index_of, fwd_y, mid, grown[1], BLK, v))
             for copy in straight:
                 copy.wait_recv()
             for copy in relay:
@@ -360,8 +386,14 @@
                 stay_second.start()
             for copy in corner + relay:
                 copy.wait_recv()
-            lateral_forward(index_of, fwd_x, fwd_y, w, mid, grown, 0, BLK, UNROLL)
-            lateral_forward(index_of, fwd_x, fwd_y, w, mid, grown, 2 * BLK, BLK, UNROLL)
+            for i in (0, 2):
+                columns_forward(index_of, fwd_x, w, mid, i * BLK)
+
+                def line_and_axial(v):
+                    line_forward(index_of, fwd_y, mid, grown[i], i * BLK, v)
+                    gather_axial(axial_ref, grown[1 - i // 2], BLK - i // 2 * BLK, v, blurred)
+
+                by_views(line_and_axial)
             if it == 0:
                 ones_response(index_of, ax, kx, ky, bx * BLK, bz * BLK, edge_x, edge_y, base, nx * BLK, nz * BLK)
                 build_bands(ky, kx, ax, bwd_y, bwd_x, True)
@@ -376,11 +408,19 @@
             for copy in near + straight + corner + relay:
                 copy.wait_send()
 
-            axial_and_ratio(axial_ref, slot_ref, grown, lambda s: arrived[s // 32, (s // 16) % 2, (s // 4) % 4, s % 4],
-                            spread)
+            by_views(lambda v: ratios(
+                axial_ref, slot_ref, grown[2], blurred,
+                lambda s: arrived[s // 32, (s // 16) % 2, (s // 4) % 4, s % 4], excess, spread[0], v))
             to_mate, straight, corner, aside = sums(it)
             for i, rows in enumerate((LOW, HIGH)):
-                lateral_backward(index_of, bwd_x, bwd_y, spread, mid, total, rows.start, BLK, UNROLL)
+                this, after = (0, 2) if i == 0 else (2, 1)
+
+                def line_and_spread(v):
+                    line_backward(index_of, bwd_y, spread[this], mid, this * BLK, v)
+                    spread_axial(axial_ref, excess, spread[after], after * BLK, v)
+
+                by_views(line_and_spread)
+                columns_backward(index_of, bwd_x, mid, total, this * BLK, 0, BLK)
                 to_mate[i].start()
                 to_corner[i] = total[rows, far_side].astype(BF)
                 corner[i].start()
@@ -388,9 +428,10 @@
                 to_mate[i].wait_recv()
                 to_far[i] = (total[rows, 1] + jnp.where((has_d, has_u)[i], part_mate[it, rows], 0.0)).astype(BF)
                 straight[i].start()
+            by_views(lambda v: line_backward(index_of, bwd_y, spread[1], mid, BLK, v))
             for half in range(2):
                 first = BLK + 8 * half
-                lateral_backward(index_of, bwd_x, bwd_y, spread, mid, total, first, 8, UNROLL)
+                columns_backward(index_of, bwd_x, mid, total, BLK, 8 * half, 8)
                 to_side[8 * half : 8 * half + 8] = total[first : first + 8, far_side].astype(BF)
                 aside[half].start()
                 to_mate[2 + half].start()
@@ -444,9 +485,11 @@
             pltpu.VMEM((KERNELS, 8, LINE), F32),
             pltpu.VMEM((KERNELS, 8, LINE), F32),
             pltpu.VMEM(block, F32),
-            pltpu.VMEM((NEAR, VIEWS * BLK, LINE), BF),
-            pltpu.VMEM((VIEWS, NEAR, BLK, LINE), F32),
-            pltpu.VMEM((VIEWS, NEAR, BLK, LINE), BF),
+            pltpu.VMEM((BLK, VIEWS, BLK, LINE), BF),
+            [pltpu.VMEM((VIEWS,) + block, F32)] * 3,
+            pltpu.VMEM((VIEWS,) + block, F32),
+            pltpu.VMEM((VIEWS,) + block, F32),
+            [pltpu.VMEM((VIEWS,) + block, BF)] * 3,
             pltpu.VMEM((NEAR, 3, BLK, LINE), F32),
             pltpu.VMEM((2,) + block, BF),
             pltpu.VMEM((2,) + block, BF),

time: 66.6 us -> 73.9 us (1.11)
  Pallas kernels: 63.2 us -> 70.8 us
    pallas_call x1, Pallas kernels: 63.2 us -> 70.8 us  [shards(): joint_kernel(nx, nz)]
where the time goes in v7:
time: 73.9 us; the launch traced here: 73.4 us
  Pallas kernels  70.8 us (96%)
  local copies, waits for them, and re-layouts  2.49 us (3%)
    pallas_call x1, Pallas kernels, shards(): joint_kernel(nx, nz)  70.8 us
    unnamed x12, local copies, waits for them, and re-layouts  2.49 us

profile of v7, /device:TPU:1, one launch (start us, length us, event | category | flops | bytes accessed | tf_op | source)
XLA Modules:
  0.0 73.4 jit_solution(10397667959927406052)
XLA Ops:
  0.0 0.0 copy-start
  0.0 0.0 copy-start.1
  0.0 0.0 copy-start.2
  0.0 1.2 %copy.7 = bf16[16,8,16,128]{3,2,1,0:T(8,128)(2,1)S(1)} copy(bf16[16,8,16,128]{3,1,2,0:T(8,128)(2,1)} %bitcast.5) | data formatting | bytes 1048576
  1.2 0.0 copy-start.3
  1.2 0.0 copy-start.4
  1.2 0.0 copy-done
  1.2 0.0 copy-done.1
  1.2 0.0 copy-done.2
  1.3 0.6 copy-done.3
  1.9 0.0 copy-done.4
  1.9 70.8 %joint.1 = f32[16,16,128]{2,1,0:T(8,128)S(1)} custom-call(s32[256]{0:T(256)S(1)} %copy-done.3, f32[6,33]{1,0:T(8,128)S(1)} %copy-done.2, f32[6,33]{1,0:T(8,128)S(1)} %copy-done.2, f32[6,16,2,33]{3,2,1,0:T(2,128)S(1)} %copy-done.1, s32[1,128]{1,0:T(1,128)S(1)} %copy-done.4, f32[16,16,128]{2,1,0:T(8,128)S(1)} %copy-done, ...), custom_call_target="tpu_custom_call" | custom-call | tf_op jit(solution)/shard_map/joint/pallas_call | solution.py:524
  72.7 0.7 copy.9
Async XLA Ops:
  0.0 1.2 %copy-start = (f32[16,16,128]{2,1,0:T(8,128)S(1)}, f32[16,16,128]{2,1,0:T(8,128)}, u32[]{:S(2)}) copy-start(f32[16,16,128]{2,1,0:T(8,128)} %estimate_ref.1) | copy-start | bytes 393220
  0.0 1.2 %copy-start.1 = (f32[6,16,2,33]{3,2,1,0:T(2,128)S(1)}, f32[6,16,2,33]{3,2,1,0:T(2,128)}, u32[]{:S(2)}) copy-start(f32[6,16,2,33]{3,2,1,0:T(2,128)} %bank_ref.1) | copy-start | bytes 76036
  0.0 1.2 %copy-start.2 = (f32[6,33]{1,0:T(8,128)S(1)}, f32[6,33]{1,0:T(8,128)}, u32[]{:S(2)}) copy-start(f32[6,33]{1,0:T(8,128)} %axial_in.1) | copy-start | bytes 2380
  1.2 0.7 copy-start.3
  1.2 0.7 copy-start.4

commit v8 on v6

--- a/solution.py
+++ b/solution.py
@@ -12,7 +12,6 @@
 KERNELS = 16
 BLK = 16
 NEAR = 48
-UNROLL = 8
 LINE = 128
 F32 = jnp.float32
 BF = jnp.bfloat16
@@ -95,66 +94,71 @@
     slots[...] = jnp.max(jnp.where(hit, iota((LINE, LINE), 0), -1), axis=0, keepdims=True)
 
 
-def lateral_forward(index_of, fwd_x, fwd_y, wide, mid, grown, first, count, unroll):
-    @pl.loop(0, count // unroll)
-    def _(s):
-        start = first + s * unroll
-        kernels = [index_of(start + u) for u in range(unroll)]
-        for u, k in enumerate(kernels):
-            mid[start + u] = jnp.dot(
-                fwd_x[k][:, :NEAR], wide[start + u].reshape(NEAR, LINE), preferred_element_type=F32
+def lateral_forward(index_of, fwd_x, fwd_y, wide, mid, grown, first):
+    depths = range(first, first + BLK)
+    for z in depths:
+        mid[z] = jnp.dot(
+            fwd_x[index_of(z)][:, :NEAR], wide[z].reshape(NEAR, LINE), preferred_element_type=F32
+        ).astype(BF)
+    for z in depths:
+        for v in range(VIEWS):
+            grown[v, z] = jnp.dot(
+                mid[z, v * BLK : (v + 1) * BLK, :], fwd_y[index_of(z), v], preferred_element_type=F32
+            )
+
+
+def lateral_backward(index_of, bwd_x, bwd_y, spread, mid, total, first):
+    depths = range(first, first + BLK)
+    for z in depths:
+        for v in range(VIEWS):
+            mid[z, v * BLK : (v + 1) * BLK, :] = jnp.dot(
+                spread[v, z], bwd_y[index_of(z), v], preferred_element_type=F32
             ).astype(BF)
-        for u, k in enumerate(kernels):
-            for v in range(VIEWS):
-                grown[v, start + u] = jnp.dot(
-                    mid[start + u, v * BLK : (v + 1) * BLK, :], fwd_y[k, v], preferred_element_type=F32
-                )
-
-
-def lateral_backward(index_of, bwd_x, bwd_y, spread, mid, total, first, count, unroll):
-    @pl.loop(0, count // unroll)
-    def _(s):
-        start = first + s * unroll
-        kernels = [index_of(start + u) for u in range(unroll)]
-        for u, k in enumerate(kernels):
-            for v in range(VIEWS):
-                mid[start + u, v * BLK : (v + 1) * BLK, :] = jnp.dot(
-                    spread[v, start + u], bwd_y[k, v], preferred_element_type=F32
-                ).astype(BF)
-        for u, k in enumerate(kernels):
-            total[start + u] = jnp.dot(
-                bwd_x[k][:NEAR], mid[start + u], preferred_element_type=F32
-            ).reshape(3, BLK, LINE)
-
-
-def taps_over(zi):
+    for z in depths:
+        total[z] = jnp.dot(bwd_x[index_of(z)][:NEAR], mid[z], preferred_element_type=F32).reshape(3, BLK, LINE)
+
+
+HALVES = (slice(0, 8), slice(8, 16))
+
+
+def reached(zi):
     return range(max(0, zi - 2 * HALO), min(BLK - 1, zi) + 1)
 
 
-def axial_and_ratio(axial_ref, slot_ref, grown, tile_of, spread):
+def axial_backward(axial_ref, excess, spread, first, v, rows):
+    for zi in range(first, first + BLK):
+        acc = None
+        for zo in reached(zi):
+            term = axial_ref[v, zi - zo] * excess[zo]
+            acc = term if acc is None else acc + term
+        spread[v, zi, rows, :] = acc.astype(BF)
+
+
+def ratios(axial_ref, slot_ref, grown, tile_of, excess, spread):
     @pl.loop(0, VIEWS)
     def _(v):
-        weights = [axial_ref[v, t] for t in range(TAPS)]
         seen = jnp.full((8, LINE), slot_ref[0, v * BLK], jnp.int32) >= 0
-        for half in range(2):
-            rows = slice(half * 8, half * 8 + 8)
+        for rows in HALVES:
             total = [None] * BLK
             for zi in range(NEAR):
                 g = grown[v, zi, rows, :]
-                for zo in taps_over(zi):
-                    term = weights[zi - zo] * g
+                for zo in reached(zi):
+                    term = axial_ref[v, zi - zo] * g
                     total[zo] = term if total[zo] is None else total[zo] + term
-            excess = []
+            over = []
             for zo in range(BLK):
                 tile = tile_of(jnp.maximum(slot_ref[0, v * BLK + zo], 0))[rows].astype(F32)
                 ratio = (tile / total[zo]).astype(BF).astype(F32)
-                excess.append(jnp.where(seen, ratio - 1.0, 0.0))
-            for zi in range(NEAR):
-                acc = None
-                for zo in taps_over(zi):
-                    term = weights[zi - zo] * excess[zo]
-                    acc = term if acc is None else acc + term
-                spread[v, zi, rows, :] = acc.astype(BF)
+                over.append(jnp.where(seen, ratio - 1.0, 0.0))
+                excess[v, zo, rows, :] = over[-1]
+            axial_backward(axial_ref, over, spread, 0, v, rows)
+
+
+def spread_axial(axial_ref, excess, spread, first):
+    @pl.loop(0, VIEWS)
+    def _(v):
+        for rows in HALVES:
+            axial_backward(axial_ref, [excess[v, zo, rows, :] for zo in range(BLK)], spread, first, v, rows)
 
 
 LOW, OWN, HIGH = slice(0, BLK), slice(BLK, 2 * BLK), slice(2 * BLK, NEAR)
@@ -194,7 +198,7 @@
 
 def joint_kernel(nx, nz):
     def body(index_ref, axial_ref, axial_in, bank_ref, labels_ref, estimate_ref, outgoing,
-             out_ref, kx, ky, ky_back, ax, fwd_y, bwd_y, fwd_x, bwd_x, edge_x, edge_y, base, mid, grown, spread, total,
+             out_ref, kx, ky, ky_back, ax, fwd_y, bwd_y, fwd_x, bwd_x, edge_x, edge_y, base, mid, grown, excess, spread, total,
              to_far, to_corner, to_side, staged, wide, part_mate, part, product, back,
              passing, arrived, labels, slots, slot_ref,
              move_sems, halo_sems, sum_sems, first_sems, second_sems, local_sems):
@@ -215,17 +219,6 @@
         def index_of(z):
             return index_ref[jnp.clip(bz * BLK - HALO + z, 0, nz * BLK - 1)]
 
-        staged[...] = estimate_ref[...].astype(BF)
-        for it in range(ITERS):
-            @pl.when(jnp.logical_not(has_c))
-            def _():
-                wide[it, :, far_side] = jnp.zeros((NEAR, BLK, LINE), BF)
-
-            for there, rows in ((has_d, LOW), (has_u, HIGH)):
-                @pl.when(jnp.logical_not(there))
-                def _():
-                    wide[it, rows] = jnp.zeros((BLK, 3, BLK, LINE), BF)
-
         barrier = pltpu.get_barrier_semaphore()
 
         def greet(device):
@@ -241,6 +234,7 @@
         ):
             pl.when(there)(lambda device=device: greet(device))
             extra = extra + there.astype(jnp.int32)
+        staged[...] = estimate_ref[...].astype(BF)
         pl.semaphore_wait(barrier, 22 + extra)
 
         moves = [
@@ -276,10 +270,9 @@
         def sums(it):
             sems = (sum_sems[0].at[it], sum_sems[1].at[it])
             p = part.at[it]
-            halves = [slice(BLK, BLK + 8), slice(BLK + 8, 2 * BLK)]
             to_mate = [
                 Copy(total.at[rows, mate_side], part_mate.at[it, rows], sems, i, mate, there, there)
-                for i, (rows, there) in enumerate(((LOW, has_d), (HIGH, has_u), (halves[0], True), (halves[1], True)))
+                for i, (rows, there) in enumerate(((LOW, has_d), (HIGH, has_u), (OWN, True)))
             ]
             straight = [
                 Copy(to_far.at[0], p.at[0], sems, 4, down, has_d, has_u),
@@ -289,10 +282,7 @@
                 Copy(to_corner.at[0], p.at[2], sems, 6, across_down, has_c & has_d, has_c & has_u),
                 Copy(to_corner.at[1], p.at[3], sems, 7, across_up, has_c & has_u, has_c & has_d),
             ]
-            aside = [
-                Copy(to_side.at[rows], p.at[4, rows], sems, 8 + i, across, has_c, has_c)
-                for i, rows in enumerate((slice(0, 8), slice(8, 16)))
-            ]
+            aside = [Copy(to_side, p.at[4], sems, 8, across, has_c, has_c)]
             return to_mate, straight, corner, aside
 
         def first_stage(d):
@@ -331,6 +321,16 @@
         for d in range(1, 16):
             first_stage(d).start()
         load_taps(bank_ref, axial_in, kx, ky, ax)
+        for it in range(ITERS):
+            @pl.when(jnp.logical_not(has_c))
+            def _():
+                wide[it, :, far_side] = jnp.zeros((NEAR, BLK, LINE), BF)
+
+            for there, rows in ((has_d, LOW), (has_u, HIGH)):
+                @pl.when(jnp.logical_not(there))
+                def _():
+                    wide[it, rows] = jnp.zeros((BLK, 3, BLK, LINE), BF)
+
         reverse_taps(ky, ky_back)
         for copy in moves:
             copy.wait_recv()
@@ -346,7 +346,7 @@
                 slot_copy.start()
             for copy in near:
                 copy.wait_recv()
-            lateral_forward(index_of, fwd_x, fwd_y, w, mid, grown, BLK, BLK, UNROLL)
+            lateral_forward(index_of, fwd_x, fwd_y, w, mid, grown, BLK)
             for copy in straight:
                 copy.wait_recv()
             for copy in relay:
@@ -360,8 +360,8 @@
                 stay_second.start()
             for copy in corner + relay:
                 copy.wait_recv()
-            lateral_forward(index_of, fwd_x, fwd_y, w, mid, grown, 0, BLK, UNROLL)
-            lateral_forward(index_of, fwd_x, fwd_y, w, mid, grown, 2 * BLK, BLK, UNROLL)
+            lateral_forward(index_of, fwd_x, fwd_y, w, mid, grown, 0)
+            lateral_forward(index_of, fwd_x, fwd_y, w, mid, grown, 2 * BLK)
             if it == 0:
                 ones_response(index_of, ax, kx, ky, bx * BLK, bz * BLK, edge_x, edge_y, base, nx * BLK, nz * BLK)
                 build_bands(ky, kx, ax, bwd_y, bwd_x, True)
@@ -376,24 +376,31 @@
             for copy in near + straight + corner + relay:
                 copy.wait_send()
 
-            axial_and_ratio(axial_ref, slot_ref, grown, lambda s: arrived[s // 32, (s // 16) % 2, (s // 4) % 4, s % 4],
-                            spread)
+            ratios(axial_ref, slot_ref, grown,
+                   lambda s: arrived[s // 32, (s // 16) % 2, (s // 4) % 4, s % 4], excess, spread)
             to_mate, straight, corner, aside = sums(it)
-            for i, rows in enumerate((LOW, HIGH)):
-                lateral_backward(index_of, bwd_x, bwd_y, spread, mid, total, rows.start, BLK, UNROLL)
-                to_mate[i].start()
-                to_corner[i] = total[rows, far_side].astype(BF)
-                corner[i].start()
-            for i, rows in enumerate((LOW, HIGH)):
+
+            def send_straight(i, rows, there):
                 to_mate[i].wait_recv()
-                to_far[i] = (total[rows, 1] + jnp.where((has_d, has_u)[i], part_mate[it, rows], 0.0)).astype(BF)
+                to_far[i] = (total[rows, 1] + jnp.where(there, part_mate[it, rows], 0.0)).astype(BF)
                 straight[i].start()
-            for half in range(2):
-                first = BLK + 8 * half
-                lateral_backward(index_of, bwd_x, bwd_y, spread, mid, total, first, 8, UNROLL)
-                to_side[8 * half : 8 * half + 8] = total[first : first + 8, far_side].astype(BF)
-                aside[half].start()
-                to_mate[2 + half].start()
+
+            lateral_backward(index_of, bwd_x, bwd_y, spread, mid, total, 0)
+            to_mate[0].start()
+            to_corner[0] = total[LOW, far_side].astype(BF)
+            corner[0].start()
+            spread_axial(axial_ref, excess, spread, 2 * BLK)
+            lateral_backward(index_of, bwd_x, bwd_y, spread, mid, total, 2 * BLK)
+            to_mate[1].start()
+            to_corner[1] = total[HIGH, far_side].astype(BF)
+            corner[1].start()
+            send_straight(0, LOW, has_d)
+            spread_axial(axial_ref, excess, spread, BLK)
+            send_straight(1, HIGH, has_u)
+            lateral_backward(index_of, bwd_x, bwd_y, spread, mid, total, BLK)
+            to_side[...] = total[OWN, far_side].astype(BF)
+            aside[0].start()
+            to_mate[2].start()
             inner = base[...] + total[OWN, 1]
             gain = (1.0 / VIEWS) if it == 0 else product[...] * (1.0 / VIEWS)
             for copy in to_mate[2:]:
@@ -446,6 +453,7 @@
             pltpu.VMEM(block, F32),
             pltpu.VMEM((NEAR, VIEWS * BLK, LINE), BF),
             pltpu.VMEM((VIEWS, NEAR, BLK, LINE), F32),
+            pltpu.VMEM((VIEWS,) + block, F32),
             pltpu.VMEM((VIEWS, NEAR, BLK, LINE), BF),
             pltpu.VMEM((NEAR, 3, BLK, LINE), F32),
             pltpu.VMEM((2,) + block, BF),

time: 66.6 us -> 68 us (1.021)
  Pallas kernels: 63.2 us -> 65 us
    pallas_call x1, Pallas kernels: 63.2 us -> 65 us  [shards(): joint_kernel(nx, nz)]
where the time goes in v8:
time: 68 us; the launch traced here: 67.6 us
  Pallas kernels  65 us (96%)
  local copies, waits for them, and re-layouts  2.49 us (4%)
    pallas_call x1, Pallas kernels, shards(): joint_kernel(nx, nz)  65 us
    unnamed x12, local copies, waits for them, and re-layouts  2.49 us

profile of v8, /device:TPU:1, one launch (start us, length us, event | category | flops | bytes accessed | tf_op | source)
XLA Modules:
  0.0 67.6 jit_solution(2920552759402984314)
XLA Ops:
  0.0 0.0 copy-start
  0.0 0.0 copy-start.1
  0.0 0.0 copy-start.2
  0.0 1.2 %copy.7 = bf16[16,8,16,128]{3,2,1,0:T(8,128)(2,1)S(1)} copy(bf16[16,8,16,128]{3,1,2,0:T(8,128)(2,1)} %bitcast.5) | data formatting | bytes 1048576
  1.2 0.0 copy-start.3
  1.2 0.0 copy-start.4
  1.2 0.0 copy-done
  1.2 0.0 copy-done.1
  1.2 0.0 copy-done.2
  1.3 0.6 copy-done.3
  1.9 0.0 copy-done.4
  1.9 65.0 %joint.1 = f32[16,16,128]{2,1,0:T(8,128)S(1)} custom-call(s32[256]{0:T(256)S(1)} %copy-done.3, f32[6,33]{1,0:T(8,128)S(1)} %copy-done.2, f32[6,33]{1,0:T(8,128)S(1)} %copy-done.2, f32[6,16,2,33]{3,2,1,0:T(2,128)S(1)} %copy-done.1, s32[1,128]{1,0:T(1,128)S(1)} %copy-done.4, f32[16,16,128]{2,1,0:T(8,128)S(1)} %copy-done, ...), custom_call_target="tpu_custom_call" | custom-call | tf_op jit(solution)/shard_map/joint/pallas_call | solution.py:489
  66.9 0.7 copy.9
Async XLA Ops:
  0.0 1.2 %copy-start = (f32[16,16,128]{2,1,0:T(8,128)S(1)}, f32[16,16,128]{2,1,0:T(8,128)}, u32[]{:S(2)}) copy-start(f32[16,16,128]{2,1,0:T(8,128)} %estimate_ref.1) | copy-start | bytes 393220
  0.0 1.2 %copy-start.1 = (f32[6,16,2,33]{3,2,1,0:T(2,128)S(1)}, f32[6,16,2,33]{3,2,1,0:T(2,128)}, u32[]{:S(2)}) copy-start(f32[6,16,2,33]{3,2,1,0:T(2,128)} %bank_ref.1) | copy-start | bytes 76036
  0.0 1.2 %copy-start.2 = (f32[6,33]{1,0:T(8,128)S(1)}, f32[6,33]{1,0:T(8,128)}, u32[]{:S(2)}) copy-start(f32[6,33]{1,0:T(8,128)} %axial_in.1) | copy-start | bytes 2380
  1.2 0.7 %copy-start.3 = (s32[256]{0:T(256)S(1)}, s32[256]{0:T(256)}, u32[]{:S(2)}) copy-start(s32[256]{0:T(256)} %index_ref.1) | copy-start | bytes 3076
  1.2 0.7 copy-start.4

commit v9 on v8

--- a/solution.py
+++ b/solution.py
@@ -125,11 +125,11 @@
     return range(max(0, zi - 2 * HALO), min(BLK - 1, zi) + 1)
 
 
-def axial_backward(axial_ref, excess, spread, first, v, rows):
+def axial_backward(weights, excess, spread, first, v, rows):
     for zi in range(first, first + BLK):
         acc = None
         for zo in reached(zi):
-            term = axial_ref[v, zi - zo] * excess[zo]
+            term = weights[zi - zo] * excess[zo]
             acc = term if acc is None else acc + term
         spread[v, zi, rows, :] = acc.astype(BF)
 
@@ -137,13 +137,14 @@
 def ratios(axial_ref, slot_ref, grown, tile_of, excess, spread):
     @pl.loop(0, VIEWS)
     def _(v):
+        weights = [axial_ref[v, t] for t in range(TAPS)]
         seen = jnp.full((8, LINE), slot_ref[0, v * BLK], jnp.int32) >= 0
         for rows in HALVES:
             total = [None] * BLK
             for zi in range(NEAR):
                 g = grown[v, zi, rows, :]
                 for zo in reached(zi):
-                    term = axial_ref[v, zi - zo] * g
+                    term = weights[zi - zo] * g
                     total[zo] = term if total[zo] is None else total[zo] + term
             over = []
             for zo in range(BLK):
@@ -151,14 +152,15 @@
                 ratio = (tile / total[zo]).astype(BF).astype(F32)
                 over.append(jnp.where(seen, ratio - 1.0, 0.0))
                 excess[v, zo, rows, :] = over[-1]
-            axial_backward(axial_ref, over, spread, 0, v, rows)
+            axial_backward(weights, over, spread, 0, v, rows)
 
 
 def spread_axial(axial_ref, excess, spread, first):
     @pl.loop(0, VIEWS)
     def _(v):
+        weights = [axial_ref[v, t] for t in range(TAPS)]
         for rows in HALVES:
-            axial_backward(axial_ref, [excess[v, zo, rows, :] for zo in range(BLK)], spread, first, v, rows)
+            axial_backward(weights, [excess[v, zo, rows, :] for zo in range(BLK)], spread, first, v, rows)
 
 
 LOW, OWN, HIGH = slice(0, BLK), slice(BLK, 2 * BLK), slice(2 * BLK, NEAR)

time: 68 us -> 63.4 us (0.932)
  Pallas kernels: 65 us -> 60.5 us
    pallas_call x1, Pallas kernels: 65 us -> 60.5 us  [shards(): joint_kernel(nx, nz)]
where the time goes in v9:
time: 63.4 us; the launch traced here: 63 us
  Pallas kernels  60.5 us (95%)
  local copies, waits for them, and re-layouts  2.49 us (4%)
    pallas_call x1, Pallas kernels, shards(): joint_kernel(nx, nz)  60.5 us
    unnamed x12, local copies, waits for them, and re-layouts  2.49 us

profile of v9, /device:TPU:1, one launch (start us, length us, event | category | flops | bytes accessed | tf_op | source)
XLA Modules:
  0.0 63.0 jit_solution(7208689434142231557)
XLA Ops:
  0.0 0.0 copy-start
  0.0 0.0 copy-start.1
  0.0 0.0 copy-start.2
  0.0 1.2 %copy.7 = bf16[16,8,16,128]{3,2,1,0:T(8,128)(2,1)S(1)} copy(bf16[16,8,16,128]{3,1,2,0:T(8,128)(2,1)} %bitcast.5) | data formatting | bytes 1048576
  1.2 0.0 copy-start.3
  1.2 0.0 copy-start.4
  1.2 0.0 copy-done
  1.2 0.0 copy-done.1
  1.2 0.0 copy-done.2
  1.3 0.6 copy-done.3
  1.9 0.0 copy-done.4
  1.9 60.5 %joint.1 = f32[16,16,128]{2,1,0:T(8,128)S(1)} custom-call(s32[256]{0:T(256)S(1)} %copy-done.3, f32[6,33]{1,0:T(8,128)S(1)} %copy-done.2, f32[6,33]{1,0:T(8,128)S(1)} %copy-done.2, f32[6,16,2,33]{3,2,1,0:T(2,128)S(1)} %copy-done.1, s32[1,128]{1,0:T(1,128)S(1)} %copy-done.4, f32[16,16,128]{2,1,0:T(8,128)S(1)} %copy-done, ...), custom_call_target="tpu_custom_call" | custom-call | tf_op jit(solution)/shard_map/joint/pallas_call | solution.py:491
  62.4 0.7 %copy.9 = f32[16,16,128]{2,1,0:T(8,128)} copy(f32[16,16,128]{2,1,0:T(8,128)S(1)} %joint.1) | data formatting | bytes 262144
Async XLA Ops:
  0.0 1.2 %copy-start = (f32[16,16,128]{2,1,0:T(8,128)S(1)}, f32[16,16,128]{2,1,0:T(8,128)}, u32[]{:S(2)}) copy-start(f32[16,16,128]{2,1,0:T(8,128)} %estimate_ref.1) | copy-start | bytes 393220
  0.0 1.2 %copy-start.1 = (f32[6,16,2,33]{3,2,1,0:T(2,128)S(1)}, f32[6,16,2,33]{3,2,1,0:T(2,128)}, u32[]{:S(2)}) copy-start(f32[6,16,2,33]{3,2,1,0:T(2,128)} %bank_ref.1) | copy-start | bytes 76036
  0.0 1.2 %copy-start.2 = (f32[6,33]{1,0:T(8,128)S(1)}, f32[6,33]{1,0:T(8,128)}, u32[]{:S(2)}) copy-start(f32[6,33]{1,0:T(8,128)} %axial_in.1) | copy-start | bytes 2380
  1.2 0.7 %copy-start.3 = (s32[256]{0:T(256)S(1)}, s32[256]{0:T(256)}, u32[]{:S(2)}) copy-start(s32[256]{0:T(256)} %index_ref.1) | copy-start | bytes 3076
  1.2 0.7 %copy-start.4 = (s32[1,128]{1,0:T(1,128)S(1)}, s32[1,128]{1,0:T(1,128)}, u32[]{:S(2)}) copy-start(s32[1,128]{1,0:T(1,128)} %labels_ref.1) | copy-start | bytes 1540

commit v10 on v9

--- a/solution.py
+++ b/solution.py
@@ -334,25 +334,24 @@
                     wide[it, rows] = jnp.zeros((BLK, 3, BLK, LINE), BF)
 
         reverse_taps(ky, ky_back)
+        build_bands(ky_back, kx, ax, fwd_y, fwd_x, False)
         for copy in moves:
             copy.wait_recv()
 
+        pending = []
         for it in range(ITERS):
             w = wide.at[it]
             near, straight, corner, relay = halo(it)
             for copy in near + straight + corner:
                 copy.start()
+            for copy in pending:
+                copy.wait_send()
             if it == 0:
-                build_bands(ky_back, kx, ax, fwd_y, fwd_x, False)
+                build_bands(ky, kx, ax, bwd_y, bwd_x, True)
                 slots_of(labels[...], slots)
                 slot_copy.start()
             for copy in near:
                 copy.wait_recv()
-            lateral_forward(index_of, fwd_x, fwd_y, w, mid, grown, BLK)
-            for copy in straight:
-                copy.wait_recv()
-            for copy in relay:
-                copy.start()
             if it == 0:
                 stay_first.wait()
                 for d in range(1, 16):
@@ -360,13 +359,17 @@
                 for d in range(1, 8):
                     second_stage(d).start()
                 stay_second.start()
+            lateral_forward(index_of, fwd_x, fwd_y, w, mid, grown, BLK)
+            for copy in straight:
+                copy.wait_recv()
+            for copy in relay:
+                copy.start()
             for copy in corner + relay:
                 copy.wait_recv()
             lateral_forward(index_of, fwd_x, fwd_y, w, mid, grown, 0)
             lateral_forward(index_of, fwd_x, fwd_y, w, mid, grown, 2 * BLK)
             if it == 0:
                 ones_response(index_of, ax, kx, ky, bx * BLK, bz * BLK, edge_x, edge_y, base, nx * BLK, nz * BLK)
-                build_bands(ky, kx, ax, bwd_y, bwd_x, True)
                 for d in range(1, 16):
                     first_stage(d).wait_send()
                 for d in range(1, 8):
@@ -420,13 +423,14 @@
                 wide[it + 1, OWN, 1] = (wide[it, OWN, 1].astype(F32) * product[...]).astype(BF)
             else:
                 bring.start()
-            for copy in to_mate + straight + corner + aside:
-                copy.wait_send()
+            pending = to_mate + straight + corner + aside
 
         @pl.when(jnp.logical_not(moved))
         def _():
             back[...] = product[...]
 
+        for copy in pending:
+            copy.wait_send()
         bring.wait_recv()
         out_ref[...] = estimate_ref[...] * back[...]
         bring.wait_send()

time: 63.4 us -> 62.5 us (0.986)
  Pallas kernels: 60.5 us -> 59.8 us
    pallas_call x1, Pallas kernels: 60.5 us -> 59.8 us  [shards(): joint_kernel(nx, nz)]
where the time goes in v10:
time: 62.5 us; the launch traced here: 62.3 us
  Pallas kernels  59.8 us (96%)
  local copies, waits for them, and re-layouts  2.49 us (4%)
    pallas_call x1, Pallas kernels, shards(): joint_kernel(nx, nz)  59.8 us
    unnamed x12, local copies, waits for them, and re-layouts  2.49 us

profile of v10, /device:TPU:1, one launch (start us, length us, event | category | flops | bytes accessed | tf_op | source)
XLA Modules:
  0.0 62.3 jit_solution(509130253626627071)
XLA Ops:
  0.0 0.0 copy-start
  0.0 0.0 copy-start.1
  0.0 0.0 copy-start.2
  0.0 1.2 %copy.7 = bf16[16,8,16,128]{3,2,1,0:T(8,128)(2,1)S(1)} copy(bf16[16,8,16,128]{3,1,2,0:T(8,128)(2,1)} %bitcast.5) | data formatting | bytes 1048576
  1.2 0.0 copy-start.3
  1.2 0.0 copy-start.4
  1.2 0.0 copy-done
  1.2 0.0 copy-done.1
  1.2 0.0 copy-done.2
  1.3 0.6 %copy-done.3 = s32[256]{0:T(256)S(1)} copy-done((s32[256]{0:T(256)S(1)}, s32[256]{0:T(256)}, u32[]{:S(2)}) %copy-start.3) | copy-done | bytes 1048
  1.9 0.0 copy-done.4
  1.9 59.8 %joint.1 = f32[16,16,128]{2,1,0:T(8,128)S(1)} custom-call(s32[256]{0:T(256)S(1)} %copy-done.3, f32[6,33]{1,0:T(8,128)S(1)} %copy-done.2, f32[6,33]{1,0:T(8,128)S(1)} %copy-done.2, f32[6,16,2,33]{3,2,1,0:T(2,128)S(1)} %copy-done.1, s32[1,128]{1,0:T(1,128)S(1)} %copy-done.4, f32[16,16,128]{2,1,0:T(8,128)S(1)} %copy-done, ...), custom_call_target="tpu_custom_call" | custom-call | tf_op jit(solution)/shard_map/joint/pallas_call | solution.py:495
  61.7 0.7 %copy.9 = f32[16,16,128]{2,1,0:T(8,128)} copy(f32[16,16,128]{2,1,0:T(8,128)S(1)} %joint.1) | data formatting | bytes 262144
Async XLA Ops:
  0.0 1.2 %copy-start = (f32[16,16,128]{2,1,0:T(8,128)S(1)}, f32[16,16,128]{2,1,0:T(8,128)}, u32[]{:S(2)}) copy-start(f32[16,16,128]{2,1,0:T(8,128)} %estimate_ref.1) | copy-start | bytes 393220
  0.0 1.2 %copy-start.1 = (f32[6,16,2,33]{3,2,1,0:T(2,128)S(1)}, f32[6,16,2,33]{3,2,1,0:T(2,128)}, u32[]{:S(2)}) copy-start(f32[6,16,2,33]{3,2,1,0:T(2,128)} %bank_ref.1) | copy-start | bytes 76036
  0.0 1.2 %copy-start.2 = (f32[6,33]{1,0:T(8,128)S(1)}, f32[6,33]{1,0:T(8,128)}, u32[]{:S(2)}) copy-start(f32[6,33]{1,0:T(8,128)} %axial_in.1) | copy-start | bytes 2380
  1.2 0.7 %copy-start.3 = (s32[256]{0:T(256)S(1)}, s32[256]{0:T(256)}, u32[]{:S(2)}) copy-start(s32[256]{0:T(256)} %index_ref.1) | copy-start | bytes 3076
  1.2 0.7 %copy-start.4 = (s32[1,128]{1,0:T(1,128)S(1)}, s32[1,128]{1,0:T(1,128)}, u32[]{:S(2)}) copy-start(s32[1,128]{1,0:T(1,128)} %labels_ref.1) | copy-start | bytes 1540

commit v11 on v10

--- a/solution.py
+++ b/solution.py
@@ -243,7 +243,7 @@
             Copy(staged, wide.at[0, OWN, 1], move_sems, 0, worker, moved, moved),
             Copy(labels_ref, labels, move_sems, 1, worker, moved, moved),
         ]
-        bring = Copy(product, back, move_sems, 2, owner, moved, moved)
+        bring = [Copy(product.at[rows], back.at[rows], move_sems, 2 + i, owner, moved, moved) for i, rows in enumerate(HALVES)]
 
         def halo(it):
             w = wide.at[it]
@@ -418,11 +418,14 @@
             for copy in aside:
                 copy.wait_recv()
             inner = inner + jnp.where(has_c, part[it, 4].astype(F32), 0.0)
-            product[...] = inner * gain
+            scaled = inner * gain
             if it + 1 < ITERS:
+                product[...] = scaled
                 wide[it + 1, OWN, 1] = (wide[it, OWN, 1].astype(F32) * product[...]).astype(BF)
             else:
-                bring.start()
+                for rows, copy in zip(HALVES, bring):
+                    product[rows] = scaled[rows]
+                    copy.start()
             pending = to_mate + straight + corner + aside
 
         @pl.when(jnp.logical_not(moved))
@@ -431,9 +434,11 @@
 
         for copy in pending:
             copy.wait_send()
-        bring.wait_recv()
-        out_ref[...] = estimate_ref[...] * back[...]
-        bring.wait_send()
+        for rows, copy in zip(HALVES, bring):
+            copy.wait_recv()
+            out_ref[rows] = estimate_ref[rows] * back[rows]
+        for copy in bring:
+            copy.wait_send()
 
     smem = pl.BlockSpec(memory_space=pltpu.SMEM)
     vmem = pl.BlockSpec(memory_space=pltpu.VMEM)
@@ -476,7 +481,7 @@
             pltpu.VMEM((1, LINE), jnp.int32),
             pltpu.VMEM((1, LINE), jnp.int32),
             pltpu.SMEM((1, LINE), jnp.int32),
-            (dma((3,)), dma((3,))),
+            (dma((4,)), dma((4,))),
             (dma((ITERS, 8)), dma((ITERS, 8))),
             (dma((ITERS, 10)), dma((ITERS, 10))),
             (dma((16,)), dma((16,))),

time: 62.5 us -> 62.5 us (level)
  no operation moved by 1% of the time
where the time goes in v11:
time: 62.5 us; the launch traced here: 62.3 us
  Pallas kernels  59.8 us (96%)
  local copies, waits for them, and re-layouts  2.49 us (4%)
    pallas_call x1, Pallas kernels, shards(): joint_kernel(nx, nz)  59.8 us
    unnamed x12, local copies, waits for them, and re-layouts  2.49 us

profile of v11, /device:TPU:1, one launch (start us, length us, event | category | flops | bytes accessed | tf_op | source)
XLA Modules:
  0.0 62.3 jit_solution(14119607190261956623)
XLA Ops:
  0.0 0.0 copy-start
  0.0 0.0 copy-start.1
  0.0 0.0 copy-start.2
  0.0 1.2 %copy.7 = bf16[16,8,16,128]{3,2,1,0:T(8,128)(2,1)S(1)} copy(bf16[16,8,16,128]{3,1,2,0:T(8,128)(2,1)} %bitcast.5) | data formatting | bytes 1048576
  1.2 0.0 copy-start.3
  1.2 0.0 copy-start.4
  1.2 0.0 copy-done
  1.2 0.0 copy-done.1
  1.2 0.0 copy-done.2
  1.3 0.6 %copy-done.3 = s32[256]{0:T(256)S(1)} copy-done((s32[256]{0:T(256)S(1)}, s32[256]{0:T(256)}, u32[]{:S(2)}) %copy-start.3) | copy-done | bytes 1048
  1.9 0.0 copy-done.4
  1.9 59.8 %joint.1 = f32[16,16,128]{2,1,0:T(8,128)S(1)} custom-call(s32[256]{0:T(256)S(1)} %copy-done.3, f32[6,33]{1,0:T(8,128)S(1)} %copy-done.2, f32[6,33]{1,0:T(8,128)S(1)} %copy-done.2, f32[6,16,2,33]{3,2,1,0:T(2,128)S(1)} %copy-done.1, s32[1,128]{1,0:T(1,128)S(1)} %copy-done.4, f32[16,16,128]{2,1,0:T(8,128)S(1)} %copy-done, ...), custom_call_target="tpu_custom_call" | custom-call | tf_op jit(solution)/shard_map/joint/pallas_call | solution.py:500
  61.7 0.7 %copy.9 = f32[16,16,128]{2,1,0:T(8,128)} copy(f32[16,16,128]{2,1,0:T(8,128)S(1)} %joint.1) | data formatting | bytes 262144
Async XLA Ops:
  0.0 1.2 %copy-start = (f32[16,16,128]{2,1,0:T(8,128)S(1)}, f32[16,16,128]{2,1,0:T(8,128)}, u32[]{:S(2)}) copy-start(f32[16,16,128]{2,1,0:T(8,128)} %estimate_ref.1) | copy-start | bytes 393220
  0.0 1.2 %copy-start.1 = (f32[6,16,2,33]{3,2,1,0:T(2,128)S(1)}, f32[6,16,2,33]{3,2,1,0:T(2,128)}, u32[]{:S(2)}) copy-start(f32[6,16,2,33]{3,2,1,0:T(2,128)} %bank_ref.1) | copy-start | bytes 76036
  0.0 1.2 %copy-start.2 = (f32[6,33]{1,0:T(8,128)S(1)}, f32[6,33]{1,0:T(8,128)}, u32[]{:S(2)}) copy-start(f32[6,33]{1,0:T(8,128)} %axial_in.1) | copy-start | bytes 2380
  1.2 0.7 %copy-start.3 = (s32[256]{0:T(256)S(1)}, s32[256]{0:T(256)}, u32[]{:S(2)}) copy-start(s32[256]{0:T(256)} %index_ref.1) | copy-start | bytes 3076
  1.2 0.7 %copy-start.4 = (s32[1,128]{1,0:T(1,128)S(1)}, s32[1,128]{1,0:T(1,128)}, u32[]{:S(2)}) copy-start(s32[1,128]{1,0:T(1,128)} %labels_ref.1) | copy-start | bytes 1540
